TPU v7x, 32 devices: a whole 2x2x4 slice. The times are simulated.
32 devices in a mesh: dp: 8 (over y, x, core), tensor: 4 (over z).
Axes of the slice: x: 2, y: 2, z: 4, core: 2. Of those that a mesh axis runs over, the one named last changes fastest.
Arguments:
- tokens: bfloat16 [16384, 1536], P('dp'), may hold values from -6 to 6
- lengths: int32 [8], P('dp'), may hold values from 1024 to 2048, as said below
- cotangent: bfloat16 [16384, 1536], P('dp'), may hold values from -6 to 6
- norm_gain: float32 [1536], replicated, may hold values from 0.1 to 1.9
- query_w: bfloat16 [1536, 1536], P(None, 'tensor'), may hold values from -0.15625 to 0.15625
- key_weight: bfloat16 [1536, 512], P(None, 'tensor'), may hold values from -0.15625 to 0.15625
- value_weight: bfloat16 [1536, 512], P(None, 'tensor'), may hold values from -0.15625 to 0.15625
- out_w: bfloat16 [1536, 1536], P('tensor'), may hold values from -0.625 to 0.625
- query_gain: float32 [64], replicated, may hold values from 0.1 to 1.9
- key_gain: float32 [64], replicated, may hold values from 0.1 to 1.9
- mlp_gain: float32 [1536], replicated, may hold values from 0.1 to 1.9
- gate_w: bfloat16 [1536, 6912], P(None, 'tensor'), may hold values from -0.15625 to 0.15625
- up_w: bfloat16 [1536, 6912], P(None, 'tensor'), may hold values from -0.15625 to 0.15625
- down_w: bfloat16 [6912, 1536], P('tensor'), may hold values from -0.078125 to 0.078125
Outputs:
- block_out: bfloat16 [16384, 1536], P('dp')
- input_grad: float32 [16384, 1536], P('dp')
- norm_gain_grad: float32 [1536], replicated
- query_w_grad: float32 [1536, 1536], P(None, 'tensor')
- key_w_grad: float32 [1536, 512], P(None, 'tensor')
- value_weight_gradient: float32 [1536, 512], P(None, 'tensor')
- out_w_grad: float32 [1536, 1536], P('tensor')
- query_gain_grad: float32 [64], replicated
- key_gain_grad: float32 [64], replicated
- mlp_gain_grad: float32 [1536], replicated
- gate_w_grad: float32 [1536, 6912], P(None, 'tensor')
- up_w_grad: float32 [1536, 6912], P(None, 'tensor')
- down_w_grad: float32 [6912, 1536], P('tensor')
Inputs may be any that keep to these rules, and one draw needn't show every extreme that they name: `lengths`: each sequence's live slots are its first ones; some sequence fills all 2048 slots.
All inputs are finite; a program needn't handle non-finite values.
Results may differ from a plain program's by a relative error of at most 0.024.
Values may be sent and summed in bfloat16 or wider, within the bound.
A program may use at most 384 MiB of HBM per device.

v0:
```python
import math

import jax
import jax.numpy as jnp
from jax import lax
from jax.sharding import PartitionSpec as P

HEAD_SIZE = 64
BLK = 512


EPSILON = 1e-05
ROPE_BASE = 1000000.0


def rms_scale(inputs, gain_vec):
    return (
        inputs * lax.rsqrt(jnp.mean(inputs * inputs, axis=-1, keepdims=True) + EPSILON) * gain_vec
    )


def rotary(inputs, head_count):
    row_count = inputs.shape[0]
    half_dim = HEAD_SIZE // 2
    positions = jnp.arange(row_count).astype(jnp.float32)[:, None]
    inv_freq = jnp.exp(
        jnp.arange(half_dim).astype(jnp.float32) * (-2.0 * math.log(ROPE_BASE) / HEAD_SIZE)
    )
    angles = positions * inv_freq[None, :]
    cosine = jnp.cos(angles)[:, None, :]
    sine_tab = jnp.sin(angles)[:, None, :]
    split_heads = inputs.reshape(row_count, head_count, HEAD_SIZE)
    lower_half = split_heads[..., :half_dim]
    upper_half = split_heads[..., half_dim:]
    turned = jnp.concatenate(
        [lower_half * cosine - upper_half * sine_tab, upper_half * cosine + lower_half * sine_tab],
        axis=-1,
    )
    return turned.reshape(row_count, head_count * HEAD_SIZE)


def head_norm(inputs, gain_vec, head_count):
    row_count = inputs.shape[0]
    return rms_scale(inputs.reshape(row_count, head_count, HEAD_SIZE), gain_vec).reshape(
        row_count, head_count * HEAD_SIZE
    )


def prepare(queries, keys_val, q_gain, k_gain):
    q_count = queries.shape[1] // HEAD_SIZE
    kv_count = keys_val.shape[1] // HEAD_SIZE
    return (
        rotary(head_norm(queries, q_gain, q_count), q_count),
        rotary(head_norm(keys_val, k_gain, kv_count), kv_count),
    )


def swiglu(gate_val, up_val):
    return gate_val * jax.nn.sigmoid(gate_val) * up_val


def left_dot(left, right):
    return lax.dot_general(
        left, right, (((0,), (0,)), ((), ())), preferred_element_type=jnp.float32
    )


def right_dot(left, right):
    return lax.dot_general(
        left, right, (((1,), (1,)), ((), ())), preferred_element_type=jnp.float32
    )


def masked_scores(q_block, k_block, first_row, length):
    raw_scores = jnp.einsum("kgqd,kjd->kgqj", q_block, k_block, preferred_element_type=jnp.float32)
    scaled = raw_scores * float(HEAD_SIZE) ** (-0.5)
    query_pos = first_row + jnp.arange(q_block.shape[2], dtype=jnp.int32)
    key_pos = jnp.arange(k_block.shape[1], dtype=jnp.int32)
    allowed = (key_pos[None, :] <= query_pos[:, None]) & (key_pos[None, :] < length)
    return jnp.where(allowed, scaled, -jnp.inf)


def on_device(
    tokens,
    lengths,
    cotangent,
    norm_gain,
    query_w,
    key_weight,
    value_weight,
    out_w,
    query_gain,
    key_gain,
    mlp_gain,
    gate_w,
    up_w,
    down_w,
):
    row_count = tokens.shape[0]
    length = lengths[0]
    live_rows = (jnp.arange(row_count, dtype=jnp.int32) < length).astype(jnp.float32)
    inputs = tokens.astype(jnp.float32)
    normed, norm_pull = jax.vjp(rms_scale, inputs, norm_gain)
    normed_b = normed.astype(jnp.bfloat16)
    queries = jnp.dot(normed_b, query_w, preferred_element_type=jnp.float32)
    keys_val = jnp.dot(normed_b, key_weight, preferred_element_type=jnp.float32)
    values_b = jnp.dot(normed_b, value_weight, preferred_element_type=jnp.float32).astype(
        jnp.bfloat16
    )
    (query_r, keys_r), prep_pull = jax.vjp(prepare, queries, keys_val, query_gain, key_gain)
    kv_count = key_weight.shape[1] // HEAD_SIZE
    group_size = query_w.shape[1] // key_weight.shape[1]
    q_heads = (
        query_r.astype(jnp.bfloat16)
        .reshape(row_count, kv_count, group_size, HEAD_SIZE)
        .transpose(1, 2, 0, 3)
    )
    k_heads = keys_r.astype(jnp.bfloat16).reshape(row_count, kv_count, HEAD_SIZE).transpose(1, 0, 2)
    v_heads = values_b.reshape(row_count, kv_count, HEAD_SIZE).transpose(1, 0, 2)
    block_outs = []
    log_sums = []
    for first_row in range(0, row_count, BLK):
        last_row = first_row + BLK
        scores = masked_scores(
            q_heads[:, :, first_row:last_row], k_heads[:, :last_row], first_row, length
        )
        row_max = jnp.max(scores, axis=-1, keepdims=True)
        weight = jnp.exp(scores - row_max)
        row_sum = jnp.sum(weight, axis=-1, keepdims=True)
        attn_prob = (weight / row_sum).astype(jnp.bfloat16)
        block_outs.append(
            jnp.einsum(
                "kgqj,kjd->kgqd",
                attn_prob,
                v_heads[:, :last_row],
                preferred_element_type=jnp.float32,
            )
        )
        log_sums.append(row_max + jnp.log(row_sum))
    mixed_b = (
        jnp.concatenate(block_outs, axis=2)
        .transpose(2, 0, 1, 3)
        .reshape(row_count, kv_count * group_size * HEAD_SIZE)
        .astype(jnp.bfloat16)
    )
    attn_out = lax.psum(
        jnp.dot(mixed_b, out_w, preferred_element_type=jnp.float32).astype(jnp.bfloat16), "tensor"
    ).astype(jnp.float32)
    residual = inputs + attn_out
    normed2, norm2_pull = jax.vjp(rms_scale, residual, mlp_gain)
    normed2_b = normed2.astype(jnp.bfloat16)
    gate_val = jnp.dot(normed2_b, gate_w, preferred_element_type=jnp.float32)
    up_val = jnp.dot(normed2_b, up_w, preferred_element_type=jnp.float32)
    hidden, glu_pull = jax.vjp(swiglu, gate_val, up_val)
    hidden_b = hidden.astype(jnp.bfloat16)
    mlp_out = lax.psum(
        jnp.dot(hidden_b, down_w, preferred_element_type=jnp.float32).astype(jnp.bfloat16), "tensor"
    ).astype(jnp.float32)
    block_out = (residual + mlp_out).astype(jnp.bfloat16)
    d_out = cotangent.astype(jnp.float32) * live_rows[:, None]
    d_out_b = d_out.astype(jnp.bfloat16)
    d_down = left_dot(hidden_b, d_out_b)
    d_hidden = right_dot(d_out_b, down_w)
    d_gate, d_up = glu_pull(d_hidden)
    d_gate_b = d_gate.astype(jnp.bfloat16)
    d_up_b = d_up.astype(jnp.bfloat16)
    d_gate_w = left_dot(normed2_b, d_gate_b)
    d_up_w = left_dot(normed2_b, d_up_b)
    d_normed2 = lax.psum(
        (right_dot(d_gate_b, gate_w) + right_dot(d_up_b, up_w)).astype(jnp.bfloat16), "tensor"
    ).astype(jnp.float32)
    d_resid_norm, d_mlp_gain = norm2_pull(d_normed2)
    d_resid = d_out + d_resid_norm
    d_resid_b = d_resid.astype(jnp.bfloat16)
    output_weight_cotangent = left_dot(mixed_b, d_resid_b)
    d_mixed = right_dot(d_resid_b, out_w).astype(jnp.bfloat16)
    d_heads = d_mixed.reshape(row_count, kv_count, group_size, HEAD_SIZE).transpose(1, 2, 0, 3)
    d_keys = jnp.zeros((kv_count, row_count, HEAD_SIZE), jnp.float32)
    d_values = jnp.zeros((kv_count, row_count, HEAD_SIZE), jnp.float32)
    d_queries = []
    for block_idx in range(row_count // BLK):
        first_row = block_idx * BLK
        last_row = first_row + BLK
        q_block = q_heads[:, :, first_row:last_row]
        scores = masked_scores(q_block, k_heads[:, :last_row], first_row, length)
        attn_prob = jnp.exp(scores - log_sums[block_idx])
        d_block = d_heads[:, :, first_row:last_row]
        d_values = d_values.at[:, :last_row].add(
            jnp.einsum(
                "kgqj,kgqd->kjd",
                attn_prob.astype(jnp.bfloat16),
                d_block,
                preferred_element_type=jnp.float32,
            )
        )
        d_prob = jnp.einsum(
            "kgqd,kjd->kgqj", d_block, v_heads[:, :last_row], preferred_element_type=jnp.float32
        )
        spread = jnp.sum(attn_prob * d_prob, axis=-1, keepdims=True)
        d_scores = (attn_prob * (d_prob - spread) * float(HEAD_SIZE) ** (-0.5)).astype(jnp.bfloat16)
        d_queries.append(
            jnp.einsum(
                "kgqj,kjd->kgqd",
                d_scores,
                k_heads[:, :last_row],
                preferred_element_type=jnp.float32,
            )
        )
        d_keys = d_keys.at[:, :last_row].add(
            jnp.einsum("kgqj,kgqd->kjd", d_scores, q_block, preferred_element_type=jnp.float32)
        )
    d_query_r = (
        jnp.concatenate(d_queries, axis=2)
        .transpose(2, 0, 1, 3)
        .reshape(row_count, kv_count * group_size * HEAD_SIZE)
    )
    d_keys_r = d_keys.transpose(1, 0, 2).reshape(row_count, kv_count * HEAD_SIZE)
    d_values_b = (
        d_values.transpose(1, 0, 2).reshape(row_count, kv_count * HEAD_SIZE).astype(jnp.bfloat16)
    )
    d_query_f, d_keys_f, d_qgain, d_kgain = prep_pull((d_query_r, d_keys_r))
    d_query_b = d_query_f.astype(jnp.bfloat16)
    d_keys_b = d_keys_f.astype(jnp.bfloat16)
    d_query_w = left_dot(normed_b, d_query_b)
    d_key_w = left_dot(normed_b, d_keys_b)
    d_value_w = left_dot(normed_b, d_values_b)
    d_normed = lax.psum(
        (
            right_dot(d_query_b, query_w)
            + right_dot(d_keys_b, key_weight)
            + right_dot(d_values_b, value_weight)
        ).astype(jnp.bfloat16),
        "tensor",
    ).astype(jnp.float32)
    d_input_norm, norm_gain_cotangent = norm_pull(d_normed)
    d_inputs = d_resid + d_input_norm
    head_totals = lax.psum((d_qgain, d_kgain), ("dp", "tensor"))
    all_totals = (
        lax.psum(norm_gain_cotangent.astype(jnp.bfloat16), "dp").astype(jnp.float32),
        lax.psum(d_query_w.astype(jnp.bfloat16), "dp").astype(jnp.float32),
        lax.psum(d_key_w.astype(jnp.bfloat16), "dp").astype(jnp.float32),
        lax.psum(d_value_w.astype(jnp.bfloat16), "dp").astype(jnp.float32),
        lax.psum(output_weight_cotangent.astype(jnp.bfloat16), "dp").astype(jnp.float32),
        lax.psum(d_gate_w.astype(jnp.bfloat16), "dp").astype(jnp.float32),
        lax.psum(d_up_w.astype(jnp.bfloat16), "dp").astype(jnp.float32),
        lax.psum(d_down.astype(jnp.bfloat16), "dp").astype(jnp.float32),
        lax.psum(d_mlp_gain.astype(jnp.bfloat16), "dp").astype(jnp.float32),
    )
    g_norm, g_query, g_key, g_value, g_out, g_gate, g_up, g_down, g_mlp = all_totals
    return (
        block_out,
        d_inputs,
        g_norm,
        g_query,
        g_key,
        g_value,
        g_out,
        head_totals[0],
        head_totals[1],
        g_mlp,
        g_gate,
        g_up,
        g_down,
    )


def solution(mesh):
    return jax.shard_map(
        on_device,
        mesh=mesh,
        in_specs=(
            P("dp", None),
            P("dp"),
            P("dp", None),
            P(),
            P(None, "tensor"),
            P(None, "tensor"),
            P(None, "tensor"),
            P("tensor", None),
            P(),
            P(),
            P(),
            P(None, "tensor"),
            P(None, "tensor"),
            P("tensor", None),
        ),
        out_specs=(
            P("dp", None),
            P("dp", None),
            P(),
            P(None, "tensor"),
            P(None, "tensor"),
            P(None, "tensor"),
            P("tensor", None),
            P(),
            P(),
            P(),
            P(None, "tensor"),
            P(None, "tensor"),
            P("tensor", None),
        ),
        check_vma=False,
    )
```

profile of v0, /device:TPU:0, one launch (start us, length us, event | category | flops | bytes accessed | tf_op | source)
XLA Modules:
  0.0 1743.3 jit_solution(18047508188142419568)
XLA Ops:
  116.9 223.2 %all-reduce.15.cloned.1.call-done = bf16[2048,1536]{1,0:T(8,128)(2,1)} async-done(((bf16[2048,1536]{1,0:T(8,128)(2,1)}), bf16[2048,1536]{1,0:T(8,128)(2,1)}) %all-reduce.15.cloned.1.call-update) | async-done | bytes 6291472 | tf_op jit(solution)/shard_map/psum | solution.py:146
  353.2 16.7 fusion.282
  369.9 13.7 fusion.281
  383.6 28.7 %multiply_convert_fusion.2 = (bf16[2048,1728]{0,1:T(8,128)(2,1)}, bf16[2048,1728]{0,1:T(8,128)(2,1)}, bf16[2048,1728]{0,1:T(8,128)(2,1)}) fusion(f32[2048,1728]{0,1:T(8,128)} %fusion.281, f32[2048,1728]{0,1:T(8,128)} %fusion.282, bf16[1728,1536]{1,0:T(8,128)(2,1)} %param.47, bf16[2048,1536]{1,0:T(8,128)(2,1)} %param.36, f32[2048]{0:T(1024)S(1)} %fusion.239), kind=kOutput, calls=%fused_computation.41 | convolution fusion | flops 10937696256 | bytes 61153280 | tf_op jit(solution)/shard_map/dot_general | solution.py:69
  412.3 16.5 fusion.283
  428.8 17.7 %add_convert_fusion.1 = bf16[2048,1536]{1,0:T(8,128)(2,1)} fusion(f32[2048,1536]{1,0:T(8,128)S(1)} %fusion.283, bf16[2048,1728]{0,1:T(8,128)(2,1)} %get-tuple-element.146, bf16[1536,1728]{0,1:T(8,128)(2,1)} %param.46), kind=kOutput, calls=%fused_computation.63 | convolution fusion | flops 10877927424 | bytes 31260672 | tf_op jit(solution)/shard_map/dot_general | solution.py:69
  446.5 17.0 convolution_convert_fusion
  463.5 16.9 convolution_convert_fusion.1
  480.4 13.3 convolution_convert_fusion.2
  493.8 174.6 %all-reduce.17.cloned.1.call-done = bf16[2048,1536]{1,0:T(8,128)(2,1)} async-done(((bf16[2048,1536]{1,0:T(8,128)(2,1)}), bf16[2048,1536]{1,0:T(8,128)(2,1)}) %all-reduce.17.cloned.1.call-update) | async-done | bytes 6291472 | tf_op jit(solution)/shard_map/psum | solution.py:169
  715.0 12.1 fusion.116
  780.0 33.9 %fusion.84 = f32[2,3,512,64]{2,3,1,0:T(8,128)} fusion(f32[2,3,512,1024]{3,2,1,0:T(8,128)} %fusion.220, f32[2,3,512,1024]{3,2,1,0:T(8,128)} %copy-done.11, f32[2,3,512]{2,1,0:T(4,128)S(1)} %copy-done.79, pred[512,1024]{1,0:T(8,128)(4,1)} %copy-done.22, bf16[2,2048,64]{1,2,0:T(8,128)(2,1)S(1)} %copy-done.47), kind=kOutput, calls=%fused_computation.99 | convolution fusion | flops 437260288 | bytes 52461568 | tf_op jit(solution)/shard_map/kgqj,kjd->kgqd/dot_general | solution.py:202
  813.9 34.6 %fusion.193 = f32[2,2048,64]{1,2,0:T(8,128)} fusion(f32[2,2048,64]{1,2,0:T(8,128)} %scatter-add.20, f32[2,3,512,1024]{3,2,1,0:T(8,128)} %fusion.220, f32[2,3,512,1024]{3,2,1,0:T(8,128)} %copy-done.11, f32[2,3,512]{2,1,0:T(4,128)S(1)} %copy-done.79, pred[512,1024]{1,0:T(8,128)(4,1)} %copy-done.22, bf16[2,3,2048,64]{2,3,1,0:T(8,128)(2,1)S(1)} %bitcast.225), kind=kOutput, calls=%fused_computation.180 | convolution fusion | flops 437391360 | bytes 52854784 | tf_op jit(solution)/shard_map/kgqj,kgqd->kjd/dot_general | solution.py:210
  848.5 29.6 %fusion.63 = f32[2,3,512,64]{2,3,1,0:T(8,128)} fusion(f32[2,3,512,1536]{3,2,1,0:T(8,128)} %fusion.217, f32[2,3,512,1536]{3,2,1,0:T(8,128)} %get-tuple-element.166, f32[2,3,512]{2,1,0:T(4,128)S(1)} %copy-done.77, bf16[2,2048,64]{1,2,0:T(8,128)(2,1)S(1)} %copy-done.47), kind=kOutput, calls=%fused_computation.82 | convolution fusion | flops 637014528 | bytes 76709888 | tf_op jit(solution)/shard_map/kgqj,kjd->kgqd/dot_general | solution.py:202
  878.1 30.0 %fusion.167 = f32[2,2048,64]{1,2,0:T(8,128)} fusion(f32[2,2048,64]{1,2,0:T(8,128)} %fusion.193, f32[2,3,512,1536]{3,2,1,0:T(8,128)} %fusion.217, f32[2,3,512,1536]{3,2,1,0:T(8,128)} %get-tuple-element.166, f32[2,3,512]{2,1,0:T(4,128)S(1)} %copy-done.77, bf16[2,3,2048,64]{2,3,1,0:T(8,128)(2,1)S(1)} %bitcast.226), kind=kOutput, calls=%fused_computation.157 | convolution fusion | flops 637211136 | bytes 77496320 | tf_op jit(solution)/shard_map/kgqj,kgqd->kjd/dot_general | solution.py:210
  908.2 45.0 %fusion.27 = f32[2,3,512,64]{2,3,1,0:T(8,128)} fusion(f32[2,3,512,2048]{3,2,1,0:T(8,128)} %fusion.214, f32[2,3,512,2048]{3,2,1,0:T(8,128)} %get-tuple-element.164, f32[2,3,512]{2,1,0:T(4,128)S(1)} %copy-done.78, pred[512,2048]{1,0:T(8,128)(4,1)} %copy-done.20, bf16[2048,2,32]{0,2,1:T(8,128)(2,1)S(1)} %copy-done.41, bf16[2048,2,32]{0,2,1:T(8,128)(2,1)S(1)} %copy-done.38), kind=kOutput, calls=%fused_computation.47 | convolution fusion | flops 875566080 | bytes 52703232 | tf_op jit(solution)/shard_map/kgqj,kjd->kgqd/dot_general | solution.py:202
  953.2 48.7 %fusion.173 = f32[2048,2,64]{0,2,1:T(8,128)} fusion(f32[2,2048,64]{1,2,0:T(8,128)} %fusion.167, f32[2,3,512,2048]{3,2,1,0:T(8,128)} %fusion.214, f32[2,3,512,2048]{3,2,1,0:T(8,128)} %get-tuple-element.164, f32[2,3,512]{2,1,0:T(4,128)S(1)} %copy-done.78, pred[512,2048]{1,0:T(8,128)(4,1)} %copy-done.20, bf16[2,3,2048,64]{2,3,1,0:T(8,128)(2,1)S(1)} %bitcast.227), kind=kOutput, calls=%fused_computation.159 | convolution fusion | flops 874779648 | bytes 105283584 | tf_op jit(solution)/shard_map/kgqj,kgqd->kjd/dot_general | solution.py:210
  1016.6 17.4 convolution_convert_fusion.3
  1047.0 13.2 add_convert_fusion
  1060.3 40.8 %all-reduce.6 = (f32[64]{0:T(128)}, f32[64]{0:T(128)}) all-reduce(f32[64]{0:T(128)S(1)} %get-tuple-element.129, f32[64]{0:T(128)S(1)} %get-tuple-element.131), channel_id=1, replica_groups=mesh['dp'=8,'tensor'=4] {'dp','tensor'}, use_global_device_ids=true, to_apply=%region_31.32 | all-reduce | flops 128 | bytes 1024 | tf_op jit(solution)/shard_map/psum | solution.py:237
  1101.1 160.8 %all-reduce.19.cloned.1.call-done = (bf16[1536,384]{1,0:T(8,128)(2,1)}, bf16[1536,128]{1,0:T(8,128)(2,1)}, bf16[1536,128]{1,0:T(8,128)(2,1)}, bf16[384,1536]{1,0...) async-done(((bf16[1536,384]{1,0:T(8,128)(2,1)}, bf16[1536,128]{1,0:T(8,128)(2,1)}, bf16[1536,128]{1,0:T(8,128)(2,1)}, ...) | async-done | bytes 19070992 | tf_op jit(solution)/shard_map/psum | solution.py:240
  1288.8 403.2 %all-reduce.21.cloned.1.call-done = (bf16[2048,1536]{1,0:T(8,128)(2,1)}, bf16[2048,1536]{1,0:T(8,128)(2,1)}) async-done(((bf16[2048,1536]{1,0:T(8,128)(2,1)}, bf16[2048,1536]{1,0:T(8,128)(2,1)}), (bf16[2048,1536]{1,0:T(8,128)(2,1)}, bf16[2048,1536]{1,0:T(8,128)(2,1)})) %all-reduce.21.cloned.1.call-update) | async-done | bytes 12582928 | tf_op jit(solution)/shard_map/psum | solution.py:156
  1700.2 13.9 all-reduce.7
  1715.4 20.9 %fusion.34 = (f32[2048,1536]{1,0:T(8,128)}, bf16[2048,1536]{1,0:T(8,128)(2,1)}) fusion(f32[2048,1536]{1,0:T(8,128)} %copy-done.6, bf16[2048,1536]{1,0:T(8,128)(2,1)} %get-tuple-element.145, bf16[2048,1536]{1,0:T(8,128)(2,1)} %param.34, f32[2048]{0:T(1024)S(1)} %multiply_multiply_fusion.4, f32[1536]{0:T(1024)S(1)} %copy-done.59, f32[2048]{0:T(1024)S(1)} %copy-done.56, ...), kind=kLoop, calls=%fused_computation.53 | loop fusion | flops 40894464 | bytes 56645632 | tf_op jit(solution)/shard_map/add | solution.py:236
  (321 shorter events, 284.1 us)
Async XLA Ops:
  7.2 101.7 %copy-start = (bf16[384,1536]{1,0:T(8,128)(2,1)S(1)}, bf16[384,1536]{1,0:T(8,128)(2,1)}, u32[]{:S(2)}) copy-start(bf16[384,1536]{1,0:T(8,128)(2,1)} %param.41) | copy-start | bytes 3538948
  7.2 332.9 %all-reduce.15.cloned.1.call-start = ((), (), s32[]{:S(2)}) async-start(), calls=%async_computation | async-start | bytes 12582912 | tf_op jit(solution)/shard_map/psum | solution.py:146
  19.2 76.7 %copy-start.12 = (bf16[2048,128]{0,1:T(8,128)(2,1)}, bf16[2048,128]{0,1:T(8,128)(2,1)S(1)}, u32[]{:S(2)}) copy-start(bf16[2048,128]{0,1:T(8,128)(2,1)S(1)} %convolution_convert_fusion.6) | copy-start | bytes 1572868
  27.7 45.6 %copy-start.37 = (bf16[2048,2,32]{0,2,1:T(8,128)(2,1)}, bf16[2048,2,32]{0,2,1:T(8,128)(2,1)S(1)}, u32[]{:S(2)}) copy-start(bf16[2048,2,32]{0,2,1:T(8,128)(2,1)S(1)} %get-tuple-element.157) | copy-start | bytes 786436
  28.8 44.5 %copy-start.28 = (bf16[2048,6,64]{0,2,1:T(8,128)(2,1)}, bf16[2048,6,64]{0,2,1:T(8,128)(2,1)S(1)}, u32[]{:S(2)}) copy-start(bf16[2048,6,64]{0,2,1:T(8,128)(2,1)S(1)} %pad_maximum_fusion.1) | copy-start | bytes 4718596
  73.4 22.5 %copy-start.20 = (pred[512,2048]{1,0:T(8,128)(4,1)}, pred[512,2048]{1,0:T(8,128)(4,1)S(1)}, u32[]{:S(2)}) copy-start(pred[512,2048]{1,0:T(8,128)(4,1)S(1)} %fusion.111) | copy-start | bytes 3145732
  114.4 233.2 %copy-start.64 = (f32[1536]{0:T(1024)S(1)}, f32[1536]{0:T(1024)}, u32[]{:S(2)}) copy-start(f32[1536]{0:T(1024)} %param.44) | copy-start | bytes 18436
  114.4 554.0 %all-reduce.17.cloned.1.call-start = ((), (), s32[]{:S(2)}) async-start(), calls=%async_computation.1 | async-start | bytes 12582912 | tf_op jit(solution)/shard_map/psum | solution.py:169
  446.4 815.5 %all-reduce.19.cloned.1.call-start = ((), (), s32[]{:S(2)}) async-start(), calls=%async_computation.2 | async-start | bytes 38141952 | tf_op jit(solution)/shard_map/psum | solution.py:240
  446.5 33.9 %slice-start.9 = ((s8[6291456]{0:T(1024)(128)(4,1)}), s8[4194304]{0:T(1024)(128)(4,1)S(1)}, s32[]{:S(2)}) async-start(s8[6291456]{0:T(1024)(128)(4,1)} %bitcast.204), calls=%async_computation.13 | async-start | bytes 8388608
  446.5 33.9 %slice-start.17 = ((s8[7077888]{0:T(1024)(128)(4,1)}), s8[4194304]{0:T(1024)(128)(4,1)S(1)}, s32[]{:S(2)}) async-start(s8[7077888]{0:T(1024)(128)(4,1)} %bitcast.234), calls=%async_computation.21 | async-start | bytes 8388608
  480.4 188.0 %copy-start.58 = (f32[2048]{0:T(1024)S(1)}, f32[2048]{0:T(1024)}, u32[]{:S(2)}) copy-start(f32[2048]{0:T(1024)} %copy-done.57) | copy-start | bytes 24580
  480.4 188.0 %copy-start.65 = (f32[1536]{0:T(1024)S(1)}, f32[1536]{0:T(1024)}, u32[]{:S(2)}) copy-start(f32[1536]{0:T(1024)} %param.44) | copy-start | bytes 18436
  493.8 185.0 %copy-start.63 = (f32[2048]{0:T(1024)S(1)}, f32[2048]{0:T(1024)}, u32[]{:S(2)}) copy-start(f32[2048]{0:T(1024)} %copy-done.62) | copy-start | bytes 24580
  780.0 33.9 %copy-start.29 = (bf16[2048,6,64]{0,2,1:T(8,128)(2,1)S(1)}, bf16[2048,6,64]{0,2,1:T(8,128)(2,1)}, u32[]{:S(2)}) copy-start(bf16[2048,6,64]{0,2,1:T(8,128)(2,1)} %copy-done.28) | copy-start | bytes 4718596
  878.1 30.0 %copy-start.38 = (bf16[2048,2,32]{0,2,1:T(8,128)(2,1)S(1)}, bf16[2048,2,32]{0,2,1:T(8,128)(2,1)}, u32[]{:S(2)}) copy-start(bf16[2048,2,32]{0,2,1:T(8,128)(2,1)} %copy-done.37) | copy-start | bytes 786436
  878.1 30.0 %copy-start.41 = (bf16[2048,2,32]{0,2,1:T(8,128)(2,1)S(1)}, bf16[2048,2,32]{0,2,1:T(8,128)(2,1)}, u32[]{:S(2)}) copy-start(bf16[2048,2,32]{0,2,1:T(8,128)(2,1)} %copy-done.39) | copy-start | bytes 786436
  953.2 51.1 %copy-start.15 = (f32[2048,32]{0,1:T(8,128)S(1)}, f32[2048,32]{0,1:T(8,128)}, u32[]{:S(2)}) copy-start(f32[2048,32]{0,1:T(8,128)} %copy-done.14) | copy-start | bytes 786436
  953.2 51.1 %copy-start.17 = (f32[2048,32]{0,1:T(8,128)S(1)}, f32[2048,32]{0,1:T(8,128)}, u32[]{:S(2)}) copy-start(f32[2048,32]{0,1:T(8,128)} %copy-done.16) | copy-start | bytes 786436
  1016.5 675.5 %all-reduce.21.cloned.1.call-start = ((), (), s32[]{:S(2)}) async-start(), calls=%async_computation.3 | async-start | bytes 25165824 | tf_op jit(solution)/shard_map/psum | solution.py:156
  1283.2 408.8 %copy-start.56 = (f32[2048]{0:T(1024)S(1)}, f32[2048]{0:T(1024)}, u32[]{:S(2)}) copy-start(f32[2048]{0:T(1024)} %copy-done.55) | copy-start | bytes 24580
  1283.2 408.8 %copy-start.59 = (f32[1536]{0:T(1024)S(1)}, f32[1536]{0:T(1024)}, u32[]{:S(2)}) copy-start(f32[1536]{0:T(1024)} %param.37) | copy-start | bytes 18436
  1288.8 411.4 %copy-start.61 = (f32[2048]{0:T(1024)S(1)}, f32[2048]{0:T(1024)}, u32[]{:S(2)}) copy-start(f32[2048]{0:T(1024)} %copy-done.60) | copy-start | bytes 24580
  1288.8 411.4 %copy-start.80 = (bf16[1536]{0:T(1024)(128)(2,1)S(1)}, bf16[1536]{0:T(1024)(128)(2,1)}, u32[]{:S(2)}) copy-start(bf16[1536]{0:T(1024)(128)(2,1)} %get-tuple-element.125) | copy-start | bytes 9220
  (86 other events, 604.9 us)
Sparse Core Ops, SparseCore 0:
  114.5 225.5 all-reduce.14
  446.6 221.7 all-reduce.16
  1016.6 245.2 all-reduce.18
  1265.0 426.9 all-reduce.20
where the time goes:
time: 1750 us; the launch traced here: 1740 us
  waiting for transfers between devices  962 us (55%)
  matrix products  563 us (32%)
  other arithmetic  137 us (8%)
  blocking collectives  54.8 us (3%)
    psum x1, waiting for transfers between devices, on_device(): lax.psum(jnp.dot(hidden_b, down_w, preferred_element_type=jnp.float32).as...  403 us
    psum x1, waiting for transfers between devices, on_device(): lax.psum(jnp.dot(mixed_b, out_w, preferred_element_type=jnp.float32).asty...  223 us
    psum x1, waiting for transfers between devices, on_device(): lax.psum((right_dot(d_gate_b, gate_w) + right_dot(d_up_b, up_w)).astype(j...  175 us
    psum x1, waiting for transfers between devices, on_device(): lax.psum(d_query_w.astype(jnp.bfloat16), 'dp').astype(jnp.float32)  161 us
    dot_general x4, matrix products, on_device(): jnp.einsum('kgqj,kgqd->kjd', d_scores, q_block, preferred_element_type=jn...  125 us
    dot_general x4, matrix products, on_device(): jnp.einsum('kgqj,kjd->kgqd', d_scores, k_heads[:, :last_row], preferred_e...  121 us
    dot_general x7, matrix products, right_dot(): lax.dot_general(left, right, (((1,), (1,)), ((), ())), preferred_element_...  91.9 us
    dot_general x7, matrix products, left_dot(): lax.dot_general(left, right, (((0,), (0,)), ((), ())), preferred_element_...  60.6 us
  transfers between devices with their start and end apart: 4, of which 4 were waited for; matrix products, arithmetic and copies ran while one was open for 7% of the time, Pallas kernels for 0%

commit v1 on v0

--- a/solution.py
+++ b/solution.py
@@ -1,12 +1,168 @@
+import functools
 import math
 
 import jax
 import jax.numpy as jnp
 from jax import lax
+from jax.experimental import pallas as pl
+from jax.experimental.pallas import tpu as pltpu
 from jax.sharding import PartitionSpec as P
 
 HEAD_SIZE = 64
 BLK = 512
+LANES=128
+SCALE = HEAD_SIZE ** -0.5
+LOG2E = math.log2(math.e)
+F32=jnp.float32; BF16=jnp.bfloat16
+
+def nt(a,b): return lax.dot_general(a,b,(((1,),(1,)),((),())),preferred_element_type=F32)
+def tn(a,b): return lax.dot_general(a,b,(((0,),(0,)),((),())),preferred_element_type=F32)
+def nn(a,b): return lax.dot_general(a,b,(((1,),(0,)),((),())),preferred_element_type=F32)
+
+def head_places(heads, group):
+    return [(h // 2, h % 2, h // group) for h in range(heads)]
+
+def half_mask(half, dtype=F32):
+    lane = lax.broadcasted_iota(jnp.int32, (1, LANES), 1)
+    keep = lane < HEAD_SIZE if half == 0 else lane >= HEAD_SIZE
+    return keep
+
+def stack_heads(x, places):
+    out = []
+    for tile, half, kv in places:
+        piece = x[:, tile * LANES:(tile + 1) * LANES]
+        if half != kv:
+            piece = pltpu.roll(piece, HEAD_SIZE, 1)
+        out.append(jnp.where(half_mask(kv), piece, 0.0))
+    return jnp.concatenate(out, axis=0)
+
+def unstack_heads(x, places, tiles, n):
+    pieces = {}
+    for h, (tile, half, kv) in enumerate(places):
+        piece = x[h * n:(h + 1) * n]
+        if half != kv:
+            piece = pltpu.roll(piece, HEAD_SIZE, 1)
+        pieces[tile, half] = piece
+    out = []
+    for tile in range(tiles):
+        low = pieces[tile, 0]
+        high = pieces.get((tile, 1))
+        out.append(jnp.where(half_mask(0), low, 0.0 if high is None else high))
+    return jnp.concatenate(out, axis=1)
+
+def fwd_kernel(places, tiles, bq, bk, len_ref, q_ref, k_ref, v_ref, o_ref, linv_ref, q6, vx, acc):
+    i = pl.program_id(0)
+    heads = len(places)
+    rows = k_ref.shape[0]
+    @pl.when(i == 0)
+    def _():
+        live = lax.broadcasted_iota(jnp.int32, (rows, LANES), 0) < len_ref[0]
+        vx[:, :LANES] = jnp.where(live, v_ref[...].astype(F32), 0.0).astype(BF16)
+        vx[:, LANES:] = jnp.where(live, 1.0, 0.0).astype(BF16)
+    q6[...] = stack_heads(q_ref[...].astype(F32), places).astype(BF16)
+    acc[...] = jnp.zeros_like(acc)
+    def step(j, masked):
+        ks = pl.ds(pl.multiple_of(j * bk, bk), bk)
+        s = nt(q6[...], k_ref[ks, :])
+        p = jnp.exp2(s * (SCALE * LOG2E))
+        if masked:
+            qp = i * bq + (lax.broadcasted_iota(jnp.int32, s.shape, 0) & (bq - 1))
+            kp = j * bk + lax.broadcasted_iota(jnp.int32, s.shape, 1)
+            p = jnp.where(kp <= qp, p, 0.0)
+        acc[...] += nn(p.astype(BF16), vx[ks, :])
+    full = (i * bq) // bk
+    @pl.loop(0, full)
+    def _(j): step(j, False)
+    @pl.loop(full, full + max(bq // bk, 1))
+    def _(j): step(j, True)
+    inv = 1.0 / acc[:, LANES:]
+    o_ref[...] = unstack_heads(acc[:, :LANES] * inv, places, tiles, bq).astype(BF16)
+    linv_ref[...] = unstack_heads(inv, places, tiles, bq)
+
+def attn_fwd(length, q, k, v, heads, group, bq=256, bk=256):
+    rows, width = q.shape
+    tiles = width // LANES
+    places = head_places(heads, group)
+    return pl.pallas_call(
+        functools.partial(fwd_kernel, places, tiles, bq, bk),
+        out_shape=(jax.ShapeDtypeStruct((rows, width), BF16), jax.ShapeDtypeStruct((rows, width), F32)),
+        grid_spec=pltpu.PrefetchScalarGridSpec(
+            num_scalar_prefetch=1, grid=(rows // bq,),
+            in_specs=[pl.BlockSpec((bq, width), lambda i, n: (i, 0)),
+                      pl.BlockSpec((rows, LANES), lambda i, n: (0, 0)),
+                      pl.BlockSpec((rows, LANES), lambda i, n: (0, 0))],
+            out_specs=[pl.BlockSpec((bq, width), lambda i, n: (i, 0))] * 2,
+            scratch_shapes=[pltpu.VMEM((heads * bq, LANES), BF16), pltpu.VMEM((rows, 2 * LANES), BF16),
+                            pltpu.VMEM((heads * bq, 2 * LANES), F32)]),
+        compiler_params=pltpu.CompilerParams(dimension_semantics=("arbitrary",), vmem_limit_bytes=48 << 20),
+        cost_estimate=pl.CostEstimate(flops=heads * rows * rows * 2 * LANES, transcendentals=heads * rows * rows // 2, bytes_accessed=rows * width * 8),
+        name="attention_forward",
+    )(length, q, k, v)
+
+def bwd_kernel(places, tiles, bq, bk, len_ref, q_ref, do_ref, o_ref, linv_ref, k_ref, v_ref, dq_ref, dk_ref, dv_ref, q6, do6, d_row, kx, dq6):
+    i = pl.program_id(0)
+    rows = k_ref.shape[0]
+    heads = len(places)
+    @pl.when(i == 0)
+    def _():
+        live = lax.broadcasted_iota(jnp.int32, (rows, LANES), 0) < len_ref[0]
+        kx[...] = jnp.where(live, k_ref[...].astype(F32), 0.0).astype(BF16)
+        dk_ref[...] = jnp.zeros_like(dk_ref)
+        dv_ref[...] = jnp.zeros_like(dv_ref)
+    q6[...] = stack_heads(q_ref[...].astype(F32), places).astype(BF16)
+    dob = do_ref[...].astype(F32) * linv_ref[...]
+    do6[...] = stack_heads(dob, places).astype(BF16)
+    prod = stack_heads(dob * o_ref[...].astype(F32), places)
+    hi = prod.astype(BF16)
+    lo = (prod - hi.astype(F32)).astype(BF16)
+    ones = jnp.ones((16, LANES), BF16)
+    d_row[...] = nt(ones, hi) + nt(ones, lo)
+    dq6[...] = jnp.zeros_like(dq6)
+    def step(j, masked):
+        ks = pl.ds(pl.multiple_of(j * bk, bk), bk)
+        st = nt(k_ref[ks, :], q6[...])
+        pt = jnp.exp2(st * (SCALE * LOG2E))
+        if masked:
+            kp = j * bk + lax.broadcasted_iota(jnp.int32, st.shape, 0)
+            qp = i * bq + (lax.broadcasted_iota(jnp.int32, st.shape, 1) & (bq - 1))
+            pt = jnp.where(kp <= qp, pt, 0.0)
+        dv_ref[ks, :] += nn(pt.astype(BF16), do6[...])
+        dpt = nt(v_ref[ks, :], do6[...])
+        dst = (pt * (dpt - d_row[0:1, :])).astype(BF16)
+        dk_ref[ks, :] += nn(dst, q6[...])
+        dq6[...] += tn(dst, kx[ks, :])
+    full = (i * bq) // bk
+    @pl.loop(0, full)
+    def _(j): step(j, False)
+    @pl.loop(full, full + max(bq // bk, 1))
+    def _(j): step(j, True)
+    dq_ref[...] = unstack_heads(dq6[...] * SCALE, places, tiles, bq)
+    @pl.when(i == pl.num_programs(0) - 1)
+    def _():
+        live = lax.broadcasted_iota(jnp.int32, (rows, LANES), 0) < len_ref[0]
+        dk_ref[...] = jnp.where(live, dk_ref[...] * SCALE, 0.0)
+        dv_ref[...] = jnp.where(live, dv_ref[...], 0.0)
+
+def attn_bwd(length, q, do, o, linv, k, v, heads, group, bq=256, bk=256):
+    rows, width = q.shape
+    tiles = width // LANES
+    places = head_places(heads, group)
+    blk = pl.BlockSpec((bq, width), lambda i, n: (i, 0))
+    whole = pl.BlockSpec((rows, LANES), lambda i, n: (0, 0))
+    return pl.pallas_call(
+        functools.partial(bwd_kernel, places, tiles, bq, bk),
+        out_shape=(jax.ShapeDtypeStruct((rows, width), F32), jax.ShapeDtypeStruct((rows, LANES), F32), jax.ShapeDtypeStruct((rows, LANES), F32)),
+        grid_spec=pltpu.PrefetchScalarGridSpec(
+            num_scalar_prefetch=1, grid=(rows // bq,),
+            in_specs=[blk] * 4 + [whole] * 2,
+            out_specs=[blk, whole, whole],
+            scratch_shapes=[pltpu.VMEM((heads * bq, LANES), BF16), pltpu.VMEM((heads * bq, LANES), BF16),
+                            pltpu.VMEM((16, heads * bq), F32), pltpu.VMEM((rows, LANES), BF16),
+                            pltpu.VMEM((heads * bq, LANES), F32)]),
+        compiler_params=pltpu.CompilerParams(dimension_semantics=("arbitrary",), vmem_limit_bytes=48 << 20),
+        cost_estimate=pl.CostEstimate(flops=heads * rows * rows * 5 * LANES, transcendentals=heads * rows * rows // 2, bytes_accessed=rows * width * 14),
+        name="attention_backward",
+    )(length, q, do, o, linv, k, v)
 
 
 EPSILON = 1e-05
@@ -71,13 +227,9 @@
     )
 
 
-def masked_scores(q_block, k_block, first_row, length):
-    raw_scores = jnp.einsum("kgqd,kjd->kgqj", q_block, k_block, preferred_element_type=jnp.float32)
-    scaled = raw_scores * float(HEAD_SIZE) ** (-0.5)
-    query_pos = first_row + jnp.arange(q_block.shape[2], dtype=jnp.int32)
-    key_pos = jnp.arange(k_block.shape[1], dtype=jnp.int32)
-    allowed = (key_pos[None, :] <= query_pos[:, None]) & (key_pos[None, :] < length)
-    return jnp.where(allowed, scaled, -jnp.inf)
+def to_lanes(x):
+    short = -x.shape[1] % LANES
+    return x if short == 0 else jnp.pad(x, ((0, 0), (0, short)))
 
 
 def on_device(
@@ -109,40 +261,17 @@
     )
     (query_r, keys_r), prep_pull = jax.vjp(prepare, queries, keys_val, query_gain, key_gain)
     kv_count = key_weight.shape[1] // HEAD_SIZE
-    group_size = query_w.shape[1] // key_weight.shape[1]
-    q_heads = (
-        query_r.astype(jnp.bfloat16)
-        .reshape(row_count, kv_count, group_size, HEAD_SIZE)
-        .transpose(1, 2, 0, 3)
-    )
-    k_heads = keys_r.astype(jnp.bfloat16).reshape(row_count, kv_count, HEAD_SIZE).transpose(1, 0, 2)
-    v_heads = values_b.reshape(row_count, kv_count, HEAD_SIZE).transpose(1, 0, 2)
-    block_outs = []
-    log_sums = []
-    for first_row in range(0, row_count, BLK):
-        last_row = first_row + BLK
-        scores = masked_scores(
-            q_heads[:, :, first_row:last_row], k_heads[:, :last_row], first_row, length
-        )
-        row_max = jnp.max(scores, axis=-1, keepdims=True)
-        weight = jnp.exp(scores - row_max)
-        row_sum = jnp.sum(weight, axis=-1, keepdims=True)
-        attn_prob = (weight / row_sum).astype(jnp.bfloat16)
-        block_outs.append(
-            jnp.einsum(
-                "kgqj,kjd->kgqd",
-                attn_prob,
-                v_heads[:, :last_row],
-                preferred_element_type=jnp.float32,
-            )
-        )
-        log_sums.append(row_max + jnp.log(row_sum))
-    mixed_b = (
-        jnp.concatenate(block_outs, axis=2)
-        .transpose(2, 0, 1, 3)
-        .reshape(row_count, kv_count * group_size * HEAD_SIZE)
-        .astype(jnp.bfloat16)
-    )
+    q_width = query_w.shape[1]
+    k_width = key_weight.shape[1]
+    heads = q_width // HEAD_SIZE
+    group_size = heads // kv_count
+    q_pad = to_lanes(query_r.astype(jnp.bfloat16))
+    k_pad = to_lanes(keys_r.astype(jnp.bfloat16))
+    v_pad = to_lanes(values_b)
+    mixed_pad, inverse_sums = attn_fwd(
+        lengths, q_pad, k_pad, v_pad, heads, group_size, min(row_count, 512), min(row_count, 512)
+    )
+    mixed_b = mixed_pad[:, :q_width]
     attn_out = lax.psum(
         jnp.dot(mixed_b, out_w, preferred_element_type=jnp.float32).astype(jnp.bfloat16), "tensor"
     ).astype(jnp.float32)
@@ -174,50 +303,12 @@
     d_resid_b = d_resid.astype(jnp.bfloat16)
     output_weight_cotangent = left_dot(mixed_b, d_resid_b)
     d_mixed = right_dot(d_resid_b, out_w).astype(jnp.bfloat16)
-    d_heads = d_mixed.reshape(row_count, kv_count, group_size, HEAD_SIZE).transpose(1, 2, 0, 3)
-    d_keys = jnp.zeros((kv_count, row_count, HEAD_SIZE), jnp.float32)
-    d_values = jnp.zeros((kv_count, row_count, HEAD_SIZE), jnp.float32)
-    d_queries = []
-    for block_idx in range(row_count // BLK):
-        first_row = block_idx * BLK
-        last_row = first_row + BLK
-        q_block = q_heads[:, :, first_row:last_row]
-        scores = masked_scores(q_block, k_heads[:, :last_row], first_row, length)
-        attn_prob = jnp.exp(scores - log_sums[block_idx])
-        d_block = d_heads[:, :, first_row:last_row]
-        d_values = d_values.at[:, :last_row].add(
-            jnp.einsum(
-                "kgqj,kgqd->kjd",
-                attn_prob.astype(jnp.bfloat16),
-                d_block,
-                preferred_element_type=jnp.float32,
-            )
-        )
-        d_prob = jnp.einsum(
-            "kgqd,kjd->kgqj", d_block, v_heads[:, :last_row], preferred_element_type=jnp.float32
-        )
-        spread = jnp.sum(attn_prob * d_prob, axis=-1, keepdims=True)
-        d_scores = (attn_prob * (d_prob - spread) * float(HEAD_SIZE) ** (-0.5)).astype(jnp.bfloat16)
-        d_queries.append(
-            jnp.einsum(
-                "kgqj,kjd->kgqd",
-                d_scores,
-                k_heads[:, :last_row],
-                preferred_element_type=jnp.float32,
-            )
-        )
-        d_keys = d_keys.at[:, :last_row].add(
-            jnp.einsum("kgqj,kgqd->kjd", d_scores, q_block, preferred_element_type=jnp.float32)
-        )
-    d_query_r = (
-        jnp.concatenate(d_queries, axis=2)
-        .transpose(2, 0, 1, 3)
-        .reshape(row_count, kv_count * group_size * HEAD_SIZE)
-    )
-    d_keys_r = d_keys.transpose(1, 0, 2).reshape(row_count, kv_count * HEAD_SIZE)
-    d_values_b = (
-        d_values.transpose(1, 0, 2).reshape(row_count, kv_count * HEAD_SIZE).astype(jnp.bfloat16)
-    )
+    d_query_r, d_keys_r, d_values = attn_bwd(
+        lengths, q_pad, to_lanes(d_mixed), mixed_pad, inverse_sums, k_pad, v_pad, heads, group_size
+    )
+    d_query_r = d_query_r[:, :q_width]
+    d_keys_r = d_keys_r[:, :k_width]
+    d_values_b = d_values[:, :k_width].astype(jnp.bfloat16)
     d_query_f, d_keys_f, d_qgain, d_kgain = prep_pull((d_query_r, d_keys_r))
     d_query_b = d_query_f.astype(jnp.bfloat16)
     d_keys_b = d_keys_f.astype(jnp.bfloat16)

time: 1750 us -> 1460 us (0.83)
  matrix products: 563 us -> 221 us
  Pallas kernels: 0 us -> 71.2 us
  other arithmetic: 137 us -> 113 us
    dot_general x24 -> x0, matrix products: 350 us -> none  [the longest x4 125 us: on_device(): jnp.einsum('kgqj,kgqd->kjd', d_scores, q_block, preferred_element_type=jn...]
    pallas_call x0 -> x2, Pallas kernels: none -> 71.2 us  [the longest x1 49.3 us: attn_bwd(): pl.pallas_call(functools.partial(bwd_kernel, places, tiles, bq, bk), out_...]
    reduce_sum x4 -> x0, other arithmetic: 26 us -> none  [on_device(): row_sum = jnp.sum(weight, axis=-1, keepdims=True)]
  transfers between devices with their start and end apart: 4 -> 4, of which waited for: 4 -> 4; matrix products, arithmetic and copies ran while one was open for 7% -> 8% of each run, Pallas kernels for 0% -> 0%
where the time goes in v1:
time: 1460 us; the launch traced here: 1450 us
  waiting for transfers between devices  964 us (66%)
  matrix products  221 us (15%)
  other arithmetic  113 us (8%)
  Pallas kernels  71.2 us (5%)
  blocking collectives  54.6 us (4%)
  between operations  15.9 us (1%)
    psum x1, waiting for transfers between devices, on_device(): lax.psum(jnp.dot(hidden_b, down_w, preferred_element_type=jnp.float32).as...  403 us
    psum x1, waiting for transfers between devices, on_device(): lax.psum(jnp.dot(mixed_b, out_w, preferred_element_type=jnp.float32).asty...  226 us
    psum x1, waiting for transfers between devices, on_device(): lax.psum((right_dot(d_gate_b, gate_w) + right_dot(d_up_b, up_w)).astype(j...  175 us
    psum x1, waiting for transfers between devices, on_device(): lax.psum(d_query_w.astype(jnp.bfloat16), 'dp').astype(jnp.float32)  160 us
    dot_general x7, matrix products, right_dot(): lax.dot_general(left, right, (((1,), (1,)), ((), ())), preferred_element_...  94 us
    dot_general x7, matrix products, left_dot(): lax.dot_general(left, right, (((0,), (0,)), ((), ())), preferred_element_...  63.6 us
    pallas_call x1, Pallas kernels, attn_bwd(): pl.pallas_call(functools.partial(bwd_kernel, places, tiles, bq, bk), out_...  49.3 us
    psum x1, blocking collectives, on_device(): head_totals = lax.psum((d_qgain, d_kgain), ('dp', 'tensor'))  40.6 us
  transfers between devices with their start and end apart: 4, of which 4 were waited for; matrix products, arithmetic and copies ran while one was open for 8% of the time, Pallas kernels for 0%

profile of v1, /device:TPU:0, one launch (start us, length us, event | category | flops | bytes accessed | tf_op | source)
XLA Modules:
  0.0 1452.9 jit_solution(8092312561466055466)
XLA Ops:
  37.6 21.8 %attention_forward.1 = (bf16[2048,384]{1,0:T(8,128)(2,1)S(1)}, f32[2048,384]{1,0:T(8,128)}) custom-call(s32[1]{0:T(128)} %copy.50.len_ref, bf16[2048,384]{1,0:T(8,128)(2,1)S(1)} %copy.33.q_ref, bf16[2048,128]{1,0:T(8,128)(2,1)S(1)} %copy.34.k_ref, bf16[2048,128]{1,0:T(8,128)(2,1)S(1)} %convolution_convert_fusion.6.v_ref), custom_call_target="tpu_custom_call" | custom-call | flops 6442450944 | bytes 6291456 | tf_op jit(solution)/shard_map/attention_forward/pallas_call | solution.py:86
  65.9 225.6 %all-reduce.13.cloned.1.call-done = bf16[2048,1536]{1,0:T(8,128)(2,1)} async-done(((bf16[2048,1536]{1,0:T(8,128)(2,1)}), bf16[2048,1536]{1,0:T(8,128)(2,1)}) %all-reduce.13.cloned.1.call-update) | async-done | bytes 6291472 | tf_op jit(solution)/shard_map/psum | solution.py:275
  291.6 6.8 multiply_reduce_fusion
  304.9 13.8 fusion.40
  318.7 13.7 fusion.41
  332.5 28.7 %multiply_convert_fusion = (bf16[2048,1728]{0,1:T(8,128)(2,1)}, bf16[2048,1728]{0,1:T(8,128)(2,1)}, bf16[2048,1728]{0,1:T(8,128)(2,1)}) fusion(f32[2048,1728]{0,1:T(8,128)} %fusion.40, f32[2048,1728]{0,1:T(8,128)} %fusion.41, bf16[1728,1536]{1,0:T(8,128)(2,1)} %param.27, bf16[2048,1536]{1,0:T(8,128)(2,1)} %param.16, f32[2048]{0:T(1024)S(1)} %fusion.36), kind=kOutput, calls=%fused_computation.19 | convolution fusion | flops 10937696256 | bytes 61153280 | tf_op jit(solution)/shard_map/dot_general | solution.py:225
  361.1 16.2 %fusion.42 = f32[2048,1536]{1,0:T(8,128)S(1)} fusion(bf16[2048,1728]{0,1:T(8,128)(2,1)} %get-tuple-element.45, bf16[1536,1728]{0,1:T(8,128)(2,1)} %param.25), kind=kOutput, calls=%fused_computation.101 | convolution fusion | flops 10871635968 | bytes 24969216 | tf_op jit(solution)/shard_map/dot_general | solution.py:225
  377.4 17.6 %add_convert_fusion.1 = bf16[2048,1536]{1,0:T(8,128)(2,1)} fusion(f32[2048,1536]{1,0:T(8,128)S(1)} %fusion.42, bf16[2048,1728]{0,1:T(8,128)(2,1)} %get-tuple-element.44, bf16[1536,1728]{0,1:T(8,128)(2,1)} %param.26), kind=kOutput, calls=%fused_computation.32 | convolution fusion | flops 10877927424 | bytes 31260672 | tf_op jit(solution)/shard_map/dot_general | solution.py:225
  395.1 17.1 %convolution_convert_fusion.1 = bf16[1536,1728]{0,1:T(8,128)(2,1)} fusion(bf16[2048,1728]{0,1:T(8,128)(2,1)} %get-tuple-element.45, bf16[2048,1536]{1,0:T(8,128)(2,1)} %copy-done.21), kind=kOutput, calls=%fused_computation.39 | convolution fusion | flops 10874290176 | bytes 18677760 | tf_op jit(solution)/shard_map/dot_general | solution.py:219
  412.2 16.8 %convolution_convert_fusion = bf16[1536,1728]{0,1:T(8,128)(2,1)} fusion(bf16[2048,1728]{0,1:T(8,128)(2,1)} %get-tuple-element.44, bf16[2048,1536]{1,0:T(8,128)(2,1)} %copy-done.21), kind=kOutput, calls=%fused_computation.38 | convolution fusion | flops 10874290176 | bytes 18677760 | tf_op jit(solution)/shard_map/dot_general | solution.py:219
  429.1 13.3 convolution_convert_fusion.2
  442.5 174.6 %all-reduce.15.cloned.1.call-done = bf16[2048,1536]{1,0:T(8,128)(2,1)} async-done(((bf16[2048,1536]{1,0:T(8,128)(2,1)}), bf16[2048,1536]{1,0:T(8,128)(2,1)}) %all-reduce.15.cloned.1.call-update) | async-done | bytes 6291472 | tf_op jit(solution)/shard_map/psum | solution.py:298
  617.0 10.3 fusion.10
  627.4 10.4 fusion.12
  646.7 49.3 %attention_backward.1 = (f32[2048,384]{1,0:T(8,128)}, f32[2048,128]{1,0:T(8,128)S(1)}, f32[2048,128]{1,0:T(8,128)S(1)}) custom-call(s32[1]{0:T(128)} %copy.50.len_ref, bf16[2048,384]{1,0:T(8,128)(2,1)S(1)} %copy-done.2, bf16[2048,384]{1,0:T(8,128)(2,1)} %fusion.22.do_ref, bf16[2048,384]{1,0:T(8,128)(2,1)} %copy-done.7, ...), custom_call_target="tpu_custom_call" | custom-call | flops 16106127360 | bytes 11010048 | tf_op jit(solution)/shard_map/attention_backward/pallas_call | solution.py:152
  713.4 7.5 convolution_convert_fusion.5
  726.2 17.4 %convolution_convert_fusion.3 = bf16[2048,1536]{1,0:T(8,128)(2,1)} fusion(bf16[2048,1728]{0,1:T(8,128)(2,1)} %get-tuple-element.46, bf16[1728,1536]{1,0:T(8,128)(2,1)} %param.27), kind=kOutput, calls=%fused_computation.41 | convolution fusion | flops 10874781696 | bytes 18677760 | tf_op jit(solution)/shard_map/dot_general | solution.py:286
  756.8 13.2 add_convert_fusion
  770.6 40.6 %all-reduce.4 = (f32[64]{0:T(128)}, f32[64]{0:T(128)}) all-reduce(f32[64]{0:T(128)S(1)} %copy-done.55, f32[64]{0:T(128)S(1)} %get-tuple-element.29), channel_id=1, replica_groups=mesh['dp'=8,'tensor'=4] {'dp','tensor'}, use_global_device_ids=true, to_apply=%region_19.0 | all-reduce | flops 128 | bytes 1024 | tf_op jit(solution)/shard_map/psum | solution.py:328
  811.2 160.4 %all-reduce.17.cloned.1.call-done = (bf16[1536,384]{1,0:T(8,128)(2,1)}, bf16[1536,128]{1,0:T(8,128)(2,1)}, bf16[1536,128]{1,0:T(8,128)(2,1)}, bf16[384,1536]{1,0...) async-done(((bf16[1536,384]{1,0:T(8,128)(2,1)}, bf16[1536,128]{1,0:T(8,128)(2,1)}, bf16[1536,128]{1,0:T(8,128)(2,1)}, ...) | async-done | bytes 19070992 | tf_op jit(solution)/shard_map/psum | solution.py:331
  998.5 403.2 %all-reduce.19.cloned.1.call-done = (bf16[2048,1536]{1,0:T(8,128)(2,1)}, bf16[2048,1536]{1,0:T(8,128)(2,1)}) async-done(((bf16[2048,1536]{1,0:T(8,128)(2,1)}, bf16[2048,1536]{1,0:T(8,128)(2,1)}), (bf16[2048,1536]{1,0:T(8,128)(2,1)}, bf16[2048,1536]{1,0:T(8,128)(2,1)})) %all-reduce.19.cloned.1.call-update) | async-done | bytes 12582928 | tf_op jit(solution)/shard_map/psum | solution.py:285
  1401.7 8.2 fusion.11
  1409.9 13.9 all-reduce.5
  1425.1 20.9 %fusion.13 = (f32[2048,1536]{1,0:T(8,128)}, bf16[2048,1536]{1,0:T(8,128)(2,1)}) fusion(f32[2048,1536]{1,0:T(8,128)} %copy-done.14, bf16[2048,1536]{1,0:T(8,128)(2,1)} %get-tuple-element.43, bf16[2048,1536]{1,0:T(8,128)(2,1)} %param.14, f32[2048]{0:T(1024)S(1)} %multiply_multiply_fusion.4, f32[1536]{0:T(1024)S(1)} %copy-done.43, f32[2048]{0:T(1024)S(1)} %copy-done.39, ...), kind=kLoop, calls=%fused_computation.28 | loop fusion | flops 40894464 | bytes 56645632 | tf_op jit(solution)/shard_map/add | solution.py:327
  (206 shorter events, 115.5 us)
Async XLA Ops:
  7.2 53.4 %copy-start = (bf16[384,1536]{1,0:T(8,128)(2,1)S(1)}, bf16[384,1536]{1,0:T(8,128)(2,1)}, u32[]{:S(2)}) copy-start(bf16[384,1536]{1,0:T(8,128)(2,1)} %param.21) | copy-start | bytes 3538948
  7.2 284.4 %all-reduce.13.cloned.1.call-start = ((), (), s32[]{:S(2)}) async-start(), calls=%async_computation | async-start | bytes 12582912 | tf_op jit(solution)/shard_map/psum | solution.py:275
  23.8 13.7 copy-start.1
  32.7 26.7 %copy-start.3 = (bf16[2048,128]{1,0:T(8,128)(2,1)}, bf16[2048,128]{1,0:T(8,128)(2,1)S(1)}, u32[]{:S(2)}) copy-start(bf16[2048,128]{1,0:T(8,128)(2,1)S(1)} %copy.34.k_ref) | copy-start | bytes 1572868
  37.5 21.9 %copy-start.5 = (bf16[2048,128]{1,0:T(8,128)(2,1)}, bf16[2048,128]{1,0:T(8,128)(2,1)S(1)}, u32[]{:S(2)}) copy-start(bf16[2048,128]{1,0:T(8,128)(2,1)S(1)} %convolution_convert_fusion.6.v_ref) | copy-start | bytes 1572868
  65.9 551.1 %all-reduce.15.cloned.1.call-start = ((), (), s32[]{:S(2)}) async-start(), calls=%async_computation.1 | async-start | bytes 12582912 | tf_op jit(solution)/shard_map/psum | solution.py:298
  65.9 233.1 %copy-start.48 = (f32[1536]{0:T(1024)S(1)}, f32[1536]{0:T(1024)}, u32[]{:S(2)}) copy-start(f32[1536]{0:T(1024)} %param.24) | copy-start | bytes 18436
  291.6 13.3 slice-start.8
  299.1 19.7 %slice-start.10 = ((s8[5308416]{0:T(1024)(128)(4,1)}), s8[4194304]{0:T(1024)(128)(4,1)S(1)}, s32[]{:S(2)}) async-start(s8[5308416]{0:T(1024)(128)(4,1)} %bitcast.73), calls=%async_computation.14 | async-start | bytes 8388608
  304.9 13.8 copy-start.21
  304.9 13.8 slice-start.11
  395.1 576.6 %all-reduce.17.cloned.1.call-start = ((), (), s32[]{:S(2)}) async-start(), calls=%async_computation.2 | async-start | bytes 38141952 | tf_op jit(solution)/shard_map/psum | solution.py:331
  395.1 33.9 %slice-start.2 = ((s8[6291456]{0:T(1024)(128)(4,1)}), s8[4194304]{0:T(1024)(128)(4,1)S(1)}, s32[]{:S(2)}) async-start(s8[6291456]{0:T(1024)(128)(4,1)} %bitcast.61), calls=%async_computation.6 | async-start | bytes 8388608
  395.1 33.9 %slice-start.12 = ((s8[7077888]{0:T(1024)(128)(4,1)}), s8[4194304]{0:T(1024)(128)(4,1)S(1)}, s32[]{:S(2)}) async-start(s8[7077888]{0:T(1024)(128)(4,1)} %bitcast.75), calls=%async_computation.16 | async-start | bytes 8388608
  412.2 16.9 %slice-start.3 = ((s8[6291456]{0:T(1024)(128)(4,1)}), s8[2097152]{0:T(1024)(128)(4,1)S(1)}, s32[]{:S(2)}) async-start(s8[6291456]{0:T(1024)(128)(4,1)} %bitcast.61), calls=%async_computation.7 | async-start | bytes 4194304
  412.2 16.9 %slice-start.13 = ((s8[7077888]{0:T(1024)(128)(4,1)}), s8[2883584]{0:T(1024)(128)(4,1)S(1)}, s32[]{:S(2)}) async-start(s8[7077888]{0:T(1024)(128)(4,1)} %bitcast.75), calls=%async_computation.17 | async-start | bytes 5767168
  429.1 187.9 %copy-start.41 = (f32[2048]{0:T(1024)S(1)}, f32[2048]{0:T(1024)}, u32[]{:S(2)}) copy-start(f32[2048]{0:T(1024)} %copy-done.40) | copy-start | bytes 24580
  429.1 187.9 %copy-start.49 = (f32[1536]{0:T(1024)S(1)}, f32[1536]{0:T(1024)}, u32[]{:S(2)}) copy-start(f32[1536]{0:T(1024)} %param.24) | copy-start | bytes 18436
  442.4 184.9 %copy-start.47 = (f32[2048]{0:T(1024)S(1)}, f32[2048]{0:T(1024)}, u32[]{:S(2)}) copy-start(f32[2048]{0:T(1024)} %copy-done.46) | copy-start | bytes 24580
  726.2 17.5 %copy-start.26 = (bf16[2048,2,64]{0,2,1:T(8,128)(2,1)S(1)}, bf16[2048,2,64]{0,2,1:T(8,128)(2,1)}, u32[]{:S(2)}) copy-start(bf16[2048,2,64]{0,2,1:T(8,128)(2,1)} %copy-done.25) | copy-start | bytes 1572868
  726.2 17.5 %copy-start.27 = (bf16[1536,128]{1,0:T(8,128)(2,1)S(1)}, bf16[1536,128]{1,0:T(8,128)(2,1)}, u32[]{:S(2)}) copy-start(bf16[1536,128]{1,0:T(8,128)(2,1)} %param.19) | copy-start | bytes 1179652
  726.2 675.4 %all-reduce.19.cloned.1.call-start = ((), (), s32[]{:S(2)}) async-start(), calls=%async_computation.3 | async-start | bytes 25165824 | tf_op jit(solution)/shard_map/psum | solution.py:285
  992.9 408.8 %copy-start.39 = (f32[2048]{0:T(1024)S(1)}, f32[2048]{0:T(1024)}, u32[]{:S(2)}) copy-start(f32[2048]{0:T(1024)} %copy-done.38) | copy-start | bytes 24580
  992.9 408.8 %copy-start.43 = (f32[1536]{0:T(1024)S(1)}, f32[1536]{0:T(1024)}, u32[]{:S(2)}) copy-start(f32[1536]{0:T(1024)} %param.17) | copy-start | bytes 18436
  (50 other events, 260.2 us)
Sparse Core Ops, SparseCore 0:
  66.0 225.5 all-reduce.12
  395.2 221.7 all-reduce.14
  726.3 245.2 all-reduce.16
  974.7 426.9 all-reduce.18

commit v2 on v1

v2 whole, which is shorter than its diff:
```python
import functools
import math

import jax
import jax.numpy as jnp
from jax import lax
from jax.experimental import pallas as pl
from jax.experimental.pallas import tpu as pltpu
from jax.sharding import PartitionSpec as P

HEAD_SIZE = 64
LANES = 128
SCALE = HEAD_SIZE**-0.5
LOG2E = math.log2(math.e)
EPSILON = 1e-05
ROPE_BASE = 1000000.0
PIECES = 8
F32 = jnp.float32
BF16 = jnp.bfloat16
MESH = pl.DeviceIdType.MESH


def nt(a,b): return lax.dot_general(a,b,(((1,),(1,)),((),())),preferred_element_type=F32)
def tn(a,b): return lax.dot_general(a,b,(((0,),(0,)),((),())),preferred_element_type=F32)
def nn(a,b): return lax.dot_general(a,b,(((1,),(0,)),((),())),preferred_element_type=F32)

def head_places(heads, group):
    return [(h // 2, h % 2, h // group) for h in range(heads)]

def half_mask(half, dtype=F32):
    lane = lax.broadcasted_iota(jnp.int32, (1, LANES), 1)
    keep = lane < HEAD_SIZE if half == 0 else lane >= HEAD_SIZE
    return keep

def stack_heads(x, places):
    out = []
    for tile, half, kv in places:
        piece = x[:, tile * LANES:(tile + 1) * LANES]
        if half != kv:
            piece = pltpu.roll(piece, HEAD_SIZE, 1)
        out.append(jnp.where(half_mask(kv), piece, 0.0))
    return jnp.concatenate(out, axis=0)

def unstack_heads(x, places, tiles, n):
    pieces = {}
    for h, (tile, half, kv) in enumerate(places):
        piece = x[h * n:(h + 1) * n]
        if half != kv:
            piece = pltpu.roll(piece, HEAD_SIZE, 1)
        pieces[tile, half] = piece
    out = []
    for tile in range(tiles):
        low = pieces[tile, 0]
        high = pieces.get((tile, 1))
        out.append(jnp.where(half_mask(0), low, 0.0 if high is None else high))
    return jnp.concatenate(out, axis=1)

def fwd_kernel(places, tiles, bq, bk, len_ref, q_ref, k_ref, v_ref, o_ref, linv_ref, q6, vx, acc):
    i = pl.program_id(0)
    heads = len(places)
    rows = k_ref.shape[0]
    @pl.when(i == 0)
    def _():
        live = lax.broadcasted_iota(jnp.int32, (rows, LANES), 0) < len_ref[0]
        vx[:, :LANES] = jnp.where(live, v_ref[...].astype(F32), 0.0).astype(BF16)
        vx[:, LANES:] = jnp.where(live, 1.0, 0.0).astype(BF16)
    q6[...] = stack_heads(q_ref[...].astype(F32), places).astype(BF16)
    acc[...] = jnp.zeros_like(acc)
    def step(j, masked):
        ks = pl.ds(pl.multiple_of(j * bk, bk), bk)
        s = nt(q6[...], k_ref[ks, :])
        p = jnp.exp2(s * (SCALE * LOG2E))
        if masked:
            qp = i * bq + (lax.broadcasted_iota(jnp.int32, s.shape, 0) & (bq - 1))
            kp = j * bk + lax.broadcasted_iota(jnp.int32, s.shape, 1)
            p = jnp.where(kp <= qp, p, 0.0)
        acc[...] += nn(p.astype(BF16), vx[ks, :])
    full = (i * bq) // bk
    @pl.loop(0, full)
    def _(j): step(j, False)
    @pl.loop(full, full + max(bq // bk, 1))
    def _(j): step(j, True)
    inv = 1.0 / acc[:, LANES:]
    o_ref[...] = unstack_heads(acc[:, :LANES] * inv, places, tiles, bq).astype(BF16)
    linv_ref[...] = unstack_heads(inv, places, tiles, bq)

def attn_fwd(length, q, k, v, heads, group, bq=256, bk=256):
    rows, width = q.shape
    tiles = width // LANES
    places = head_places(heads, group)
    return pl.pallas_call(
        functools.partial(fwd_kernel, places, tiles, bq, bk),
        out_shape=(jax.ShapeDtypeStruct((rows, width), BF16), jax.ShapeDtypeStruct((rows, width), F32)),
        grid_spec=pltpu.PrefetchScalarGridSpec(
            num_scalar_prefetch=1, grid=(rows // bq,),
            in_specs=[pl.BlockSpec((bq, width), lambda i, n: (i, 0)),
                      pl.BlockSpec((rows, LANES), lambda i, n: (0, 0)),
                      pl.BlockSpec((rows, LANES), lambda i, n: (0, 0))],
            out_specs=[pl.BlockSpec((bq, width), lambda i, n: (i, 0))] * 2,
            scratch_shapes=[pltpu.VMEM((heads * bq, LANES), BF16), pltpu.VMEM((rows, 2 * LANES), BF16),
                            pltpu.VMEM((heads * bq, 2 * LANES), F32)]),
        compiler_params=pltpu.CompilerParams(dimension_semantics=("arbitrary",), vmem_limit_bytes=48 << 20),
        cost_estimate=pl.CostEstimate(flops=heads * rows * rows * 2 * LANES, transcendentals=heads * rows * rows // 2, bytes_accessed=rows * width * 8),
        name="attention_forward",
    )(length, q, k, v)

def bwd_kernel(places, tiles, bq, bk, len_ref, q_ref, do_ref, o_ref, linv_ref, k_ref, v_ref, dq_ref, dk_ref, dv_ref, q6, do6, d_row, kx, dq6):
    i = pl.program_id(0)
    rows = k_ref.shape[0]
    heads = len(places)
    @pl.when(i == 0)
    def _():
        live = lax.broadcasted_iota(jnp.int32, (rows, LANES), 0) < len_ref[0]
        kx[...] = jnp.where(live, k_ref[...].astype(F32), 0.0).astype(BF16)
        dk_ref[...] = jnp.zeros_like(dk_ref)
        dv_ref[...] = jnp.zeros_like(dv_ref)
    q6[...] = stack_heads(q_ref[...].astype(F32), places).astype(BF16)
    dob = do_ref[...].astype(F32) * linv_ref[...]
    do6[...] = stack_heads(dob, places).astype(BF16)
    prod = stack_heads(dob * o_ref[...].astype(F32), places)
    hi = prod.astype(BF16)
    lo = (prod - hi.astype(F32)).astype(BF16)
    ones = jnp.ones((16, LANES), BF16)
    d_row[...] = nt(ones, hi) + nt(ones, lo)
    dq6[...] = jnp.zeros_like(dq6)
    def step(j, masked):
        ks = pl.ds(pl.multiple_of(j * bk, bk), bk)
        st = nt(k_ref[ks, :], q6[...])
        pt = jnp.exp2(st * (SCALE * LOG2E))
        if masked:
            kp = j * bk + lax.broadcasted_iota(jnp.int32, st.shape, 0)
            qp = i * bq + (lax.broadcasted_iota(jnp.int32, st.shape, 1) & (bq - 1))
            pt = jnp.where(kp <= qp, pt, 0.0)
        dv_ref[ks, :] += nn(pt.astype(BF16), do6[...])
        dpt = nt(v_ref[ks, :], do6[...])
        dst = (pt * (dpt - d_row[0:1, :])).astype(BF16)
        dk_ref[ks, :] += nn(dst, q6[...])
        dq6[...] += tn(dst, kx[ks, :])
    full = (i * bq) // bk
    @pl.loop(0, full)
    def _(j): step(j, False)
    @pl.loop(full, full + max(bq // bk, 1))
    def _(j): step(j, True)
    dq_ref[...] = unstack_heads(dq6[...] * SCALE, places, tiles, bq)
    @pl.when(i == pl.num_programs(0) - 1)
    def _():
        live = lax.broadcasted_iota(jnp.int32, (rows, LANES), 0) < len_ref[0]
        dk_ref[...] = jnp.where(live, dk_ref[...] * SCALE, 0.0)
        dv_ref[...] = jnp.where(live, dv_ref[...], 0.0)

def attn_bwd(length, q, do, o, linv, k, v, heads, group, bq=256, bk=256):
    rows, width = q.shape
    tiles = width // LANES
    places = head_places(heads, group)
    blk = pl.BlockSpec((bq, width), lambda i, n: (i, 0))
    whole = pl.BlockSpec((rows, LANES), lambda i, n: (0, 0))
    return pl.pallas_call(
        functools.partial(bwd_kernel, places, tiles, bq, bk),
        out_shape=(jax.ShapeDtypeStruct((rows, width), F32), jax.ShapeDtypeStruct((rows, LANES), F32), jax.ShapeDtypeStruct((rows, LANES), F32)),
        grid_spec=pltpu.PrefetchScalarGridSpec(
            num_scalar_prefetch=1, grid=(rows // bq,),
            in_specs=[blk] * 4 + [whole] * 2,
            out_specs=[blk, whole, whole],
            scratch_shapes=[pltpu.VMEM((heads * bq, LANES), BF16), pltpu.VMEM((heads * bq, LANES), BF16),
                            pltpu.VMEM((16, heads * bq), F32), pltpu.VMEM((rows, LANES), BF16),
                            pltpu.VMEM((heads * bq, LANES), F32)]),
        compiler_params=pltpu.CompilerParams(dimension_semantics=("arbitrary",), vmem_limit_bytes=48 << 20),
        cost_estimate=pl.CostEstimate(flops=heads * rows * rows * 5 * LANES, transcendentals=heads * rows * rows // 2, bytes_accessed=rows * width * 14),
        name="attention_backward",
    )(length, q, do, o, linv, k, v)


def line_copy(src, dst, sems, where, to):
    return pltpu.make_async_remote_copy(
        src_ref=src,
        dst_ref=dst,
        send_sem=sems[0].at[where],
        recv_sem=sems[1].at[where],
        device_id={"tensor": to},
        device_id_type=MESH,
    )


def greet_line(count):
    me = lax.axis_index("tensor")
    barrier = pltpu.get_barrier_semaphore()

    @pl.when(me > 0)
    def _():
        pl.semaphore_signal(barrier, inc=1, device_id={"tensor": me - 1}, device_id_type=MESH)

    @pl.when(me < count - 1)
    def _():
        pl.semaphore_signal(barrier, inc=1, device_id={"tensor": me + 1}, device_id_type=MESH)

    @pl.when((me > 0) & (me < count - 1))
    def _():
        pl.semaphore_wait(barrier, 2)

    @pl.when((me == 0) | (me == count - 1))
    def _():
        pl.semaphore_wait(barrier, 1)


def line_sum_kernel(
    count, pieces, finish, kinds, part_ref, *refs
):
    (own_refs, full_ref, out_refs), scratch = split_refs(refs, kinds)
    up_buf, down_buf, acc = scratch[:3]
    sems = scratch[3:]
    sum_up, sum_down, give_up, give_down = (sems[0:2], sems[2:4], sems[4:6], sems[6:8])
    me = lax.axis_index("tensor")
    last = count - 1
    own = part_ref.shape[0] // count
    size = own // pieces

    def rows(block, c):
        return pl.ds(pl.multiple_of(block * own + c * size, size), size)

    def sum_copy(c, s, upward):
        buf, sem = (up_buf, sum_up) if upward else (down_buf, sum_down)
        to = me + 1 if upward else me - 1
        return buf, lambda src: line_copy(src, buf.at[c, s - 1], sem, (c, s - 1), to)

    def sum_start(c, s, upward):
        buf, copy = sum_copy(c, s, upward)
        first = me == 0 if upward else me == last
        block = count - s + me if upward else me - (count - s)
        sends = me <= s - 1 if upward else me >= count - s
        sends = sends & (me < last if upward else me > 0)

        @pl.when(sends & first)
        def _():
            copy(part_ref.at[rows(block, c)]).start()

        if s > 1:

            @pl.when(sends & jnp.logical_not(first))
            def _():
                sum_wait(c, s - 1, upward)
                held = buf.at[c, s - 2]
                held[...] = (held[...].astype(F32) + part_ref[rows(block, c), :].astype(F32)).astype(BF16)
                copy(held).start()

    def sum_wait(c, s, upward):
        buf, copy = sum_copy(c, s, upward)
        copy(buf.at[c, s - 1]).wait_recv()

    def give_copy(c, s, upward):
        block = me - s + 1 if upward else me + s - 1
        sem = give_up if upward else give_down
        place = full_ref.at[rows(block, c)]
        return line_copy(place, place, sem, (c, s - 1), me + 1 if upward else me - 1)

    def give_wait(c, s, upward):
        block = me - s if upward else me + s
        sem = give_up if upward else give_down
        place = full_ref.at[rows(block, c)]
        line_copy(place, place, sem, (c, s - 1), me + 1 if upward else me - 1).wait_recv()

    def give_start(c, s, upward):
        sends = (me >= s - 1) & (me < last) if upward else (me > 0) & (me <= count - s)
        if s > 1:
            got = (me >= s - 1) if upward else (me <= count - s)

            @pl.when(got)
            def _():
                give_wait(c, s - 1, upward)

        @pl.when(sends)
        def _():
            give_copy(c, s, upward).start()

    def settle(c):
        acc[...] = part_ref[rows(me, c), :].astype(F32)

        @pl.when(me > 0)
        def _():
            sum_wait(c, last, True)
            acc[...] += up_buf[c, last - 1].astype(F32)

        @pl.when(me < last)
        def _():
            sum_wait(c, last, False)
            acc[...] += down_buf[c, last - 1].astype(F32)

        mine = pl.ds(c * size, size)
        full_ref[rows(me, c), :] = finish(c, mine, acc[...], own_refs, out_refs)

    greet_line(count)
    for slot in range(pieces + 2 * last):
        if slot < pieces:
            for upward in (True, False):
                sum_start(slot, 1, upward)
        for s in range(last, 1, -1):
            c = slot - last - (s - 1)
            if 0 <= c < pieces:
                for upward in (True, False):
                    give_start(c, s, upward)
        c = slot - last
        if 0 <= c < pieces:
            settle(c)
            for upward in (True, False):
                give_start(c, 1, upward)
        for s in range(last, 1, -1):
            c = slot - (s - 1)
            if 0 <= c < pieces:
                for upward in (True, False):
                    sum_start(c, s, upward)
    for c in range(pieces):

        @pl.when(me == last)
        def _():
            give_wait(c, last, True)

        @pl.when(me == 0)
        def _():
            give_wait(c, last, False)

        for s in range(1, count):
            for upward in (True, False):
                sends = me <= s - 1 if upward else me >= count - s
                sends = sends & (me < last if upward else me > 0)

                @pl.when(sends)
                def _():
                    buf, copy = sum_copy(c, s, upward)
                    copy(buf.at[c, s - 1]).wait_send()

                sends = (me >= s - 1) & (me < last) if upward else (me > 0) & (me <= count - s)

                @pl.when(sends)
                def _():
                    give_copy(c, s, upward).wait_send()


def split_refs(refs, kinds):
    n_own, n_out = kinds
    own_refs = refs[:n_own]
    full_ref = refs[n_own]
    out_refs = refs[n_own + 1 : n_own + 1 + n_out]
    return (own_refs, full_ref, out_refs), refs[n_own + 1 + n_out :]


def line_sum(part, owned, outs, finish, pieces, collective_id):
    count = lax.axis_size("tensor")
    rows, width = part.shape
    size = rows // count // pieces
    vmem = pl.BlockSpec(memory_space=pltpu.VMEM)
    hops = (pieces, count - 1)
    return pl.pallas_call(
        functools.partial(line_sum_kernel, count, pieces, finish, (len(owned), len(outs))),
        out_shape=(jax.ShapeDtypeStruct((rows, width), BF16), *outs),
        in_specs=[vmem] * (1 + len(owned)),
        out_specs=(vmem,) * (1 + len(outs)),
        scratch_shapes=[
            pltpu.VMEM((*hops, size, width), BF16),
            pltpu.VMEM((*hops, size, width), BF16),
            pltpu.VMEM((size, width), F32),
        ]
        + [pltpu.SemaphoreType.DMA(hops)] * 8,
        compiler_params=pltpu.CompilerParams(
            collective_id=collective_id, has_side_effects=True, vmem_limit_bytes=56 << 20
        ),
        cost_estimate=pl.CostEstimate(
            flops=rows * width * 8, transcendentals=0, bytes_accessed=rows * width * 8
        ),
        name="line_sum",
    )(part, *owned)


def finish_attention(c, mine, total, own_refs, out_refs):
    inputs, gain = own_refs
    resid = inputs[mine, :] + total
    out_refs[0][mine, :] = resid
    return (resid * inverse_rms(resid) * gain[...]).astype(BF16)


def finish_back(c, mine, total, own_refs, out_refs):
    base, value, gain = own_refs
    x = value[mine, :]
    r = inverse_rms(x)
    y = x * r
    e = gain[...] * total
    out = base[mine, :] + r * (e - y * jnp.mean(e * y, axis=-1, keepdims=True))
    out_refs[0][mine, :] = out
    term = jnp.sum(total * y, axis=0, keepdims=True)
    if c == 0:
        out_refs[1][...] = term
    else:
        out_refs[1][...] += term
    return out.astype(BF16)


def finish_add(c, mine, total, own_refs, out_refs):
    return (own_refs[0][mine, :] + total).astype(BF16)


def inverse_rms(x):
    return lax.rsqrt(jnp.mean(x * x, axis=-1, keepdims=True) + EPSILON)


def norm_back(x, r, gain, grad):
    y = x * r
    e = gain * grad
    return r * (e - y * jnp.mean(e * y, axis=-1, keepdims=True)), jnp.sum(grad * y, axis=0)


def rope_tables(row_count):
    half = HEAD_SIZE // 2
    positions = jnp.arange(row_count).astype(F32)[:, None]
    freq = jnp.exp(jnp.arange(half).astype(F32) * (-2.0 * math.log(ROPE_BASE) / HEAD_SIZE))
    angles = positions * freq[None, :]
    return jnp.cos(angles)[:, None, :], jnp.sin(angles)[:, None, :]


def turn(x, cosine, sine):
    half = HEAD_SIZE // 2
    low, high = x[..., :half], x[..., half:]
    return jnp.concatenate([low * cosine - high * sine, high * cosine + low * sine], axis=-1)


def by_head(x):
    return x.reshape(x.shape[0], x.shape[1] // HEAD_SIZE, HEAD_SIZE)


def flat(x):
    return x.reshape(x.shape[0], x.shape[1] * x.shape[2])


def prepare(x, gain, tables):
    heads = by_head(x)
    return flat(turn(heads * inverse_rms(heads) * gain, *tables))


def prepare_back(x, gain, tables, grad):
    heads = by_head(x)
    back = turn(by_head(grad), tables[0], -tables[1])
    dx, d_gain = norm_back(heads, inverse_rms(heads), gain, back)
    return flat(dx), jnp.sum(d_gain, axis=0)


def to_lanes(x):
    short = -x.shape[1] % LANES
    return x if short == 0 else jnp.pad(x, ((0, 0), (0, short)))


def on_device(
    tokens,
    lengths,
    cotangent,
    norm_gain,
    query_w,
    key_weight,
    value_weight,
    out_w,
    query_gain,
    key_gain,
    mlp_gain,
    gate_w,
    up_w,
    down_w,
):
    row_count, width = tokens.shape
    me = lax.axis_index("tensor")
    count = lax.axis_size("tensor")
    m = row_count // count
    q_width = query_w.shape[1]
    k_width = key_weight.shape[1]
    heads = q_width // HEAD_SIZE
    group = q_width // k_width
    own_shape = jax.ShapeDtypeStruct((m, width), F32)
    gain_shape = jax.ShapeDtypeStruct((1, width), F32)

    def own(x):
        return lax.dynamic_slice_in_dim(x, me * m, m, axis=0)

    live = (jnp.arange(row_count, dtype=jnp.int32) < lengths[0])[:, None]
    d_out = jnp.where(live, cotangent, jnp.zeros_like(cotangent))
    inputs = tokens.astype(F32)
    normed = (inputs * inverse_rms(inputs) * norm_gain).astype(BF16)
    inputs_own = own(tokens).astype(F32)
    queries = nn(normed, query_w)
    keys_val = nn(normed, key_weight)
    tables = rope_tables(row_count)
    q_pad = to_lanes(prepare(queries, query_gain, tables).astype(BF16))
    k_pad = to_lanes(prepare(keys_val, key_gain, tables).astype(BF16))
    v_pad = to_lanes(nn(normed, value_weight).astype(BF16))
    mixed_pad, inverse_sums = attn_fwd(lengths, q_pad, k_pad, v_pad, heads, group, 512, 512)
    mixed = mixed_pad[:, :q_width]

    normed2, resid_own = line_sum(
        nn(mixed, out_w).astype(BF16),
        (inputs_own, mlp_gain[None]),
        (own_shape,),
        finish_attention,
        PIECES,
        1,
    )
    gate = nn(normed2, gate_w)
    up = nn(normed2, up_w)
    sig = jax.nn.sigmoid(gate)
    hidden = (gate * sig * up).astype(BF16)
    d_hidden = nt(d_out, down_w)
    d_gate = (d_hidden * up * sig * (1.0 + gate * (1.0 - sig))).astype(BF16)
    d_up = (d_hidden * gate * sig).astype(BF16)
    d_normed2 = (nt(d_gate, gate_w) + nt(d_up, up_w)).astype(BF16)
    mlp_own = lax.psum_scatter(
        nn(hidden, down_w).astype(BF16), "tensor", scatter_dimension=0, tiled=True
    )
    block_out = lax.all_gather(
        (resid_own + mlp_own.astype(F32)).astype(BF16), "tensor", axis=0, tiled=True
    )
    d_resid, d_resid_own, d_mlp_gain = line_sum(
        d_normed2,
        (own(d_out).astype(F32), resid_own, mlp_gain[None]),
        (own_shape, gain_shape),
        finish_back,
        PIECES,
        2,
    )
    g_gate = tn(normed2, d_gate).astype(BF16)
    g_up = tn(normed2, d_up).astype(BF16)
    g_down = tn(hidden, d_out).astype(BF16)
    g_gate, g_up, g_down = lax.psum((g_gate, g_up, g_down), "dp")

    d_mixed = nt(d_resid, out_w).astype(BF16)
    dq, dk, dv = attn_bwd(
        lengths, q_pad, to_lanes(d_mixed), mixed_pad, inverse_sums, k_pad, v_pad, heads, group
    )
    dq, d_qgain = prepare_back(queries, query_gain, tables, dq[:, :q_width])
    dk, d_kgain = prepare_back(keys_val, key_gain, tables, dk[:, :k_width])
    d_q, d_k, d_v = dq.astype(BF16), dk.astype(BF16), dv[:, :k_width].astype(BF16)
    d_normed = (nt(d_q, query_w) + nt(d_k, key_weight) + nt(d_v, value_weight)).astype(BF16)
    d_inputs, _, d_norm_gain = line_sum(
        d_normed,
        (d_resid_own, inputs_own, norm_gain[None]),
        (own_shape, gain_shape),
        finish_back,
        PIECES,
        3,
    )
    g_out = tn(mixed, d_resid).astype(BF16)
    g_query = tn(normed, d_q).astype(BF16)
    g_key = tn(normed, d_k).astype(BF16)
    g_value = tn(normed, d_v).astype(BF16)
    g_out, g_query, g_key, g_value, g_gate, g_up, g_down = lax.optimization_barrier(
        (g_out, g_query, g_key, g_value, g_gate, g_up, g_down)
    )
    g_out, g_query, g_key, g_value = lax.psum((g_out, g_query, g_key, g_value), "dp")
    g_norm, g_mlp, g_qgain, g_kgain = lax.psum(
        (d_norm_gain[0], d_mlp_gain[0], d_qgain, d_kgain), ("dp", "tensor")
    )
    return (
        block_out,
        d_inputs.astype(F32),
        g_norm,
        g_query.astype(F32),
        g_key.astype(F32),
        g_value.astype(F32),
        g_out.astype(F32),
        g_qgain,
        g_kgain,
        g_mlp,
        g_gate.astype(F32),
        g_up.astype(F32),
        g_down.astype(F32),
    )


def solution(mesh):
    rows, whole = P("dp", None), P()
    columns, depth = P(None, "tensor"), P("tensor", None)
    return jax.shard_map(
        on_device,
        mesh=mesh,
        in_specs=(
            rows,
            P("dp"),
            rows,
            whole,
            columns,
            columns,
            columns,
            depth,
            whole,
            whole,
            whole,
            columns,
            columns,
            depth,
        ),
        out_specs=(
            rows,
            rows,
            whole,
            columns,
            columns,
            columns,
            depth,
            whole,
            whole,
            whole,
            columns,
            columns,
            depth,
        ),
        check_vma=False,
    )
```

time: 1460 us -> 1110 us (0.76)
  waiting for transfers between devices: 964 us -> 0.09 us
  Pallas kernels: 71.2 us -> 723 us
  other arithmetic: 113 us -> 72.4 us
    psum x4 -> x2, waiting for transfers between devices: 964 us -> 0.01 us  [the longest x1 0.01 us: on_device(): lax.psum((g_out, g_query, g_key, g_value), 'dp')]
    pallas_call x0 -> x3, Pallas kernels: none -> 652 us  [line_sum(): pl.pallas_call(functools.partial(line_sum_kernel, count, pieces, finish,...]
    add x2 -> x0, other arithmetic: 31.3 us -> none  [the longest x1 20.9 us: on_device(): d_inputs = d_resid + d_input_norm]
    reduce_sum x7 -> x8, other arithmetic: 34.2 us -> 8.77 us  [the longest x2 4.63 us: inverse_rms(): return lax.rsqrt(jnp.mean(x * x, axis=-1, keepdims=True) + EPSILON)]
    psum x2 -> x1, blocking collectives: 54.6 us -> 40.2 us  [on_device(): lax.psum((d_norm_gain[0], d_mlp_gain[0], d_qgain, d_kgain), ('dp', 'tenso...]
    convert_element_type x15 -> x13, other arithmetic: 38.2 us -> 51.9 us  [the longest x1 9.34 us: on_device(): d_inputs.astype(F32)]
  transfers between devices with their start and end apart: 4 -> 4, of which waited for: 4 -> 0; matrix products, arithmetic and copies ran while one was open for 8% -> 15% of each run, Pallas kernels for 0% -> 48%
where the time goes in v2:
time: 1110 us; the launch traced here: 1100 us
  Pallas kernels  723 us (65%)
  matrix products  222 us (20%)
  other arithmetic  72.4 us (7%)
  blocking collectives  40.2 us (4%)
  local copies, waits for them, and re-layouts  24.7 us (2%)
  between operations  17.2 us (2%)
    pallas_call x3, Pallas kernels, line_sum(): pl.pallas_call(functools.partial(line_sum_kernel, count, pieces, finish,...  652 us
    dot_general x7, matrix products, nt(): lax.dot_general(a, b, (((1,), (1,)), ((), ())), preferred_element_type=F32)  94.4 us
    dot_general x7, matrix products, nn(): lax.dot_general(a, b, (((1,), (0,)), ((), ())), preferred_element_type=F32)  69.2 us
    dot_general x7, matrix products, tn(): lax.dot_general(a, b, (((0,), (0,)), ((), ())), preferred_element_type=F32)  58.5 us
    pallas_call x1, Pallas kernels, attn_bwd(): pl.pallas_call(functools.partial(bwd_kernel, places, tiles, bq, bk), out_...  49.3 us
    psum x1, blocking collectives, on_device(): lax.psum((d_norm_gain[0], d_mlp_gain[0], d_qgain, d_kgain), ('dp', 'tenso...  40.2 us
  transfers between devices with their start and end apart: 4, of which 0 were waited for; matrix products, arithmetic and copies ran while one was open for 15% of the time, Pallas kernels for 48%

profile of v2, /device:TPU:0, one launch (start us, length us, event | category | flops | bytes accessed | tf_op | source)
XLA Modules:
  0.0 1100.1 jit_solution(6690266109321756838)
XLA Ops:
  43.9 21.8 %attention_forward.1 = (bf16[2048,384]{1,0:T(8,128)(2,1)S(1)}, f32[2048,384]{1,0:T(8,128)}) custom-call(s32[1]{0:T(128)} %copy.55.len_ref, bf16[2048,384]{1,0:T(8,128)(2,1)S(1)} %copy.41.q_ref, bf16[2048,128]{1,0:T(8,128)(2,1)S(1)} %copy.42.k_ref, bf16[2048,128]{1,0:T(8,128)(2,1)S(1)} %copy-done.5), custom_call_target="tpu_custom_call" | custom-call | flops 6442450944 | bytes 6291456 | tf_op jit(solution)/shard_map/attention_forward/pallas_call | solution.py:91
  72.1 171.6 %line_sum.3 = (bf16[2048,1536]{1,0:T(8,128)(2,1)}, f32[512,1536]{1,0:T(8,128)}) custom-call(bf16[2048,1536]{1,0:T(8,128)(2,1)} %convolution_convert_fusion.4.part_ref, f32[512,1536]{1,0:T(8,128)} %dynamic-slice_convert_fusion.1.refs_0_.refs_1_, f32[1,1536]{1,0:T(1,128)} %broadcast_in_dim.14.refs_1_.refs_2_), custom_call_target="tpu_custom_call" | custom-call | flops 25165824 | bytes 25165824 | tf_op jit(solution)/shard_map/line_sum/pallas_call | solution.py:351
  243.8 17.3 %fusion.13 = f32[2048,1728]{0,1:T(8,128)} fusion(bf16[2048,1536]{1,0:T(8,128)(2,1)} %get-tuple-element.34, bf16[1536,1728]{0,1:T(8,128)(2,1)} %param.25), kind=kOutput, calls=%fused_computation.74 | convolution fusion | flops 10871635968 | bytes 25755648 | tf_op jit(solution)/shard_map/dot_general | solution.py:25
  261.1 15.5 %fusion.14 = f32[2048,1728]{0,1:T(8,128)} fusion(bf16[2048,1536]{1,0:T(8,128)(2,1)S(1)} %copy-done.43, bf16[1536,1728]{0,1:T(8,128)(2,1)} %param.26), kind=kOutput, calls=%fused_computation.75 | convolution fusion | flops 10871635968 | bytes 25755648 | tf_op jit(solution)/shard_map/dot_general | solution.py:25
  280.2 25.5 %multiply_convert_fusion = (bf16[2048,1728]{0,1:T(8,128)(2,1)}, bf16[2048,1728]{0,1:T(8,128)(2,1)}, bf16[2048,1728]{0,1:T(8,128)(2,1)}) fusion(f32[2048,1728]{0,1:T(8,128)} %fusion.13, f32[2048,1728]{0,1:T(8,128)} %fusion.14, bf16[2048,1536]{1,0:T(8,128)(2,1)} %broadcast_select_fusion, bf16[1728,1536]{1,0:T(8,128)(2,1)S(1)} %bitcast.113), kind=kOutput, calls=%fused_computation.2 | convolution fusion | flops 10928259072 | bytes 61145088 | tf_op jit(solution)/shard_map/dot_general | solution.py:23
  305.8 16.9 %convolution_convert_fusion = bf16[1536,1728]{0,1:T(8,128)(2,1)} fusion(bf16[2048,1728]{0,1:T(8,128)(2,1)} %get-tuple-element.62, bf16[2048,1536]{1,0:T(8,128)(2,1)} %get-tuple-element.34), kind=kOutput, calls=%fused_computation.11 | convolution fusion | flops 10874290176 | bytes 18677760 | tf_op jit(solution)/shard_map/dot_general | solution.py:24
  322.7 15.1 %convolution_convert_fusion.1 = bf16[1536,1728]{0,1:T(8,128)(2,1)} fusion(bf16[2048,1728]{0,1:T(8,128)(2,1)S(1)} %copy-done.44, bf16[2048,1536]{1,0:T(8,128)(2,1)} %get-tuple-element.34), kind=kOutput, calls=%fused_computation.12 | convolution fusion | flops 10874290176 | bytes 18677760 | tf_op jit(solution)/shard_map/dot_general | solution.py:24
  337.9 12.8 %convolution_convert_fusion.2 = bf16[1728,1536]{1,0:T(8,128)(2,1)} fusion(bf16[2048,1728]{0,1:T(8,128)(2,1)S(1)} %bitcast.117, bf16[2048,1536]{1,0:T(8,128)(2,1)S(1)} %bitcast.102), kind=kOutput, calls=%fused_computation.13 | convolution fusion | flops 10874290176 | bytes 18677760 | tf_op jit(solution)/shard_map/dot_general | solution.py:24
  350.7 17.2 %convolution_convert_fusion.3 = bf16[2048,1536]{1,0:T(8,128)(2,1)} fusion(bf16[2048,1728]{0,1:T(8,128)(2,1)} %get-tuple-element.64, bf16[1728,1536]{1,0:T(8,128)(2,1)} %param.27), kind=kOutput, calls=%fused_computation.14 | convolution fusion | flops 10874781696 | bytes 18677760 | tf_op jit(solution)/shard_map/dot_general | solution.py:25
  371.7 19.5 %fusion.15 = f32[2048,1536]{1,0:T(8,128)} fusion(bf16[2048,1728]{0,1:T(8,128)(2,1)} %get-tuple-element.63, bf16[1536,1728]{0,1:T(8,128)(2,1)} %param.25), kind=kOutput, calls=%fused_computation.76 | convolution fusion | flops 10871635968 | bytes 24969216 | tf_op jit(solution)/shard_map/dot_general | solution.py:23
  391.3 16.0 %add_convert_fusion.1.part_ref = bf16[2048,1536]{1,0:T(8,128)(2,1)} fusion(f32[2048,1536]{1,0:T(8,128)} %fusion.15, bf16[2048,1728]{0,1:T(8,128)(2,1)S(1)} %bitcast.119, bf16[1536,1728]{0,1:T(8,128)(2,1)S(1)} %bitcast.115), kind=kOutput, calls=%fused_computation.10 | convolution fusion | flops 10877927424 | bytes 31260672 | tf_op jit(solution)/shard_map/dot_general | solution.py:23
  407.3 231.7 %line_sum.4 = (bf16[2048,1536]{1,0:T(8,128)(2,1)}, f32[512,1536]{1,0:T(8,128)}, f32[1,1536]{1,0:T(1,128)}) custom-call(bf16[2048,1536]{1,0:T(8,128)(2,1)} %add_convert_fusion.1.part_ref, f32[512,1536]{1,0:T(8,128)} %dynamic-slice_convert_fusion.refs_0_, f32[512,1536]{1,0:T(8,128)} %get-tuple-element.33.refs_1_, f32[1,1536]{1,0:T(1,128)} %broadcast_in_dim.14.refs_1_.refs_2_), custom_call_target="tpu_custom_call" | custom-call | flops 25165824 | bytes 25165824 | tf_op jit(solution)/shard_map/line_sum/pallas_call | solution.py:351
  639.0 7.5 convolution_convert_fusion.7.do_ref
  646.5 49.3 %attention_backward.1 = (f32[2048,384]{1,0:T(8,128)}, f32[2048,128]{1,0:T(8,128)S(1)}, f32[2048,128]{1,0:T(8,128)S(1)}) custom-call(s32[1]{0:T(128)} %copy.55.len_ref, bf16[2048,384]{1,0:T(8,128)(2,1)S(1)} %copy-done.2, bf16[2048,384]{1,0:T(8,128)(2,1)} %convolution_convert_fusion.7.do_ref, bf16[2048,384]{1,0:T(8,128)(2,1)} %copy-done.7, ...), custom_call_target="tpu_custom_call" | custom-call | flops 16106127360 | bytes 11010048 | tf_op jit(solution)/shard_map/attention_backward/pallas_call | solution.py:157
  731.7 6.5 fusion.17
  738.1 6.8 fusion.16
  744.9 12.6 %add_convert_fusion.part_ref = bf16[2048,1536]{1,0:T(8,128)(2,1)} fusion(f32[2048,1536]{1,0:T(8,128)} %fusion.16, f32[2048,1536]{1,0:T(8,128)} %fusion.17, bf16[1536,128]{1,0:T(8,128)(2,1)S(1)} %copy-done.28, f32[2048,128]{1,0:T(8,128)S(1)} %get-tuple-element.39), kind=kOutput, calls=%fused_computation.9 | convolution fusion | flops 815005696 | bytes 32899072 | tf_op jit(solution)/shard_map/dot_general | solution.py:23
  757.5 248.8 %line_sum.5 = (bf16[2048,1536]{1,0:T(8,128)(2,1)}, f32[512,1536]{1,0:T(8,128)}, f32[1,1536]{1,0:T(1,128)}) custom-call(bf16[2048,1536]{1,0:T(8,128)(2,1)} %add_convert_fusion.part_ref, f32[512,1536]{1,0:T(8,128)} %get-tuple-element.40.refs_0_, f32[512,1536]{1,0:T(8,128)} %dynamic-slice_convert_fusion.1.refs_0_.refs_1_, f32[1,1536]{1,0:T(1,128)} %broadcast_in_dim.17.refs_2_), custom_call_target="tpu_custom_call" | custom-call | flops 25165824 | bytes 25165824 | tf_op jit(solution)/shard_map/line_sum/pallas_call | solution.py:351
  1007.1 9.3 convert_element_type.201
  1016.4 40.2 %all-reduce = (f32[1536]{0:T(1024)}, f32[64]{0:T(128)}, f32[64]{0:T(128)}, f32[1536]{0:T(1024)}) all-reduce(f32[1536]{0:T(1024)S(1)} %reduce.6, f32[64]{0:T(128)S(1)} %reduce_sum.100, f32[64]{0:T(128)S(1)} %reduce_sum.103, f32[1536]{0:T(1024)S(1)} %reduce.7), channel_id=1, replica_groups=mesh['dp'=8,'tensor'=4] {'dp','tensor'}, use_global_device_ids=true, to_apply=%region_6.7 | all-reduce | flops 3200 | bytes 25600 | tf_op jit(solution)/shard_map/psum | solution.py:551
  1056.6 8.3 convert_element_type.213
  1064.9 8.2 convert_element_type.214
  1073.1 5.6 convert_element_type.215
  1086.5 5.9 copy.56
  (203 shorter events, 92.8 us)
Async XLA Ops:
  8.0 58.9 %copy-start = (bf16[384,1536]{1,0:T(8,128)(2,1)S(1)}, bf16[384,1536]{1,0:T(8,128)(2,1)}, u32[]{:S(2)}) copy-start(bf16[384,1536]{1,0:T(8,128)(2,1)} %param.21) | copy-start | bytes 3538948
  8.0 718.6 %all-reduce.8.cloned.1.call-start = ((), (), s32[]{:S(2)}) async-start(), calls=%async_computation.4 | async-start | bytes 31850496 | tf_op jit(solution)/shard_map/psum | solution.py:525
  23.7 19.2 %copy-start.1 = (bf16[2048,384]{1,0:T(8,128)(2,1)}, bf16[2048,384]{1,0:T(8,128)(2,1)S(1)}, u32[]{:S(2)}) copy-start(bf16[2048,384]{1,0:T(8,128)(2,1)S(1)} %copy.41.q_ref) | copy-start | bytes 4718596
  243.8 17.4 %copy-start.43 = (bf16[2048,1536]{1,0:T(8,128)(2,1)S(1)}, bf16[2048,1536]{1,0:T(8,128)(2,1)}, u32[]{:S(2)}) copy-start(bf16[2048,1536]{1,0:T(8,128)(2,1)} %get-tuple-element.34) | copy-start | bytes 18874372
  243.8 32.9 %slice-start.4 = ((s8[6291456]{0:T(1024)(128)(4,1)}), s8[4194304]{0:T(1024)(128)(4,1)S(1)}, s32[]{:S(2)}) async-start(s8[6291456]{0:T(1024)(128)(4,1)} %bitcast.104), calls=%async_computation.9 | async-start | bytes 8388608
  243.8 36.4 %slice-start.10 = ((s8[5308416]{0:T(1024)(128)(4,1)}), s8[4194304]{0:T(1024)(128)(4,1)S(1)}, s32[]{:S(2)}) async-start(s8[5308416]{0:T(1024)(128)(4,1)} %bitcast.112), calls=%async_computation.15 | async-start | bytes 8388608
  261.1 15.5 %slice-start.5 = ((s8[6291456]{0:T(1024)(128)(4,1)}), s8[2097152]{0:T(1024)(128)(4,1)S(1)}, s32[]{:S(2)}) async-start(s8[6291456]{0:T(1024)(128)(4,1)} %bitcast.104), calls=%async_computation.10 | async-start | bytes 4194304
  261.1 19.1 %slice-start.11 = ((s8[5308416]{0:T(1024)(128)(4,1)}), s8[1114112]{0:T(1024)(128)(4,1)S(1)}, s32[]{:S(2)}) async-start(s8[5308416]{0:T(1024)(128)(4,1)} %bitcast.112), calls=%async_computation.16 | async-start | bytes 2228224
  305.7 17.0 %copy-start.44 = (bf16[2048,1728]{0,1:T(8,128)(2,1)S(1)}, bf16[2048,1728]{0,1:T(8,128)(2,1)}, u32[]{:S(2)}) copy-start(bf16[2048,1728]{0,1:T(8,128)(2,1)} %get-tuple-element.63) | copy-start | bytes 21233668
  305.7 32.1 %slice-start.2 = ((s8[6291456]{0:T(1024)(128)(4,1)}), s8[4194304]{0:T(1024)(128)(4,1)S(1)}, s32[]{:S(2)}) async-start(s8[6291456]{0:T(1024)(128)(4,1)} %bitcast.101), calls=%async_computation.7 | async-start | bytes 8388608
  305.8 32.1 %slice-start.14 = ((s8[7077888]{0:T(1024)(128)(4,1)}), s8[4194304]{0:T(1024)(128)(4,1)S(1)}, s32[]{:S(2)}) async-start(s8[7077888]{0:T(1024)(128)(4,1)} %bitcast.116), calls=%async_computation.19 | async-start | bytes 8388608
  322.7 15.1 %slice-start.3 = ((s8[6291456]{0:T(1024)(128)(4,1)}), s8[2097152]{0:T(1024)(128)(4,1)S(1)}, s32[]{:S(2)}) async-start(s8[6291456]{0:T(1024)(128)(4,1)} %bitcast.101), calls=%async_computation.8 | async-start | bytes 4194304
  322.7 15.2 %slice-start.15 = ((s8[7077888]{0:T(1024)(128)(4,1)}), s8[2883584]{0:T(1024)(128)(4,1)S(1)}, s32[]{:S(2)}) async-start(s8[7077888]{0:T(1024)(128)(4,1)} %bitcast.116), calls=%async_computation.20 | async-start | bytes 5767168
  350.7 376.0 %reduce-scatter.2.cloned.1.call-start = ((), (), s32[]{:S(2)}) async-start(), calls=%async_computation.1 | async-start | bytes 7864320 | tf_op jit(solution)/shard_map/reduce_scatter | solution.py:508
  367.9 23.3 %slice-start.12 = ((s8[5308416]{0:T(1024)(128)(4,1)}), s8[1114112]{0:T(1024)(128)(4,1)S(1)}, s32[]{:S(2)}) async-start(s8[5308416]{0:T(1024)(128)(4,1)} %bitcast.114), calls=%async_computation.17 | async-start | bytes 2228224
  367.9 710.8 %all-reduce.6.cloned.1.call-start = ((), (), s32[]{:S(2)}) async-start(), calls=%async_computation.3 | async-start | bytes 6291456 | tf_op jit(solution)/shard_map/psum | solution.py:550
  368.0 23.3 %slice-start.16 = ((s8[7077888]{0:T(1024)(128)(4,1)}), s8[4194304]{0:T(1024)(128)(4,1)S(1)}, s32[]{:S(2)}) async-start(s8[7077888]{0:T(1024)(128)(4,1)} %bitcast.118), calls=%async_computation.21 | async-start | bytes 8388608
  371.7 19.6 %slice-start.13 = ((s8[5308416]{0:T(1024)(128)(4,1)}), s8[4194304]{0:T(1024)(128)(4,1)S(1)}, s32[]{:S(2)}) async-start(s8[5308416]{0:T(1024)(128)(4,1)} %bitcast.114), calls=%async_computation.18 | async-start | bytes 8388608
  371.7 19.6 %slice-start.17 = ((s8[7077888]{0:T(1024)(128)(4,1)}), s8[2883584]{0:T(1024)(128)(4,1)S(1)}, s32[]{:S(2)}) async-start(s8[7077888]{0:T(1024)(128)(4,1)} %bitcast.118), calls=%async_computation.22 | async-start | bytes 5767168
  695.9 11.7 %copy-start.32 = (f32[2048,2]{0,1:T(2,128)S(1)}, f32[2048,2]{0,1:T(2,128)}, u32[]{:S(2)}) copy-start(f32[2048,2]{0,1:T(2,128)} %copy-done.31) | copy-start | bytes 49156
  697.2 10.4 copy-start.14
  726.7 359.9 %all-gather.2.cloned.1.call-start = ((), (), s32[]{:S(2)}) async-start(), calls=%async_computation.2 | async-start | bytes 7864320 | tf_op jit(solution)/shard_map/all_gather | solution.py:511
  757.5 249.5 %copy-start.37 = (f32[1,1536]{1,0:T(1,128)S(1)}, f32[1,1536]{1,0:T(1,128)}, u32[]{:S(2)}) copy-start(f32[1,1536]{1,0:T(1,128)} %get-tuple-element.47) | copy-start | bytes 18436
  1056.6 16.5 %slice-start.6 = ((s8[5308416]{0:T(1024)(128)(4,1)}), s8[4194304]{0:T(1024)(128)(4,1)S(1)}, s32[]{:S(2)}) async-start(s8[5308416]{0:T(1024)(128)(4,1)} %bitcast.106), calls=%async_computation.11 | async-start | bytes 8388608
  (43 other events, 206.3 us)
Sparse Core Ops, SparseCore 0:
  350.8 207.8 all-reduce.7
  726.8 70.5 all-reduce.5
Sparse Core Ops, SparseCore 1:
  368.0 171.1 reduce-scatter.1
  730.9 191.0 all-gather.1

commit v3 on v2

--- a/solution.py
+++ b/solution.py
@@ -54,55 +54,6 @@
         high = pieces.get((tile, 1))
         out.append(jnp.where(half_mask(0), low, 0.0 if high is None else high))
     return jnp.concatenate(out, axis=1)
-
-def fwd_kernel(places, tiles, bq, bk, len_ref, q_ref, k_ref, v_ref, o_ref, linv_ref, q6, vx, acc):
-    i = pl.program_id(0)
-    heads = len(places)
-    rows = k_ref.shape[0]
-    @pl.when(i == 0)
-    def _():
-        live = lax.broadcasted_iota(jnp.int32, (rows, LANES), 0) < len_ref[0]
-        vx[:, :LANES] = jnp.where(live, v_ref[...].astype(F32), 0.0).astype(BF16)
-        vx[:, LANES:] = jnp.where(live, 1.0, 0.0).astype(BF16)
-    q6[...] = stack_heads(q_ref[...].astype(F32), places).astype(BF16)
-    acc[...] = jnp.zeros_like(acc)
-    def step(j, masked):
-        ks = pl.ds(pl.multiple_of(j * bk, bk), bk)
-        s = nt(q6[...], k_ref[ks, :])
-        p = jnp.exp2(s * (SCALE * LOG2E))
-        if masked:
-            qp = i * bq + (lax.broadcasted_iota(jnp.int32, s.shape, 0) & (bq - 1))
-            kp = j * bk + lax.broadcasted_iota(jnp.int32, s.shape, 1)
-            p = jnp.where(kp <= qp, p, 0.0)
-        acc[...] += nn(p.astype(BF16), vx[ks, :])
-    full = (i * bq) // bk
-    @pl.loop(0, full)
-    def _(j): step(j, False)
-    @pl.loop(full, full + max(bq // bk, 1))
-    def _(j): step(j, True)
-    inv = 1.0 / acc[:, LANES:]
-    o_ref[...] = unstack_heads(acc[:, :LANES] * inv, places, tiles, bq).astype(BF16)
-    linv_ref[...] = unstack_heads(inv, places, tiles, bq)
-
-def attn_fwd(length, q, k, v, heads, group, bq=256, bk=256):
-    rows, width = q.shape
-    tiles = width // LANES
-    places = head_places(heads, group)
-    return pl.pallas_call(
-        functools.partial(fwd_kernel, places, tiles, bq, bk),
-        out_shape=(jax.ShapeDtypeStruct((rows, width), BF16), jax.ShapeDtypeStruct((rows, width), F32)),
-        grid_spec=pltpu.PrefetchScalarGridSpec(
-            num_scalar_prefetch=1, grid=(rows // bq,),
-            in_specs=[pl.BlockSpec((bq, width), lambda i, n: (i, 0)),
-                      pl.BlockSpec((rows, LANES), lambda i, n: (0, 0)),
-                      pl.BlockSpec((rows, LANES), lambda i, n: (0, 0))],
-            out_specs=[pl.BlockSpec((bq, width), lambda i, n: (i, 0))] * 2,
-            scratch_shapes=[pltpu.VMEM((heads * bq, LANES), BF16), pltpu.VMEM((rows, 2 * LANES), BF16),
-                            pltpu.VMEM((heads * bq, 2 * LANES), F32)]),
-        compiler_params=pltpu.CompilerParams(dimension_semantics=("arbitrary",), vmem_limit_bytes=48 << 20),
-        cost_estimate=pl.CostEstimate(flops=heads * rows * rows * 2 * LANES, transcendentals=heads * rows * rows // 2, bytes_accessed=rows * width * 8),
-        name="attention_forward",
-    )(length, q, k, v)
 
 def bwd_kernel(places, tiles, bq, bk, len_ref, q_ref, do_ref, o_ref, linv_ref, k_ref, v_ref, dq_ref, dk_ref, dv_ref, q6, do6, d_row, kx, dq6):
     i = pl.program_id(0)
@@ -165,7 +116,7 @@
                             pltpu.VMEM((16, heads * bq), F32), pltpu.VMEM((rows, LANES), BF16),
                             pltpu.VMEM((heads * bq, LANES), F32)]),
         compiler_params=pltpu.CompilerParams(dimension_semantics=("arbitrary",), vmem_limit_bytes=48 << 20),
-        cost_estimate=pl.CostEstimate(flops=heads * rows * rows * 5 * LANES, transcendentals=heads * rows * rows // 2, bytes_accessed=rows * width * 14),
+        cost_estimate=pl.CostEstimate(flops=rows * width, transcendentals=0, bytes_accessed=rows * width * 2),
         name="attention_backward",
     )(length, q, do, o, linv, k, v)
 
@@ -181,17 +132,30 @@
     )
 
 
-def greet_line(count):
+def greet_line(count, everyone=False):
     me = lax.axis_index("tensor")
     barrier = pltpu.get_barrier_semaphore()
 
+    def greet(peer):
+        pl.semaphore_signal(barrier, inc=1, device_id={"tensor": peer}, device_id_type=MESH)
+
+    if everyone:
+        for peer in range(count):
+
+            @pl.when(peer != me)
+            def _():
+                greet(peer)
+
+        pl.semaphore_wait(barrier, count - 1)
+        return
+
     @pl.when(me > 0)
     def _():
-        pl.semaphore_signal(barrier, inc=1, device_id={"tensor": me - 1}, device_id_type=MESH)
+        greet(me - 1)
 
     @pl.when(me < count - 1)
     def _():
-        pl.semaphore_signal(barrier, inc=1, device_id={"tensor": me + 1}, device_id_type=MESH)
+        greet(me + 1)
 
     @pl.when((me > 0) & (me < count - 1))
     def _():
@@ -203,11 +167,11 @@
 
 
 def line_sum_kernel(
-    count, pieces, finish, kinds, part_ref, *refs
+    count, pieces, finish, kinds, share_terms, part_ref, *refs
 ):
     (own_refs, full_ref, out_refs), scratch = split_refs(refs, kinds)
-    up_buf, down_buf, acc = scratch[:3]
-    sems = scratch[3:]
+    up_buf, down_buf, acc, shared = scratch[:4]
+    sems = scratch[4:]
     sum_up, sum_down, give_up, give_down = (sems[0:2], sems[2:4], sems[4:6], sems[6:8])
     me = lax.axis_index("tensor")
     last = count - 1
@@ -287,7 +251,17 @@
         mine = pl.ds(c * size, size)
         full_ref[rows(me, c), :] = finish(c, mine, acc[...], own_refs, out_refs)
 
-    greet_line(count)
+    def share(to):
+        return pltpu.make_async_remote_copy(
+            src_ref=out_refs[1],
+            dst_ref=shared.at[me],
+            send_sem=sems[8].at[to],
+            recv_sem=sems[9].at[me],
+            device_id={"tensor": to},
+            device_id_type=MESH,
+        )
+
+    greet_line(count, share_terms)
     for slot in range(pieces + 2 * last):
         if slot < pieces:
             for upward in (True, False):
@@ -302,6 +276,12 @@
             settle(c)
             for upward in (True, False):
                 give_start(c, 1, upward)
+            if share_terms and c == pieces - 1:
+                for to in range(count):
+
+                    @pl.when(to != me)
+                    def _():
+                        share(to).start()
         for s in range(last, 1, -1):
             c = slot - (s - 1)
             if 0 <= c < pieces:
@@ -333,6 +313,30 @@
                 def _():
                     give_copy(c, s, upward).wait_send()
 
+    if share_terms:
+        for peer in range(count):
+
+            @pl.when(peer != me)
+            def _():
+                share(peer).wait_send()
+                pltpu.make_async_remote_copy(
+                    src_ref=out_refs[1],
+                    dst_ref=shared.at[peer],
+                    send_sem=sems[8].at[peer],
+                    recv_sem=sems[9].at[peer],
+                    device_id={"tensor": peer},
+                    device_id_type=MESH,
+                ).wait_recv()
+
+            @pl.when(peer == me)
+            def _():
+                shared[peer] = out_refs[1][...]
+
+        terms = shared[0]
+        for peer in range(1, count):
+            terms = terms + shared[peer]
+        out_refs[1][...] = terms
+
 
 def split_refs(refs, kinds):
     n_own, n_out = kinds
@@ -342,14 +346,14 @@
     return (own_refs, full_ref, out_refs), refs[n_own + 1 + n_out :]
 
 
-def line_sum(part, owned, outs, finish, pieces, collective_id):
+def line_sum(part, owned, outs, finish, pieces, collective_id, share_terms=False):
     count = lax.axis_size("tensor")
     rows, width = part.shape
     size = rows // count // pieces
     vmem = pl.BlockSpec(memory_space=pltpu.VMEM)
     hops = (pieces, count - 1)
     return pl.pallas_call(
-        functools.partial(line_sum_kernel, count, pieces, finish, (len(owned), len(outs))),
+        functools.partial(line_sum_kernel, count, pieces, finish, (len(owned), len(outs)), share_terms),
         out_shape=(jax.ShapeDtypeStruct((rows, width), BF16), *outs),
         in_specs=[vmem] * (1 + len(owned)),
         out_specs=(vmem,) * (1 + len(outs)),
@@ -357,27 +361,22 @@
             pltpu.VMEM((*hops, size, width), BF16),
             pltpu.VMEM((*hops, size, width), BF16),
             pltpu.VMEM((size, width), F32),
+            pltpu.VMEM((count, 8, width), F32),
         ]
-        + [pltpu.SemaphoreType.DMA(hops)] * 8,
+        + [pltpu.SemaphoreType.DMA(hops)] * 8
+        + [pltpu.SemaphoreType.DMA((count,))] * 2,
         compiler_params=pltpu.CompilerParams(
             collective_id=collective_id, has_side_effects=True, vmem_limit_bytes=56 << 20
         ),
         cost_estimate=pl.CostEstimate(
-            flops=rows * width * 8, transcendentals=0, bytes_accessed=rows * width * 8
+            flops=rows * width * 8, transcendentals=0, bytes_accessed=rows * width * 200
         ),
         name="line_sum",
     )(part, *owned)
 
 
-def finish_attention(c, mine, total, own_refs, out_refs):
-    inputs, gain = own_refs
-    resid = inputs[mine, :] + total
-    out_refs[0][mine, :] = resid
-    return (resid * inverse_rms(resid) * gain[...]).astype(BF16)
-
-
 def finish_back(c, mine, total, own_refs, out_refs):
-    base, value, gain = own_refs
+    base, value, gain = own_refs[:3]
     x = value[mine, :]
     r = inverse_rms(x)
     y = x * r
@@ -385,15 +384,241 @@
     out = base[mine, :] + r * (e - y * jnp.mean(e * y, axis=-1, keepdims=True))
     out_refs[0][mine, :] = out
     term = jnp.sum(total * y, axis=0, keepdims=True)
+    row = lax.broadcasted_iota(jnp.int32, (8, 1), 0)
     if c == 0:
-        out_refs[1][...] = term
+        more = own_refs[3][...] if len(own_refs) > 3 else 0.0
+        out_refs[1][...] = jnp.where(row == 0, term, more)
     else:
-        out_refs[1][...] += term
+        out_refs[1][...] += jnp.where(row == 0, term, 0.0)
     return out.astype(BF16)
 
 
-def finish_add(c, mine, total, own_refs, out_refs):
-    return (own_refs[0][mine, :] + total).astype(BF16)
+def attn_gather_kernel(
+    count,
+    ways,
+    places,
+    tiles,
+    bq,
+    len_ref,
+    q_ref,
+    k_ref,
+    v_ref,
+    w_ref,
+    full_ref,
+    linv_ref,
+    whole_ref,
+    q6,
+    vx,
+    acc,
+    *sems,
+):
+    give_up, give_down, line_sems, way_sems = sems[0:2], sems[2:4], sems[4:6], sems[6:8]
+    me = lax.axis_index("tensor")
+    spot = lax.axis_index("dp")
+    piece = w_ref.shape[0] // ways
+    weight_slots = [1, 3, 4, 5]
+    levels = ways.bit_length() - 1
+    last = count - 1
+    rows, width = q_ref.shape
+    chunks = rows // bq
+
+    def place(block, c):
+        at = pl.multiple_of(block * width, width)
+        return full_ref.at[pl.ds(c * bq, bq), pl.ds(at, width)]
+
+    def copy(c, s, upward):
+        there = place(me - s + 1 if upward else me + s - 1, c)
+        sem = give_up if upward else give_down
+        return line_copy(there, there, sem, (c, s - 1), me + 1 if upward else me - 1)
+
+    def wait(c, s, upward):
+        there = place(me - s if upward else me + s, c)
+        sem = give_up if upward else give_down
+        line_copy(there, there, sem, (c, s - 1), me + 1 if upward else me - 1).wait_recv()
+
+    def sends(s, upward):
+        return (me >= s - 1) & (me < last) if upward else (me > 0) & (me <= count - s)
+
+    def start(c, s, upward):
+        if s > 1:
+
+            @pl.when((me >= s - 1) if upward else (me <= count - s))
+            def _():
+                wait(c, s - 1, upward)
+
+        @pl.when(sends(s, upward))
+        def _():
+            copy(c, s, upward).start()
+
+    def attend(c):
+        first = c * bq
+        span = pl.ds(first, bq)
+        q6[...] = stack_heads(q_ref[span, :].astype(F32), places).astype(BF16)
+        acc[...] = jnp.zeros_like(acc)
+
+        def step(j, masked):
+            ks = pl.ds(pl.multiple_of(j * bq, bq), bq)
+            prob = jnp.exp2(nt(q6[...], k_ref[ks, :]) * (SCALE * LOG2E))
+            if masked:
+                q_pos = lax.broadcasted_iota(jnp.int32, prob.shape, 0) & (bq - 1)
+                k_pos = lax.broadcasted_iota(jnp.int32, prob.shape, 1)
+                prob = jnp.where(k_pos <= q_pos, prob, 0.0)
+            acc[...] += nn(prob.astype(BF16), vx[ks, :])
+
+        if c > 0:
+
+            @pl.loop(0, c)
+            def _(j):
+                step(j, False)
+
+        step(c, True)
+        inv = 1.0 / acc[:, LANES:]
+        out = unstack_heads(acc[:, :LANES] * inv, places, tiles, bq)
+        place(me, c)[...] = out.astype(BF16)
+        linv_ref[span, :] = unstack_heads(inv, places, tiles, bq)
+
+
+    bits = [(spot // (1 << (levels - 1 - level))) % 2 for level in range(levels)]
+
+    def own_part(peer, sender):
+        return pltpu.make_async_remote_copy(
+            src_ref=whole_ref.at[(me, *bits)],
+            dst_ref=whole_ref.at[(sender, *bits)],
+            send_sem=line_sems[0].at[peer],
+            recv_sem=line_sems[1].at[sender],
+            device_id={"tensor": peer},
+            device_id_type=MESH,
+        )
+
+    def partner(level):
+        return spot + (1 - 2 * bits[level]) * (1 << (levels - 1 - level))
+
+    def held_parts(level, theirs=False):
+        ours = [1 - bits[level] if theirs else bits[level], *bits[level + 1 :]]
+        there = whole_ref.at[(slice(None),) * (level + 1) + tuple(ours)]
+        return pltpu.make_async_remote_copy(
+            src_ref=there,
+            dst_ref=there,
+            send_sem=way_sems[0].at[level],
+            recv_sem=way_sems[1].at[level],
+            device_id={"dp": partner(level)},
+            device_id_type=MESH,
+        )
+
+    def weight_step(step):
+        if step == 0:
+            mine = pl.ds(pl.multiple_of(spot * piece, piece), piece)
+            whole_ref[(me, *bits)] = w_ref[mine, :]
+            for peer in range(count):
+
+                @pl.when(peer != me)
+                def _():
+                    own_part(peer, me).start()
+
+            return
+        if step == 1:
+            for peer in range(count):
+
+                @pl.when(peer != me)
+                def _():
+                    own_part(peer, peer).wait_recv()
+
+        else:
+            held_parts(step - 2, True).wait_recv()
+        if step - 1 < levels:
+            held_parts(step - 1).start()
+
+    barrier = pltpu.get_barrier_semaphore()
+    for peer in range(count):
+
+        @pl.when(peer != me)
+        def _():
+            pl.semaphore_signal(barrier, inc=1, device_id={"tensor": peer}, device_id_type=MESH)
+
+    for level in range(levels):
+        pl.semaphore_signal(
+            barrier, inc=1, device_id={"dp": partner(level)}, device_id_type=MESH
+        )
+    pl.semaphore_wait(barrier, count - 1 + levels)
+    weight_step(0)
+    live = lax.broadcasted_iota(jnp.int32, (rows, LANES), 0) < len_ref[0]
+    vx[:, :LANES] = jnp.where(live, v_ref[...].astype(F32), 0.0).astype(BF16)
+    vx[:, LANES:] = jnp.where(live, 1.0, 0.0).astype(BF16)
+    for slot in range(chunks + last):
+        if slot < chunks:
+            attend(slot)
+            for upward in (True, False):
+                start(slot, 1, upward)
+        for s in range(last, 1, -1):
+            c = slot - (s - 1)
+            if 0 <= c < chunks:
+                for upward in (True, False):
+                    start(c, s, upward)
+        if slot in weight_slots:
+            weight_step(1 + weight_slots.index(slot))
+    for step in range(1 + len(weight_slots), levels + 2):
+        weight_step(step)
+    for peer in range(count):
+
+        @pl.when(peer != me)
+        def _():
+            own_part(peer, me).wait_send()
+
+    for level in range(levels):
+        held_parts(level).wait_send()
+    for c in range(chunks):
+
+        @pl.when(me == last)
+        def _():
+            wait(c, last, True)
+
+        @pl.when(me == 0)
+        def _():
+            wait(c, last, False)
+
+        for s in range(1, count):
+            for upward in (True, False):
+
+                @pl.when(sends(s, upward))
+                def _():
+                    copy(c, s, upward).wait_send()
+
+
+def attn_gather(length, q, k, v, w, heads, group, bq, collective_id):
+    count = lax.axis_size("tensor")
+    ways = lax.axis_size("dp")
+    rows, width = q.shape
+    vmem = pl.BlockSpec(memory_space=pltpu.VMEM)
+    hops = (rows // bq, count - 1)
+    return pl.pallas_call(
+        functools.partial(
+            attn_gather_kernel, count, ways, head_places(heads, group), width // LANES, bq
+        ),
+        out_shape=(
+            jax.ShapeDtypeStruct((rows, count * width), BF16),
+            jax.ShapeDtypeStruct((rows, width), F32),
+            jax.ShapeDtypeStruct((count, *(2,) * (ways.bit_length() - 1), w.shape[0] // ways, w.shape[1]), BF16),
+        ),
+        in_specs=[pl.BlockSpec(memory_space=pltpu.SMEM), vmem, vmem, vmem, vmem],
+        out_specs=(vmem, vmem, vmem),
+        scratch_shapes=[
+            pltpu.VMEM((heads * bq, LANES), BF16),
+            pltpu.VMEM((rows, 2 * LANES), BF16),
+            pltpu.VMEM((heads * bq, 2 * LANES), F32),
+        ]
+        + [pltpu.SemaphoreType.DMA(hops)] * 4
+        + [pltpu.SemaphoreType.DMA((count,))] * 2
+        + [pltpu.SemaphoreType.DMA((ways,))] * 2,
+        compiler_params=pltpu.CompilerParams(
+            collective_id=collective_id, has_side_effects=True, vmem_limit_bytes=56 << 20
+        ),
+        cost_estimate=pl.CostEstimate(
+            flops=heads * rows * rows * 2 * LANES,
+            transcendentals=heads * rows * rows // 2,
+            bytes_accessed=rows * count * width * 120,
+        ),
+        name="attention_gather",
+    )(length, q, k, v, w)
 
 
 def inverse_rms(x):
@@ -443,6 +668,11 @@
 def to_lanes(x):
     short = -x.shape[1] % LANES
     return x if short == 0 else jnp.pad(x, ((0, 0), (0, short)))
+
+
+def pad_rows(w):
+    short = -w.shape[0] % LANES
+    return w if short == 0 else jnp.pad(w, ((0, short), (0, 0)))
 
 
 def on_device(
@@ -470,7 +700,7 @@
     heads = q_width // HEAD_SIZE
     group = q_width // k_width
     own_shape = jax.ShapeDtypeStruct((m, width), F32)
-    gain_shape = jax.ShapeDtypeStruct((1, width), F32)
+    gain_shape = jax.ShapeDtypeStruct((8, width), F32)
 
     def own(x):
         return lax.dynamic_slice_in_dim(x, me * m, m, axis=0)
@@ -486,31 +716,28 @@
     q_pad = to_lanes(prepare(queries, query_gain, tables).astype(BF16))
     k_pad = to_lanes(prepare(keys_val, key_gain, tables).astype(BF16))
     v_pad = to_lanes(nn(normed, value_weight).astype(BF16))
-    mixed_pad, inverse_sums = attn_fwd(lengths, q_pad, k_pad, v_pad, heads, group, 512, 512)
+    mixed_all, inverse_sums, out_whole = attn_gather(
+        lengths, q_pad, k_pad, v_pad, pad_rows(out_w), heads, group, min(512, row_count), 1
+    )
+    resid = inputs + nn(mixed_all, out_whole.reshape(-1, width))
+    normed2 = (resid * inverse_rms(resid) * mlp_gain).astype(BF16)
+    resid_own = own(resid)
+    padded = q_pad.shape[1]
+    mixed_pad = lax.dynamic_slice_in_dim(mixed_all, me * padded, padded, axis=1)
     mixed = mixed_pad[:, :q_width]
-
-    normed2, resid_own = line_sum(
-        nn(mixed, out_w).astype(BF16),
-        (inputs_own, mlp_gain[None]),
-        (own_shape,),
-        finish_attention,
-        PIECES,
-        1,
-    )
     gate = nn(normed2, gate_w)
     up = nn(normed2, up_w)
     sig = jax.nn.sigmoid(gate)
     hidden = (gate * sig * up).astype(BF16)
+    mlp_part = nn(hidden, down_w).astype(BF16)
+    mlp_part, gate, up = lax.optimization_barrier((mlp_part, gate, up))
+    mlp_own = lax.psum_scatter(mlp_part, "tensor", scatter_dimension=0, tiled=True)
+    sig = jax.nn.sigmoid(gate)
     d_hidden = nt(d_out, down_w)
     d_gate = (d_hidden * up * sig * (1.0 + gate * (1.0 - sig))).astype(BF16)
     d_up = (d_hidden * gate * sig).astype(BF16)
     d_normed2 = (nt(d_gate, gate_w) + nt(d_up, up_w)).astype(BF16)
-    mlp_own = lax.psum_scatter(
-        nn(hidden, down_w).astype(BF16), "tensor", scatter_dimension=0, tiled=True
-    )
-    block_out = lax.all_gather(
-        (resid_own + mlp_own.astype(F32)).astype(BF16), "tensor", axis=0, tiled=True
-    )
+    d_normed2, mlp_own = lax.optimization_barrier((d_normed2, mlp_own))
     d_resid, d_resid_own, d_mlp_gain = line_sum(
         d_normed2,
         (own(d_out).astype(F32), resid_own, mlp_gain[None]),
@@ -524,6 +751,10 @@
     g_down = tn(hidden, d_out).astype(BF16)
     g_gate, g_up, g_down = lax.psum((g_gate, g_up, g_down), "dp")
 
+    after = d_mlp_gain[7, 0]
+    block_own = (resid_own + after + mlp_own.astype(F32)).astype(BF16)
+    block_own, d_resid = lax.optimization_barrier((block_own, d_resid))
+    block_out = lax.all_gather(block_own, "tensor", axis=0, tiled=True)
     d_mixed = nt(d_resid, out_w).astype(BF16)
     dq, dk, dv = attn_bwd(
         lengths, q_pad, to_lanes(d_mixed), mixed_pad, inverse_sums, k_pad, v_pad, heads, group
@@ -531,40 +762,49 @@
     dq, d_qgain = prepare_back(queries, query_gain, tables, dq[:, :q_width])
     dk, d_kgain = prepare_back(keys_val, key_gain, tables, dk[:, :k_width])
     d_q, d_k, d_v = dq.astype(BF16), dk.astype(BF16), dv[:, :k_width].astype(BF16)
+    d_q, d_k, d_v, block_out = lax.optimization_barrier((d_q, d_k, d_v, block_out))
     d_normed = (nt(d_q, query_w) + nt(d_k, key_weight) + nt(d_v, value_weight)).astype(BF16)
-    d_inputs, _, d_norm_gain = line_sum(
+    head_terms = jnp.concatenate([d_qgain, d_kgain])
+    terms = jnp.concatenate(
+        [
+            jnp.zeros((1, width), F32),
+            d_mlp_gain[:1],
+            jnp.pad(head_terms[None], ((0, 0), (0, width - 2 * HEAD_SIZE))),
+            jnp.zeros((5, width), F32),
+        ]
+    )
+    whole_grads = tuple(g.astype(F32) + after for g in (g_gate, g_up, g_down))
+    d_normed, *whole_grads = lax.optimization_barrier((d_normed, *whole_grads))
+    d_inputs, _, d_gains = line_sum(
         d_normed,
-        (d_resid_own, inputs_own, norm_gain[None]),
+        (d_resid_own, inputs_own, norm_gain[None], terms),
         (own_shape, gain_shape),
         finish_back,
         PIECES,
         3,
+        True,
     )
     g_out = tn(mixed, d_resid).astype(BF16)
     g_query = tn(normed, d_q).astype(BF16)
     g_key = tn(normed, d_k).astype(BF16)
     g_value = tn(normed, d_v).astype(BF16)
-    g_out, g_query, g_key, g_value, g_gate, g_up, g_down = lax.optimization_barrier(
-        (g_out, g_query, g_key, g_value, g_gate, g_up, g_down)
+    g_out, g_query, g_key, g_value, *whole_grads = lax.optimization_barrier(
+        (g_out, g_query, g_key, g_value, *whole_grads)
     )
     g_out, g_query, g_key, g_value = lax.psum((g_out, g_query, g_key, g_value), "dp")
-    g_norm, g_mlp, g_qgain, g_kgain = lax.psum(
-        (d_norm_gain[0], d_mlp_gain[0], d_qgain, d_kgain), ("dp", "tensor")
-    )
+    d_gains = lax.psum(d_gains[:3], "dp")
     return (
         block_out,
         d_inputs.astype(F32),
-        g_norm,
+        d_gains[0],
         g_query.astype(F32),
         g_key.astype(F32),
         g_value.astype(F32),
         g_out.astype(F32),
-        g_qgain,
-        g_kgain,
-        g_mlp,
-        g_gate.astype(F32),
-        g_up.astype(F32),
-        g_down.astype(F32),
+        d_gains[2, :HEAD_SIZE],
+        d_gains[2, HEAD_SIZE : 2 * HEAD_SIZE],
+        d_gains[1],
+        *whole_grads,
     )
 
 

time: 1110 us -> 939 us (0.85)
  Pallas kernels: 723 us -> 518 us
  matrix products: 222 us -> 253 us
  blocking collectives: 40.2 us -> 22.6 us
  waiting for transfers between devices: 0.09 us -> 16.3 us
    pallas_call x3 -> x2, Pallas kernels: 652 us -> 344 us  [line_sum(): pl.pallas_call(functools.partial(line_sum_kernel, count, pieces, finish,...]
    pallas_call x1, Pallas kernels: 21.8 us -> 125 us  [attn_gather(): pl.pallas_call(functools.partial(attn_gather_kernel, count, ways, head_pl...]
    dot_general x7, matrix products: 69.2 us -> 94.9 us  [nn(): lax.dot_general(a, b, (((1,), (0,)), ((), ())), preferred_element_type=F32)]
    add x0 -> x2, other arithmetic: none -> 18.3 us  [on_device(): whole_grads = tuple((g.astype(F32) + after for g in (g_gate, g_up, g_down)))]
    psum x1, blocking collectives: 40.2 us -> 22.6 us  [on_device(): d_gains = lax.psum(d_gains[:3], 'dp')]
    all_gather x1, waiting for transfers between devices: 0.01 us -> 16.3 us  [on_device(): block_out = lax.all_gather(block_own, 'tensor', axis=0, tiled=True)]
    convert_element_type x4 -> x3, other arithmetic: 26.2 us -> 13.4 us  [the longest x1 8.38 us: on_device(): normed2 = (resid * inverse_rms(resid) * mlp_gain).astype(BF16)]
  transfers between devices with their start and end apart: 4 -> 4, of which waited for: 0 -> 1; matrix products, arithmetic and copies ran while one was open for 15% -> 20% of each run, Pallas kernels for 48% -> 42%
where the time goes in v3:
time: 939 us; the launch traced here: 935 us
  Pallas kernels  518 us (55%)
  matrix products  253 us (27%)
  other arithmetic  78.7 us (8%)
  local copies, waits for them, and re-layouts  29.4 us (3%)
  blocking collectives  22.6 us (2%)
  between operations  17.1 us (2%)
  waiting for transfers between devices  16.3 us (2%)
    pallas_call x2, Pallas kernels, line_sum(): pl.pallas_call(functools.partial(line_sum_kernel, count, pieces, finish,...  344 us
    pallas_call x1, Pallas kernels, attn_gather(): pl.pallas_call(functools.partial(attn_gather_kernel, count, ways, head_pl...  125 us
    dot_general x7, matrix products, nn(): lax.dot_general(a, b, (((1,), (0,)), ((), ())), preferred_element_type=F32)  94.9 us
    dot_general x7, matrix products, nt(): lax.dot_general(a, b, (((1,), (1,)), ((), ())), preferred_element_type=F32)  92.6 us
    dot_general x7, matrix products, tn(): lax.dot_general(a, b, (((0,), (0,)), ((), ())), preferred_element_type=F32)  65.4 us
    pallas_call x1, Pallas kernels, attn_bwd(): pl.pallas_call(functools.partial(bwd_kernel, places, tiles, bq, bk), out_...  49.7 us
    psum x1, blocking collectives, on_device(): d_gains = lax.psum(d_gains[:3], 'dp')  22.6 us
  transfers between devices with their start and end apart: 4, of which 1 were waited for; matrix products, arithmetic and copies ran while one was open for 20% of the time, Pallas kernels for 42%

profile of v3, /device:TPU:0, one launch (start us, length us, event | category | flops | bytes accessed | tf_op | source)
XLA Modules:
  0.0 935.2 jit_solution(13956150269641412749)
XLA Ops:
  35.8 124.7 %attention_gather.1 = (bf16[2048,1536]{1,0:T(8,128)(2,1)}, f32[2048,384]{1,0:T(8,128)}, bf16[4,2,2,2,48,1536]{5,4,3,2,1,0:T(8,128)(2,1)}) custom-call(s32[1]{0:T(128)} %copy.59.len_ref, bf16[2048,384]{1,0:T(8,128)(2,1)} %copy.46.q_ref, bf16[2048,128]{1,0:T(8,128)(2,1)} %copy.44.k_ref, bf16[2048,128]{1,0:T(8,128)(2,1)} %convolution_convert_fusion.7.v_ref, ...), custom_call_target="tpu_custom_call" | custom-call | flops 6442450944 | bytes 377487360 | tf_op jit(solution)/shard_map/attention_gather/pallas_call | solution.py:593
  160.5 26.2 %multiply_reduce_fusion = (f32[2048]{0:T(1024)S(1)}, f32[2048,1536]{1,0:T(8,128)}) fusion(bf16[2048,1536]{1,0:T(8,128)(2,1)} %get-tuple-element.46, bf16[1536,1536]{1,0:T(8,128)(2,1)} %bitcast.125, bf16[2048,1536]{1,0:T(8,128)(2,1)S(1)} %bitcast.112), kind=kOutput, calls=%fused_computation.13 | convolution fusion | flops 9676257280 | bytes 29892608 | tf_op jit(solution)/shard_map/dot_general | solution.py:25
  186.8 8.4 multiply_convert_fusion.3
  195.2 17.2 %fusion.13 = f32[2048,1728]{0,1:T(8,128)} fusion(bf16[2048,1536]{1,0:T(8,128)(2,1)} %multiply_convert_fusion.3, bf16[1536,1728]{0,1:T(8,128)(2,1)} %param.25), kind=kOutput, calls=%fused_computation.90 | convolution fusion | flops 10871635968 | bytes 25755648 | tf_op jit(solution)/shard_map/dot_general | solution.py:25
  212.3 22.5 %multiply_convert_fusion.2 = (bf16[2048,1728]{0,1:T(8,128)(2,1)}, f32[2048,1728]{0,1:T(8,128)}) fusion(f32[2048,1728]{0,1:T(8,128)} %fusion.13, bf16[2048,1536]{1,0:T(8,128)(2,1)} %multiply_convert_fusion.3, bf16[1536,1728]{0,1:T(8,128)(2,1)} %param.26), kind=kOutput, calls=%fused_computation.6 | convolution fusion | flops 10892869632 | bytes 46989312 | tf_op jit(solution)/shard_map/dot_general | solution.py:25
  234.9 15.6 %convolution_convert_fusion.3 = bf16[2048,1536]{1,0:T(8,128)(2,1)} fusion(bf16[2048,1728]{0,1:T(8,128)(2,1)} %get-tuple-element.115, bf16[1728,1536]{1,0:T(8,128)(2,1)S(1)} %bitcast.120), kind=kOutput, calls=%fused_computation.20 | convolution fusion | flops 10874781696 | bytes 18677760 | tf_op jit(solution)/shard_map/dot_general | solution.py:25
  255.1 17.2 %convolution_convert_fusion.2 = bf16[1728,1536]{1,0:T(8,128)(2,1)} fusion(bf16[2048,1728]{0,1:T(8,128)(2,1)} %get-tuple-element.115, bf16[2048,1536]{1,0:T(8,128)(2,1)S(1)} %broadcast_select_fusion), kind=kOutput, calls=%fused_computation.19 | convolution fusion | flops 10874290176 | bytes 18677760 | tf_op jit(solution)/shard_map/dot_general | solution.py:24
  272.3 23.7 %multiply_convert_fusion = (bf16[2048,1728]{0,1:T(8,128)(2,1)}, bf16[2048,1728]{0,1:T(8,128)(2,1)}) fusion(f32[2048,1728]{0,1:T(8,128)} %fusion.13, f32[2048,1728]{0,1:T(8,128)} %get-tuple-element.48, bf16[2048,1536]{1,0:T(8,128)(2,1)S(1)} %broadcast_select_fusion, bf16[1728,1536]{1,0:T(8,128)(2,1)} %param.27), kind=kOutput, calls=%fused_computation.3 | convolution fusion | flops 10917642240 | bytes 54067200 | tf_op jit(solution)/shard_map/dot_general | solution.py:23
  296.0 16.9 %convolution_convert_fusion = bf16[1536,1728]{0,1:T(8,128)(2,1)} fusion(bf16[2048,1728]{0,1:T(8,128)(2,1)} %get-tuple-element.88, bf16[2048,1536]{1,0:T(8,128)(2,1)} %multiply_convert_fusion.3), kind=kOutput, calls=%fused_computation.17 | convolution fusion | flops 10874290176 | bytes 18677760 | tf_op jit(solution)/shard_map/dot_general | solution.py:24
  312.9 15.0 %convolution_convert_fusion.1 = bf16[1536,1728]{0,1:T(8,128)(2,1)} fusion(bf16[2048,1728]{0,1:T(8,128)(2,1)S(1)} %copy-done.44, bf16[2048,1536]{1,0:T(8,128)(2,1)} %multiply_convert_fusion.3), kind=kOutput, calls=%fused_computation.18 | convolution fusion | flops 10874290176 | bytes 18677760 | tf_op jit(solution)/shard_map/dot_general | solution.py:24
  337.4 17.0 %fusion.14 = f32[2048,1536]{1,0:T(8,128)} fusion(bf16[2048,1728]{0,1:T(8,128)(2,1)} %get-tuple-element.89, bf16[1536,1728]{0,1:T(8,128)(2,1)S(1)} %bitcast.122), kind=kOutput, calls=%fused_computation.91 | convolution fusion | flops 10871635968 | bytes 24969216 | tf_op jit(solution)/shard_map/dot_general | solution.py:23
  354.4 18.6 %add_convert_fusion.1.part_ref = bf16[2048,1536]{1,0:T(8,128)(2,1)} fusion(f32[2048,1536]{1,0:T(8,128)} %fusion.14, bf16[2048,1728]{0,1:T(8,128)(2,1)} %get-tuple-element.88, bf16[1536,1728]{0,1:T(8,128)(2,1)S(1)} %bitcast.124), kind=kOutput, calls=%fused_computation.11 | convolution fusion | flops 10877927424 | bytes 31260672 | tf_op jit(solution)/shard_map/dot_general | solution.py:23
  373.1 170.3 %line_sum.2 = (bf16[2048,1536]{1,0:T(8,128)(2,1)}, f32[512,1536]{1,0:T(8,128)}, f32[8,1536]{1,0:T(8,128)}) custom-call(bf16[2048,1536]{1,0:T(8,128)(2,1)} %add_convert_fusion.1.part_ref, f32[512,1536]{1,0:T(8,128)} %dynamic-slice_convert_fusion.1.refs_0_, f32[512,1536]{1,0:T(8,128)} %constant_dynamic-slice_fusion.1.refs_1_, f32[1,1536]{1,0:T(1,128)} %broadcast_in_dim.22.refs_2_), custom_call_target="tpu_custom_call" | custom-call | flops 25165824 | bytes 629145600 | tf_op jit(solution)/shard_map/line_sum/pallas_call | solution.py:355
  552.9 8.0 convolution_convert_fusion.6.do_ref
  561.0 49.7 %attention_backward.1 = (f32[2048,384]{1,0:T(8,128)}, f32[2048,128]{1,0:T(8,128)S(1)}, f32[2048,128]{1,0:T(8,128)S(1)}) custom-call(s32[1]{0:T(128)} %copy.59.len_ref, bf16[2048,384]{1,0:T(8,128)(2,1)S(1)} %copy-done.1, bf16[2048,384]{1,0:T(8,128)(2,1)} %convolution_convert_fusion.6.do_ref, bf16[2048,384]{1,0:T(8,128)(2,1)} %constant_dynamic-slice_fusion.o_ref, ...), custom_call_target="tpu_custom_call" | custom-call | flops 786432 | bytes 1572864 | tf_op jit(solution)/shard_map/attention_backward/pallas_call | solution.py:108
  628.9 9.4 %convert_add_fusion.1 = f32[1728,1536]{1,0:T(8,128)} fusion(bf16[1728,1536]{1,0:T(8,128)(2,1)} %get-tuple-element.87, f32[]{:T(128)} %bitcast.7), kind=kLoop, calls=%fused_computation.14 | loop fusion | flops 5308416 | bytes 15925252 | tf_op jit(solution)/shard_map/add | solution.py:776
  638.3 9.0 convert_add_fusion.2
  647.3 16.3 %all-gather.2.cloned.1.call-done = bf16[2048,1536]{1,0:T(8,128)(2,1)} async-done(((bf16[512,1536]{1,0:T(8,128)(2,1)}), bf16[2048,1536]{1,0:T(8,128)(2,1)}) %all-gather.2.cloned.1.call-update) | async-done | bytes 6291472 | tf_op jit(solution)/shard_map/all_gather | solution.py:757
  663.5 6.8 fusion.15
  670.3 7.4 convolution_convert_fusion.4
  689.5 12.0 %add_convert_fusion.part_ref = bf16[2048,1536]{1,0:T(8,128)(2,1)} fusion(f32[2048,1536]{1,0:T(8,128)} %fusion.15, f32[2048,1536]{1,0:T(8,128)} %fusion.16, bf16[2048,128]{1,0:T(8,128)(2,1)S(1)} %copy-done.19, bf16[1536,128]{1,0:T(8,128)(2,1)S(1)} %copy-done.25), kind=kOutput, calls=%fused_computation.10 | convolution fusion | flops 814743552 | bytes 32374784 | tf_op jit(solution)/shard_map/dot_general | solution.py:23
  707.5 173.3 %line_sum.3 = (bf16[2048,1536]{1,0:T(8,128)(2,1)}, f32[512,1536]{1,0:T(8,128)}, f32[8,1536]{1,0:T(8,128)}) custom-call(bf16[2048,1536]{1,0:T(8,128)(2,1)} %add_convert_fusion.part_ref, f32[512,1536]{1,0:T(8,128)} %get-tuple-element.66.refs_0_, f32[512,1536]{1,0:T(8,128)} %dynamic-slice_convert_fusion.refs_1_, f32[1,1536]{1,0:T(1,128)} %broadcast_in_dim.23.refs_2_, ...), custom_call_target="tpu_custom_call" | custom-call | flops 25165824 | bytes 629145600 | tf_op jit(solution)/shard_map/line_sum/pallas_call | solution.py:355
  880.7 9.4 %convert_element_type.209 = f32[2048,1536]{1,0:T(8,128)} convert(bf16[2048,1536]{1,0:T(8,128)(2,1)} %get-tuple-element.67) | non-fusion elementwise | flops 3145728 | bytes 18874368 | tf_op jit(solution)/shard_map/convert_element_type | solution.py:798
  890.1 22.6 %psum.59 = f32[3,1536]{1,0:T(4,128)S(1)} all-reduce(f32[3,1536]{1,0:T(4,128)S(1)} %slice.55), channel_id=1, replica_groups=mesh['dp'=8,'tensor'=4] {'dp'}, use_global_device_ids=true, to_apply=%region_14.15 | all-reduce | flops 4608 | bytes 36864 | tf_op jit(solution)/shard_map/psum | solution.py:795
  (199 shorter events, 101.1 us)
Async XLA Ops:
  8.0 365.0 %reduce-scatter.2.cloned.1.call-start = ((), (), s32[]{:S(2)}) async-start(), calls=%async_computation.1 | async-start | bytes 7864320 | tf_op jit(solution)/shard_map/reduce_scatter | solution.py:734
  19.8 8.5 copy-start.12
  29.6 130.9 %slice-start.2 = ((s8[6291456]{0:T(1024)(128)(4,1)}), s8[4194304]{0:T(1024)(128)(4,1)S(1)}, s32[]{:S(2)}) async-start(s8[6291456]{0:T(1024)(128)(4,1)} %bitcast.111), calls=%async_computation.7 | async-start | bytes 8388608
  35.8 124.7 %slice-start.3 = ((s8[6291456]{0:T(1024)(128)(4,1)}), s8[2097152]{0:T(1024)(128)(4,1)S(1)}, s32[]{:S(2)}) async-start(s8[6291456]{0:T(1024)(128)(4,1)} %bitcast.111), calls=%async_computation.8 | async-start | bytes 4194304
  160.5 26.3 %copy-start.30 = (f32[1536]{0:T(1024)S(1)}, f32[1536]{0:T(1024)}, u32[]{:S(2)}) copy-start(f32[1536]{0:T(1024)} %param.24) | copy-start | bytes 18436
  195.2 39.7 %slice-start.6 = ((s8[5308416]{0:T(1024)(128)(4,1)}), s8[4194304]{0:T(1024)(128)(4,1)S(1)}, s32[]{:S(2)}) async-start(s8[5308416]{0:T(1024)(128)(4,1)} %bitcast.119), calls=%async_computation.11 | async-start | bytes 8388608
  212.3 22.6 %slice-start.7 = ((s8[5308416]{0:T(1024)(128)(4,1)}), s8[1114112]{0:T(1024)(128)(4,1)S(1)}, s32[]{:S(2)}) async-start(s8[5308416]{0:T(1024)(128)(4,1)} %bitcast.119), calls=%async_computation.12 | async-start | bytes 2228224
  250.5 378.4 %all-reduce.8.cloned.1.call-start = ((), (), s32[]{:S(2)}) async-start(), calls=%async_computation.4 | async-start | bytes 31850496 | tf_op jit(solution)/shard_map/psum | solution.py:752
  255.1 17.2 %copy-start.11 = (bf16[2048,1536]{1,0:T(8,128)(2,1)}, bf16[2048,1536]{1,0:T(8,128)(2,1)S(1)}, u32[]{:S(2)}) copy-start(bf16[2048,1536]{1,0:T(8,128)(2,1)S(1)} %broadcast_select_fusion) | copy-start | bytes 18874372
  296.0 16.9 %copy-start.44 = (bf16[2048,1728]{0,1:T(8,128)(2,1)S(1)}, bf16[2048,1728]{0,1:T(8,128)(2,1)}, u32[]{:S(2)}) copy-start(bf16[2048,1728]{0,1:T(8,128)(2,1)} %get-tuple-element.89) | copy-start | bytes 21233668
  327.9 9.5 %slice-start.8 = ((s8[5308416]{0:T(1024)(128)(4,1)}), s8[1114112]{0:T(1024)(128)(4,1)S(1)}, s32[]{:S(2)}) async-start(s8[5308416]{0:T(1024)(128)(4,1)} %bitcast.121), calls=%async_computation.13 | async-start | bytes 2228224
  327.9 335.6 %all-gather.2.cloned.1.call-start = ((), (), s32[]{:S(2)}) async-start(), calls=%async_computation.2 | async-start | bytes 7864320 | tf_op jit(solution)/shard_map/all_gather | solution.py:757
  329.2 8.3 slice-start.9
  329.2 25.3 %slice-start.10 = ((s8[5308416]{0:T(1024)(128)(4,1)}), s8[4194304]{0:T(1024)(128)(4,1)S(1)}, s32[]{:S(2)}) async-start(s8[5308416]{0:T(1024)(128)(4,1)} %bitcast.123), calls=%async_computation.15 | async-start | bytes 8388608
  337.4 17.0 %slice-start.11 = ((s8[5308416]{0:T(1024)(128)(4,1)}), s8[1114112]{0:T(1024)(128)(4,1)S(1)}, s32[]{:S(2)}) async-start(s8[5308416]{0:T(1024)(128)(4,1)} %bitcast.123), calls=%async_computation.16 | async-start | bytes 2228224
  373.1 171.6 %copy-start.21 = (bf16[512,1536]{1,0:T(8,128)(2,1)S(1)}, bf16[512,1536]{1,0:T(8,128)(2,1)}, u32[]{:S(2)}) copy-start(bf16[512,1536]{1,0:T(8,128)(2,1)} %reduce-scatter.2.cloned.1.call-done) | copy-start | bytes 4718596
  543.4 9.5 %copy-start.43 = (bf16[384,1536]{1,0:T(8,128)(2,1)S(1)}, bf16[384,1536]{1,0:T(8,128)(2,1)}, u32[]{:S(2)}) copy-start(bf16[384,1536]{1,0:T(8,128)(2,1)} %w_ref.1) | copy-start | bytes 3538948
  548.9 365.0 %all-reduce.6.cloned.1.call-start = ((), (), s32[]{:S(2)}) async-start(), calls=%async_computation.3 | async-start | bytes 6291456 | tf_op jit(solution)/shard_map/psum | solution.py:794
  552.9 8.1 copy-start.3
  628.9 9.4 %copy-start.15 = (bf16[1536,1728]{0,1:T(8,128)(2,1)S(1)}, bf16[1536,1728]{0,1:T(8,128)(2,1)}, u32[]{:S(2)}) copy-start(bf16[1536,1728]{0,1:T(8,128)(2,1)} %get-tuple-element.85) | copy-start | bytes 15925252
  628.9 9.4 %copy-start.16 = (bf16[1536,1728]{0,1:T(8,128)(2,1)S(1)}, bf16[1536,1728]{0,1:T(8,128)(2,1)}, u32[]{:S(2)}) copy-start(bf16[1536,1728]{0,1:T(8,128)(2,1)} %get-tuple-element.86) | copy-start | bytes 15925252
  670.3 13.9 %slice-start = ((s8[6291456]{0:T(1024)(128)(4,1)}), s8[2097152]{0:T(1024)(128)(4,1)S(1)}, s32[]{:S(2)}) async-start(s8[6291456]{0:T(1024)(128)(4,1)} %bitcast.109), calls=%async_computation.5 | async-start | bytes 4194304
  689.5 12.0 %copy-start.33 = (f32[1536]{0:T(1024)S(1)}, f32[1536]{0:T(1024)}, u32[]{:S(2)}) copy-start(f32[1536]{0:T(1024)} %param.17) | copy-start | bytes 18436
  880.7 9.4 %copy-start.34 = (f32[8,1536]{1,0:T(8,128)S(1)}, f32[8,1536]{1,0:T(8,128)}, u32[]{:S(2)}) copy-start(f32[8,1536]{1,0:T(8,128)} %get-tuple-element.68) | copy-start | bytes 147460
  (37 other events, 176.5 us)
Sparse Core Ops, SparseCore 0:
  250.6 109.8 reduce-scatter.1
  549.0 114.4 all-gather.1
Sparse Core Ops, SparseCore 1:
  328.0 207.1 all-reduce.7
  701.6 67.9 all-reduce.5

commit v4 on v3

--- a/solution.py
+++ b/solution.py
@@ -14,7 +14,6 @@
 LOG2E = math.log2(math.e)
 EPSILON = 1e-05
 ROPE_BASE = 1000000.0
-PIECES = 8
 F32 = jnp.float32
 BF16 = jnp.bfloat16
 MESH = pl.DeviceIdType.MESH
@@ -132,21 +131,28 @@
     )
 
 
-def greet_line(count, everyone=False):
+def greet_line(count, ways=0):
     me = lax.axis_index("tensor")
     barrier = pltpu.get_barrier_semaphore()
 
     def greet(peer):
         pl.semaphore_signal(barrier, inc=1, device_id={"tensor": peer}, device_id_type=MESH)
 
-    if everyone:
+    if ways:
+        spot = lax.axis_index("dp")
         for peer in range(count):
 
             @pl.when(peer != me)
             def _():
                 greet(peer)
 
-        pl.semaphore_wait(barrier, count - 1)
+        for peer in range(ways):
+
+            @pl.when(peer != spot)
+            def _():
+                pl.semaphore_signal(barrier, inc=1, device_id={"dp": peer}, device_id_type=MESH)
+
+        pl.semaphore_wait(barrier, count - 1 + ways - 1)
         return
 
     @pl.when(me > 0)
@@ -170,8 +176,10 @@
     count, pieces, finish, kinds, share_terms, part_ref, *refs
 ):
     (own_refs, full_ref, out_refs), scratch = split_refs(refs, kinds)
-    up_buf, down_buf, acc, shared = scratch[:4]
-    sems = scratch[4:]
+    up_buf, down_buf, acc, shared, shared_ways = scratch[:5]
+    sems = scratch[5:]
+    ways = shared_ways.shape[0]
+    spot = lax.axis_index("dp")
     sum_up, sum_down, give_up, give_down = (sems[0:2], sems[2:4], sems[4:6], sems[6:8])
     me = lax.axis_index("tensor")
     last = count - 1
@@ -251,17 +259,42 @@
         mine = pl.ds(c * size, size)
         full_ref[rows(me, c), :] = finish(c, mine, acc[...], own_refs, out_refs)
 
-    def share(to):
+    def share(axis, to, sender, at):
+        here, place, sem = (me, shared, 8) if axis == "tensor" else (spot, shared_ways, 10)
         return pltpu.make_async_remote_copy(
             src_ref=out_refs[1],
-            dst_ref=shared.at[me],
-            send_sem=sems[8].at[to],
-            recv_sem=sems[9].at[me],
-            device_id={"tensor": to},
+            dst_ref=place.at[sender],
+            send_sem=sems[sem].at[to],
+            recv_sem=sems[sem + 1].at[sender],
+            device_id={axis: to},
             device_id_type=MESH,
         )
 
-    greet_line(count, share_terms)
+    def share_start(axis, size_of, here):
+        for to in range(size_of):
+
+            @pl.when(to != here)
+            def _():
+                share(axis, to, here, here).start()
+
+    def share_finish(axis, size_of, here, place):
+        for peer in range(size_of):
+
+            @pl.when(peer != here)
+            def _():
+                share(axis, peer, here, here).wait_send()
+                share(axis, peer, peer, here).wait_recv()
+
+            @pl.when(peer == here)
+            def _():
+                place[peer] = out_refs[1][...]
+
+        terms = place[0]
+        for peer in range(1, size_of):
+            terms = terms + place[peer]
+        out_refs[1][...] = terms
+
+    greet_line(count, ways if share_terms else 0)
     for slot in range(pieces + 2 * last):
         if slot < pieces:
             for upward in (True, False):
@@ -277,11 +310,10 @@
             for upward in (True, False):
                 give_start(c, 1, upward)
             if share_terms and c == pieces - 1:
-                for to in range(count):
-
-                    @pl.when(to != me)
-                    def _():
-                        share(to).start()
+                share_start("tensor", count, me)
+        if share_terms and c == pieces + last - 2:
+            share_finish("tensor", count, me, shared)
+            share_start("dp", ways, spot)
         for s in range(last, 1, -1):
             c = slot - (s - 1)
             if 0 <= c < pieces:
@@ -314,28 +346,7 @@
                     give_copy(c, s, upward).wait_send()
 
     if share_terms:
-        for peer in range(count):
-
-            @pl.when(peer != me)
-            def _():
-                share(peer).wait_send()
-                pltpu.make_async_remote_copy(
-                    src_ref=out_refs[1],
-                    dst_ref=shared.at[peer],
-                    send_sem=sems[8].at[peer],
-                    recv_sem=sems[9].at[peer],
-                    device_id={"tensor": peer},
-                    device_id_type=MESH,
-                ).wait_recv()
-
-            @pl.when(peer == me)
-            def _():
-                shared[peer] = out_refs[1][...]
-
-        terms = shared[0]
-        for peer in range(1, count):
-            terms = terms + shared[peer]
-        out_refs[1][...] = terms
+        share_finish("dp", ways, spot, shared_ways)
 
 
 def split_refs(refs, kinds):
@@ -348,6 +359,7 @@
 
 def line_sum(part, owned, outs, finish, pieces, collective_id, share_terms=False):
     count = lax.axis_size("tensor")
+    ways = lax.axis_size("dp")
     rows, width = part.shape
     size = rows // count // pieces
     vmem = pl.BlockSpec(memory_space=pltpu.VMEM)
@@ -362,9 +374,11 @@
             pltpu.VMEM((*hops, size, width), BF16),
             pltpu.VMEM((size, width), F32),
             pltpu.VMEM((count, 8, width), F32),
+            pltpu.VMEM((ways, 8, width), F32),
         ]
         + [pltpu.SemaphoreType.DMA(hops)] * 8
-        + [pltpu.SemaphoreType.DMA((count,))] * 2,
+        + [pltpu.SemaphoreType.DMA((count,))] * 2
+        + [pltpu.SemaphoreType.DMA((ways,))] * 2,
         compiler_params=pltpu.CompilerParams(
             collective_id=collective_id, has_side_effects=True, vmem_limit_bytes=56 << 20
         ),
@@ -404,8 +418,13 @@
     k_ref,
     v_ref,
     w_ref,
+    tokens_ref,
+    gain_ref,
+    normed_ref,
+    resid_ref,
+    mixed_ref,
+    linv_ref,
     full_ref,
-    linv_ref,
     whole_ref,
     q6,
     vx,
@@ -413,10 +432,11 @@
     *sems,
 ):
     give_up, give_down, line_sems, way_sems = sems[0:2], sems[2:4], sems[4:6], sems[6:8]
+    load_tokens = pltpu.make_async_copy(tokens_ref, normed_ref, sems[8])
     me = lax.axis_index("tensor")
     spot = lax.axis_index("dp")
     piece = w_ref.shape[0] // ways
-    weight_slots = [1, 3, 4, 5]
+    weight_slots = {1: (1,), 3: (2,), 4: tuple(range(3, ways.bit_length() + 1))}
     levels = ways.bit_length() - 1
     last = count - 1
     rows, width = q_ref.shape
@@ -475,6 +495,7 @@
         inv = 1.0 / acc[:, LANES:]
         out = unstack_heads(acc[:, :LANES] * inv, places, tiles, bq)
         place(me, c)[...] = out.astype(BF16)
+        mixed_ref[span, :] = out.astype(BF16)
         linv_ref[span, :] = unstack_heads(inv, places, tiles, bq)
 
 
@@ -528,6 +549,29 @@
         if step - 1 < levels:
             held_parts(step - 1).start()
 
+    def project(c):
+        @pl.when(me == last)
+        def _():
+            wait(c, last, True)
+
+        @pl.when(me == 0)
+        def _():
+            wait(c, last, False)
+
+        span = pl.ds(c * bq, bq)
+        resid = normed_ref[span, :].astype(F32)
+        for block in range(count):
+            weight = whole_ref[block].reshape(width, resid.shape[1])
+            resid += nn(full_ref[span, pl.ds(block * width, width)], weight)
+        normed_ref[span, :] = (resid * inverse_rms(resid) * gain_ref[...]).astype(BF16)
+        own = resid_ref.shape[0]
+        for j in range(bq // own):
+
+            @pl.when(me == c * (bq // own) + j)
+            def _():
+                resid_ref[...] = resid[j * own : (j + 1) * own]
+
+    load_tokens.start()
     barrier = pltpu.get_barrier_semaphore()
     for peer in range(count):
 
@@ -544,7 +588,7 @@
     live = lax.broadcasted_iota(jnp.int32, (rows, LANES), 0) < len_ref[0]
     vx[:, :LANES] = jnp.where(live, v_ref[...].astype(F32), 0.0).astype(BF16)
     vx[:, LANES:] = jnp.where(live, 1.0, 0.0).astype(BF16)
-    for slot in range(chunks + last):
+    for slot in range(chunks + last - 1):
         if slot < chunks:
             attend(slot)
             for upward in (True, False):
@@ -554,10 +598,14 @@
             if 0 <= c < chunks:
                 for upward in (True, False):
                     start(c, s, upward)
-        if slot in weight_slots:
-            weight_step(1 + weight_slots.index(slot))
-    for step in range(1 + len(weight_slots), levels + 2):
-        weight_step(step)
+        for step in weight_slots.get(slot, ()):
+            weight_step(step)
+        if slot == 4:
+            load_tokens.wait()
+        if slot >= max(4, last) and slot - max(4, last) < chunks:
+            project(slot - max(4, last))
+    for c in range(max(0, chunks + last - 1 - max(4, last)), chunks):
+        project(c)
     for peer in range(count):
 
         @pl.when(peer != me)
@@ -567,15 +615,6 @@
     for level in range(levels):
         held_parts(level).wait_send()
     for c in range(chunks):
-
-        @pl.when(me == last)
-        def _():
-            wait(c, last, True)
-
-        @pl.when(me == 0)
-        def _():
-            wait(c, last, False)
-
         for s in range(1, count):
             for upward in (True, False):
 
@@ -584,33 +623,41 @@
                     copy(c, s, upward).wait_send()
 
 
-def attn_gather(length, q, k, v, w, heads, group, bq, collective_id):
+def attn_gather(length, q, k, v, w, tokens, gain, heads, group, bq, collective_id):
     count = lax.axis_size("tensor")
     ways = lax.axis_size("dp")
     rows, width = q.shape
+    model = tokens.shape[1]
     vmem = pl.BlockSpec(memory_space=pltpu.VMEM)
     hops = (rows // bq, count - 1)
+    levels = ways.bit_length() - 1
     return pl.pallas_call(
         functools.partial(
             attn_gather_kernel, count, ways, head_places(heads, group), width // LANES, bq
         ),
         out_shape=(
-            jax.ShapeDtypeStruct((rows, count * width), BF16),
+            jax.ShapeDtypeStruct((rows, model), BF16),
+            jax.ShapeDtypeStruct((rows // count, model), F32),
+            jax.ShapeDtypeStruct((rows, width), BF16),
             jax.ShapeDtypeStruct((rows, width), F32),
-            jax.ShapeDtypeStruct((count, *(2,) * (ways.bit_length() - 1), w.shape[0] // ways, w.shape[1]), BF16),
         ),
-        in_specs=[pl.BlockSpec(memory_space=pltpu.SMEM), vmem, vmem, vmem, vmem],
-        out_specs=(vmem, vmem, vmem),
+        in_specs=[pl.BlockSpec(memory_space=pltpu.SMEM)]
+        + [vmem] * 4
+        + [pl.BlockSpec(memory_space=pl.ANY), vmem],
+        out_specs=(vmem,) * 4,
         scratch_shapes=[
+            pltpu.VMEM((rows, count * width), BF16),
+            pltpu.VMEM((count, *(2,) * levels, w.shape[0] // ways, model), BF16),
             pltpu.VMEM((heads * bq, LANES), BF16),
             pltpu.VMEM((rows, 2 * LANES), BF16),
             pltpu.VMEM((heads * bq, 2 * LANES), F32),
         ]
         + [pltpu.SemaphoreType.DMA(hops)] * 4
         + [pltpu.SemaphoreType.DMA((count,))] * 2
-        + [pltpu.SemaphoreType.DMA((ways,))] * 2,
+        + [pltpu.SemaphoreType.DMA((ways,))] * 2
+        + [pltpu.SemaphoreType.DMA(())],
         compiler_params=pltpu.CompilerParams(
-            collective_id=collective_id, has_side_effects=True, vmem_limit_bytes=56 << 20
+            collective_id=collective_id, has_side_effects=True, vmem_limit_bytes=58 << 20
         ),
         cost_estimate=pl.CostEstimate(
             flops=heads * rows * rows * 2 * LANES,
@@ -618,7 +665,7 @@
             bytes_accessed=rows * count * width * 120,
         ),
         name="attention_gather",
-    )(length, q, k, v, w)
+    )(length, q, k, v, w, tokens, gain)
 
 
 def inverse_rms(x):
@@ -699,6 +746,7 @@
     k_width = key_weight.shape[1]
     heads = q_width // HEAD_SIZE
     group = q_width // k_width
+    pieces = 64 // count
     own_shape = jax.ShapeDtypeStruct((m, width), F32)
     gain_shape = jax.ShapeDtypeStruct((8, width), F32)
 
@@ -716,14 +764,19 @@
     q_pad = to_lanes(prepare(queries, query_gain, tables).astype(BF16))
     k_pad = to_lanes(prepare(keys_val, key_gain, tables).astype(BF16))
     v_pad = to_lanes(nn(normed, value_weight).astype(BF16))
-    mixed_all, inverse_sums, out_whole = attn_gather(
-        lengths, q_pad, k_pad, v_pad, pad_rows(out_w), heads, group, min(512, row_count), 1
+    normed2, resid_own, mixed_pad, inverse_sums = attn_gather(
+        lengths,
+        q_pad,
+        k_pad,
+        v_pad,
+        pad_rows(out_w),
+        tokens,
+        mlp_gain[None],
+        heads,
+        group,
+        min(512, row_count),
+        1,
     )
-    resid = inputs + nn(mixed_all, out_whole.reshape(-1, width))
-    normed2 = (resid * inverse_rms(resid) * mlp_gain).astype(BF16)
-    resid_own = own(resid)
-    padded = q_pad.shape[1]
-    mixed_pad = lax.dynamic_slice_in_dim(mixed_all, me * padded, padded, axis=1)
     mixed = mixed_pad[:, :q_width]
     gate = nn(normed2, gate_w)
     up = nn(normed2, up_w)
@@ -743,7 +796,7 @@
         (own(d_out).astype(F32), resid_own, mlp_gain[None]),
         (own_shape, gain_shape),
         finish_back,
-        PIECES,
+        pieces,
         2,
     )
     g_gate = tn(normed2, d_gate).astype(BF16)
@@ -780,7 +833,7 @@
         (d_resid_own, inputs_own, norm_gain[None], terms),
         (own_shape, gain_shape),
         finish_back,
-        PIECES,
+        pieces,
         3,
         True,
     )
@@ -792,7 +845,6 @@
         (g_out, g_query, g_key, g_value, *whole_grads)
     )
     g_out, g_query, g_key, g_value = lax.psum((g_out, g_query, g_key, g_value), "dp")
-    d_gains = lax.psum(d_gains[:3], "dp")
     return (
         block_out,
         d_inputs.astype(F32),

time: 939 us -> 881 us (0.938)
  matrix products: 253 us -> 225 us
  blocking collectives: 22.6 us -> 0 us
    dot_general x7 -> x6, matrix products: 94.9 us -> 68.6 us  [nn(): lax.dot_general(a, b, (((1,), (0,)), ((), ())), preferred_element_type=F32)]
    psum x1 -> x0, blocking collectives: 22.6 us -> none  [on_device(): d_gains = lax.psum(d_gains[:3], 'dp')]
    pallas_call x1, Pallas kernels: 125 us -> 138 us  [attn_gather(): pl.pallas_call(functools.partial(attn_gather_kernel, count, ways, head_pl...]
    convert_element_type x2 -> x0, other arithmetic: 12.7 us -> none  [the longest x1 8.38 us: on_device(): normed2 = (resid * inverse_rms(resid) * mlp_gain).astype(BF16)]
    pallas_call x2, Pallas kernels: 344 us -> 332 us  [line_sum(): pl.pallas_call(functools.partial(line_sum_kernel, count, pieces, finish,...]
    add x2 -> x3, other arithmetic: 18.3 us -> 22 us  [on_device(): whole_grads = tuple((g.astype(F32) + after for g in (g_gate, g_up, g_down)))]
  transfers between devices with their start and end apart: 4 -> 4, of which waited for: 1 -> 1; matrix products, arithmetic and copies ran while one was open for 20% -> 21% of each run, Pallas kernels for 42% -> 44%
where the time goes in v4:
time: 881 us; the launch traced here: 872 us
  Pallas kernels  519 us (59%)
  matrix products  225 us (26%)
  other arithmetic  70.4 us (8%)
  local copies, waits for them, and re-layouts  23.7 us (3%)
  between operations  17.2 us (2%)
  waiting for transfers between devices  16.3 us (2%)
    pallas_call x2, Pallas kernels, line_sum(): pl.pallas_call(functools.partial(line_sum_kernel, count, pieces, finish,...  332 us
    pallas_call x1, Pallas kernels, attn_gather(): pl.pallas_call(functools.partial(attn_gather_kernel, count, ways, head_pl...  138 us
    dot_general x7, matrix products, nt(): lax.dot_general(a, b, (((1,), (1,)), ((), ())), preferred_element_type=F32)  90.7 us
    dot_general x6, matrix products, nn(): lax.dot_general(a, b, (((1,), (0,)), ((), ())), preferred_element_type=F32)  68.6 us
    dot_general x7, matrix products, tn(): lax.dot_general(a, b, (((0,), (0,)), ((), ())), preferred_element_type=F32)  65.6 us
    pallas_call x1, Pallas kernels, attn_bwd(): pl.pallas_call(functools.partial(bwd_kernel, places, tiles, bq, bk), out_...  49.6 us
    add x3, other arithmetic, on_device(): whole_grads = tuple((g.astype(F32) + after for g in (g_gate, g_up, g_down)))  22 us
  transfers between devices with their start and end apart: 4, of which 1 were waited for; matrix products, arithmetic and copies ran while one was open for 21% of the time, Pallas kernels for 44%

profile of v4, /device:TPU:0, one launch (start us, length us, event | category | flops | bytes accessed | tf_op | source)
XLA Modules:
  0.0 871.9 jit_solution(13697558732006962025)
XLA Ops:
  36.2 137.9 %attention_gather.1 = (bf16[2048,1536]{1,0:T(8,128)(2,1)}, f32[512,1536]{1,0:T(8,128)}, bf16[2048,384]{1,0:T(8,128)(2,1)}, f32[2048,384]{1,0:T(8,128)}) custom-call(s32[1]{0:T(128)} %copy.55.len_ref, bf16[2048,384]{1,0:T(8,128)(2,1)} %copy.43.q_ref, bf16[2048,128]{1,0:T(8,128)(2,1)} %copy.42.k_ref, bf16[2048,128]{1,0:T(8,128)(2,1)} %convolution_convert_fusion.7.v_ref, ...), custom_call_target="tpu_custom_call" | custom-call | flops 6442450944 | bytes 377487360 | tf_op jit(solution)/shard_map/attention_gather/pallas_call | solution.py:634
  174.1 17.3 %fusion.13 = f32[2048,1728]{0,1:T(8,128)} fusion(bf16[2048,1536]{1,0:T(8,128)(2,1)} %get-tuple-element.48, bf16[1536,1728]{0,1:T(8,128)(2,1)} %param.25), kind=kOutput, calls=%fused_computation.84 | convolution fusion | flops 10871635968 | bytes 25755648 | tf_op jit(solution)/shard_map/dot_general | solution.py:24
  191.4 22.6 %multiply_convert_fusion.2 = (bf16[2048,1728]{0,1:T(8,128)(2,1)}, f32[2048,1728]{0,1:T(8,128)}) fusion(f32[2048,1728]{0,1:T(8,128)} %fusion.13, bf16[2048,1536]{1,0:T(8,128)(2,1)} %get-tuple-element.48, bf16[1536,1728]{0,1:T(8,128)(2,1)} %param.26), kind=kOutput, calls=%fused_computation.5 | convolution fusion | flops 10892869632 | bytes 46989312 | tf_op jit(solution)/shard_map/dot_general | solution.py:24
  214.0 15.6 %convolution_convert_fusion.3 = bf16[2048,1536]{1,0:T(8,128)(2,1)} fusion(bf16[2048,1728]{0,1:T(8,128)(2,1)} %get-tuple-element.115, bf16[1728,1536]{1,0:T(8,128)(2,1)S(1)} %bitcast.117), kind=kOutput, calls=%fused_computation.17 | convolution fusion | flops 10874781696 | bytes 18677760 | tf_op jit(solution)/shard_map/dot_general | solution.py:24
  234.0 17.2 %convolution_convert_fusion.2 = bf16[1728,1536]{1,0:T(8,128)(2,1)} fusion(bf16[2048,1728]{0,1:T(8,128)(2,1)} %get-tuple-element.115, bf16[2048,1536]{1,0:T(8,128)(2,1)S(1)} %broadcast_select_fusion), kind=kOutput, calls=%fused_computation.16 | convolution fusion | flops 10874290176 | bytes 18677760 | tf_op jit(solution)/shard_map/dot_general | solution.py:23
  251.2 23.6 %multiply_convert_fusion = (bf16[2048,1728]{0,1:T(8,128)(2,1)}, bf16[2048,1728]{0,1:T(8,128)(2,1)}) fusion(f32[2048,1728]{0,1:T(8,128)} %fusion.13, f32[2048,1728]{0,1:T(8,128)} %get-tuple-element.49, bf16[2048,1536]{1,0:T(8,128)(2,1)S(1)} %broadcast_select_fusion, bf16[1728,1536]{1,0:T(8,128)(2,1)} %param.27), kind=kOutput, calls=%fused_computation.2 | convolution fusion | flops 10917642240 | bytes 54067200 | tf_op jit(solution)/shard_map/dot_general | solution.py:22
  274.8 16.8 %convolution_convert_fusion = bf16[1536,1728]{0,1:T(8,128)(2,1)} fusion(bf16[2048,1728]{0,1:T(8,128)(2,1)} %get-tuple-element.90, bf16[2048,1536]{1,0:T(8,128)(2,1)} %get-tuple-element.48), kind=kOutput, calls=%fused_computation.14 | convolution fusion | flops 10874290176 | bytes 18677760 | tf_op jit(solution)/shard_map/dot_general | solution.py:23
  291.5 15.2 %convolution_convert_fusion.1 = bf16[1536,1728]{0,1:T(8,128)(2,1)} fusion(bf16[2048,1728]{0,1:T(8,128)(2,1)S(1)} %copy-done.42, bf16[2048,1536]{1,0:T(8,128)(2,1)} %get-tuple-element.48), kind=kOutput, calls=%fused_computation.15 | convolution fusion | flops 10874290176 | bytes 18677760 | tf_op jit(solution)/shard_map/dot_general | solution.py:23
  306.8 6.5 dynamic-slice_convert_fusion
  313.3 18.0 %fusion.14 = f32[2048,1536]{1,0:T(8,128)} fusion(bf16[2048,1728]{0,1:T(8,128)(2,1)} %get-tuple-element.91, bf16[1536,1728]{0,1:T(8,128)(2,1)} %param.25), kind=kOutput, calls=%fused_computation.85 | convolution fusion | flops 10871635968 | bytes 24969216 | tf_op jit(solution)/shard_map/dot_general | solution.py:22
  331.4 16.4 %add_convert_fusion.1.part_ref = bf16[2048,1536]{1,0:T(8,128)(2,1)} fusion(f32[2048,1536]{1,0:T(8,128)} %fusion.14, bf16[2048,1728]{0,1:T(8,128)(2,1)S(1)} %bitcast.121, bf16[1536,1728]{0,1:T(8,128)(2,1)S(1)} %bitcast.119), kind=kOutput, calls=%fused_computation.10 | convolution fusion | flops 10877927424 | bytes 31260672 | tf_op jit(solution)/shard_map/dot_general | solution.py:22
  347.8 161.4 %line_sum.2 = (bf16[2048,1536]{1,0:T(8,128)(2,1)}, f32[512,1536]{1,0:T(8,128)}, f32[8,1536]{1,0:T(8,128)}) custom-call(bf16[2048,1536]{1,0:T(8,128)(2,1)} %add_convert_fusion.1.part_ref, f32[512,1536]{1,0:T(8,128)} %get-tuple-element.118.refs_0_, f32[512,1536]{1,0:T(8,128)} %get-tuple-element.47.refs_1_, f32[1,1536]{1,0:T(1,128)} %broadcast_in_dim.20.gain_ref.refs_2_), custom_call_target="tpu_custom_call" | custom-call | flops 25165824 | bytes 629145600 | tf_op jit(solution)/shard_map/line_sum/pallas_call | solution.py:367
  514.2 7.5 convolution_convert_fusion.6.do_ref
  521.7 49.6 %attention_backward.1 = (f32[2048,384]{1,0:T(8,128)}, f32[2048,128]{1,0:T(8,128)S(1)}, f32[2048,128]{1,0:T(8,128)S(1)}) custom-call(s32[1]{0:T(128)} %copy.55.len_ref, bf16[2048,384]{1,0:T(8,128)(2,1)S(1)} %copy-done.1, bf16[2048,384]{1,0:T(8,128)(2,1)} %convolution_convert_fusion.6.do_ref, bf16[2048,384]{1,0:T(8,128)(2,1)} %get-tuple-element.57.o_ref, ...), custom_call_target="tpu_custom_call" | custom-call | flops 786432 | bytes 1572864 | tf_op jit(solution)/shard_map/attention_backward/pallas_call | solution.py:107
  589.3 9.3 %convert_add_fusion = f32[1728,1536]{1,0:T(8,128)} fusion(bf16[1728,1536]{1,0:T(8,128)(2,1)} %get-tuple-element.89, f32[]{:T(128)} %bitcast.6), kind=kLoop, calls=%fused_computation.11 | loop fusion | flops 5308416 | bytes 15925252 | tf_op jit(solution)/shard_map/add | solution.py:829
  598.6 6.4 convert_add_fusion.1
  605.0 6.3 convert_add_fusion.2
  611.3 16.2 %all-gather.2.cloned.1.call-done = bf16[2048,1536]{1,0:T(8,128)(2,1)} async-done(((bf16[512,1536]{1,0:T(8,128)(2,1)}), bf16[2048,1536]{1,0:T(8,128)(2,1)}) %all-gather.2.cloned.1.call-update) | async-done | bytes 6291472 | tf_op jit(solution)/shard_map/all_gather | solution.py:810
  627.5 6.8 fusion.15
  634.3 7.4 convolution_convert_fusion.4
  641.8 6.4 fusion.16
  653.4 12.0 %add_convert_fusion.part_ref = bf16[2048,1536]{1,0:T(8,128)(2,1)} fusion(f32[2048,1536]{1,0:T(8,128)} %fusion.15, f32[2048,1536]{1,0:T(8,128)} %fusion.16, bf16[2048,128]{1,0:T(8,128)(2,1)S(1)} %copy-done.18, bf16[1536,128]{1,0:T(8,128)(2,1)S(1)} %copy-done.25), kind=kOutput, calls=%fused_computation.9 | convolution fusion | flops 814743552 | bytes 32374784 | tf_op jit(solution)/shard_map/dot_general | solution.py:22
  667.9 170.3 %line_sum.3 = (bf16[2048,1536]{1,0:T(8,128)(2,1)}, f32[512,1536]{1,0:T(8,128)}, f32[8,1536]{1,0:T(8,128)}) custom-call(bf16[2048,1536]{1,0:T(8,128)(2,1)} %add_convert_fusion.part_ref, f32[512,1536]{1,0:T(8,128)} %get-tuple-element.68.refs_0_, f32[512,1536]{1,0:T(8,128)} %get-tuple-element.117.refs_1_, f32[1,1536]{1,0:T(1,128)} %broadcast_in_dim.23.refs_2_, ...), custom_call_target="tpu_custom_call" | custom-call | flops 25165824 | bytes 629145600 | tf_op jit(solution)/shard_map/line_sum/pallas_call | solution.py:367
  838.2 9.3 %convert_element_type.205 = f32[2048,1536]{1,0:T(8,128)} convert(bf16[2048,1536]{1,0:T(8,128)(2,1)} %get-tuple-element.69) | non-fusion elementwise | flops 3145728 | bytes 18874368 | tf_op jit(solution)/shard_map/convert_element_type | solution.py:850
  (188 shorter events, 78.7 us)
Async XLA Ops:
  8.0 339.7 %reduce-scatter.2.cloned.1.call-start = ((), (), s32[]{:S(2)}) async-start(), calls=%async_computation.1 | async-start | bytes 7864320 | tf_op jit(solution)/shard_map/reduce_scatter | solution.py:787
  19.9 8.4 copy-start.13
  27.2 7.8 copy-start.28
  174.1 39.9 %slice-start.6 = ((s8[5308416]{0:T(1024)(128)(4,1)}), s8[4194304]{0:T(1024)(128)(4,1)S(1)}, s32[]{:S(2)}) async-start(s8[5308416]{0:T(1024)(128)(4,1)} %bitcast.116), calls=%async_computation.11 | async-start | bytes 8388608
  191.4 22.6 %slice-start.7 = ((s8[5308416]{0:T(1024)(128)(4,1)}), s8[1114112]{0:T(1024)(128)(4,1)S(1)}, s32[]{:S(2)}) async-start(s8[5308416]{0:T(1024)(128)(4,1)} %bitcast.116), calls=%async_computation.12 | async-start | bytes 2228224
  229.6 359.7 %all-reduce.8.cloned.1.call-start = ((), (), s32[]{:S(2)}) async-start(), calls=%async_computation.4 | async-start | bytes 31850496 | tf_op jit(solution)/shard_map/psum | solution.py:805
  234.0 17.2 %copy-start.12 = (bf16[2048,1536]{1,0:T(8,128)(2,1)}, bf16[2048,1536]{1,0:T(8,128)(2,1)S(1)}, u32[]{:S(2)}) copy-start(bf16[2048,1536]{1,0:T(8,128)(2,1)S(1)} %broadcast_select_fusion) | copy-start | bytes 18874372
  274.8 16.8 %copy-start.42 = (bf16[2048,1728]{0,1:T(8,128)(2,1)S(1)}, bf16[2048,1728]{0,1:T(8,128)(2,1)}, u32[]{:S(2)}) copy-start(bf16[2048,1728]{0,1:T(8,128)(2,1)} %get-tuple-element.91) | copy-start | bytes 21233668
  306.8 320.8 %all-gather.2.cloned.1.call-start = ((), (), s32[]{:S(2)}) async-start(), calls=%async_computation.2 | async-start | bytes 7864320 | tf_op jit(solution)/shard_map/all_gather | solution.py:810
  306.8 24.5 %slice-start.8 = ((s8[5308416]{0:T(1024)(128)(4,1)}), s8[4194304]{0:T(1024)(128)(4,1)S(1)}, s32[]{:S(2)}) async-start(s8[5308416]{0:T(1024)(128)(4,1)} %bitcast.118), calls=%async_computation.13 | async-start | bytes 8388608
  306.8 24.5 %slice-start.10 = ((s8[7077888]{0:T(1024)(128)(4,1)}), s8[4194304]{0:T(1024)(128)(4,1)S(1)}, s32[]{:S(2)}) async-start(s8[7077888]{0:T(1024)(128)(4,1)} %bitcast.120), calls=%async_computation.15 | async-start | bytes 8388608
  313.3 18.0 %slice-start.9 = ((s8[5308416]{0:T(1024)(128)(4,1)}), s8[1114112]{0:T(1024)(128)(4,1)S(1)}, s32[]{:S(2)}) async-start(s8[5308416]{0:T(1024)(128)(4,1)} %bitcast.118), calls=%async_computation.14 | async-start | bytes 2228224
  313.3 18.0 %slice-start.11 = ((s8[7077888]{0:T(1024)(128)(4,1)}), s8[2883584]{0:T(1024)(128)(4,1)S(1)}, s32[]{:S(2)}) async-start(s8[7077888]{0:T(1024)(128)(4,1)} %bitcast.120), calls=%async_computation.16 | async-start | bytes 5767168
  347.8 162.8 %copy-start.10 = (f32[512,1536]{1,0:T(8,128)S(1)}, f32[512,1536]{1,0:T(8,128)}, u32[]{:S(2)}) copy-start(f32[512,1536]{1,0:T(8,128)} %get-tuple-element.47.refs_1_) | copy-start | bytes 9437188
  347.8 162.8 %copy-start.21 = (bf16[512,1536]{1,0:T(8,128)(2,1)S(1)}, bf16[512,1536]{1,0:T(8,128)(2,1)}, u32[]{:S(2)}) copy-start(bf16[512,1536]{1,0:T(8,128)(2,1)} %reduce-scatter.2.cloned.1.call-done) | copy-start | bytes 4718596
  512.8 337.6 %all-reduce.6.cloned.1.call-start = ((), (), s32[]{:S(2)}) async-start(), calls=%async_computation.3 | async-start | bytes 6291456 | tf_op jit(solution)/shard_map/psum | solution.py:847
  514.1 7.5 copy-start.1
  514.1 7.5 copy-start.2
  514.1 7.5 copy-start.3
  589.3 9.3 %copy-start.15 = (bf16[1536,1728]{0,1:T(8,128)(2,1)S(1)}, bf16[1536,1728]{0,1:T(8,128)(2,1)}, u32[]{:S(2)}) copy-start(bf16[1536,1728]{0,1:T(8,128)(2,1)} %get-tuple-element.88) | copy-start | bytes 15925252
  589.3 15.7 %slice-start.2 = ((s8[5308416]{0:T(1024)(128)(4,1)}), s8[4194304]{0:T(1024)(128)(4,1)S(1)}, s32[]{:S(2)}) async-start(s8[5308416]{0:T(1024)(128)(4,1)} %bitcast.110), calls=%async_computation.7 | async-start | bytes 8388608
  634.3 13.8 %slice-start = ((s8[6291456]{0:T(1024)(128)(4,1)}), s8[2097152]{0:T(1024)(128)(4,1)S(1)}, s32[]{:S(2)}) async-start(s8[6291456]{0:T(1024)(128)(4,1)} %bitcast.106), calls=%async_computation.5 | async-start | bytes 4194304
  653.4 12.0 %copy-start.31 = (f32[1536]{0:T(1024)S(1)}, f32[1536]{0:T(1024)}, u32[]{:S(2)}) copy-start(f32[1536]{0:T(1024)} %param.17) | copy-start | bytes 18436
  653.4 13.5 %copy-start.39 = (f32[128]{0:T(128)S(1)}, f32[128]{0:T(128)}, u32[]{:S(2)}) copy-start(f32[128]{0:T(128)} %get-tuple-element.100) | copy-start | bytes 1540
  (35 other events, 150.6 us)
Sparse Core Ops, SparseCore 0:
  229.7 110.7 reduce-scatter.1
  512.9 114.5 all-gather.1
Sparse Core Ops, SparseCore 1:
  306.8 208.2 all-reduce.7
  665.6 67.9 all-reduce.5

commit v5 on v4

--- a/solution.py
+++ b/solution.py
@@ -668,6 +668,30 @@
     )(length, q, k, v, w, tokens, gain)
 
 
+def widen_kernel(after_ref, *refs):
+    half = len(refs) // 2
+    for narrow, wide in zip(refs[:half], refs[half:]):
+        wide[...] = narrow[...].astype(F32)
+
+
+def widen(arrays, after):
+    rows, width = arrays[0].shape
+    size = next(s for s in (288, 144, 96, 16, rows) if rows % s == 0)
+    block = pl.BlockSpec((size, width), lambda i: (i, 0))
+    return pl.pallas_call(
+        widen_kernel,
+        grid=(rows // size,),
+        out_shape=(jax.ShapeDtypeStruct((rows, width), F32),) * len(arrays),
+        in_specs=[pl.BlockSpec(after.shape, lambda i: (0, 0))] + [block] * len(arrays),
+        out_specs=(block,) * len(arrays),
+        compiler_params=pltpu.CompilerParams(
+            dimension_semantics=("arbitrary",), vmem_limit_bytes=32 << 20
+        ),
+        cost_estimate=pl.CostEstimate(flops=rows, transcendentals=0, bytes_accessed=rows * width),
+        name="widen",
+    )(after, *arrays)
+
+
 def inverse_rms(x):
     return lax.rsqrt(jnp.mean(x * x, axis=-1, keepdims=True) + EPSILON)
 
@@ -758,12 +782,13 @@
     inputs = tokens.astype(F32)
     normed = (inputs * inverse_rms(inputs) * norm_gain).astype(BF16)
     inputs_own = own(tokens).astype(F32)
-    queries = nn(normed, query_w)
-    keys_val = nn(normed, key_weight)
+    qkv_w = jnp.concatenate([query_w, key_weight, value_weight], axis=1)
+    edges = (q_width, q_width + k_width)
+    queries, keys_val, values = jnp.split(nn(normed, qkv_w), edges, axis=1)
     tables = rope_tables(row_count)
     q_pad = to_lanes(prepare(queries, query_gain, tables).astype(BF16))
     k_pad = to_lanes(prepare(keys_val, key_gain, tables).astype(BF16))
-    v_pad = to_lanes(nn(normed, value_weight).astype(BF16))
+    v_pad = to_lanes(values.astype(BF16))
     normed2, resid_own, mixed_pad, inverse_sums = attn_gather(
         lengths,
         q_pad,
@@ -799,8 +824,8 @@
         pieces,
         2,
     )
-    g_gate = tn(normed2, d_gate).astype(BF16)
-    g_up = tn(normed2, d_up).astype(BF16)
+    g_gate = tn(d_gate, normed2).astype(BF16)
+    g_up = tn(d_up, normed2).astype(BF16)
     g_down = tn(hidden, d_out).astype(BF16)
     g_gate, g_up, g_down = lax.psum((g_gate, g_up, g_down), "dp")
 
@@ -815,8 +840,9 @@
     dq, d_qgain = prepare_back(queries, query_gain, tables, dq[:, :q_width])
     dk, d_kgain = prepare_back(keys_val, key_gain, tables, dk[:, :k_width])
     d_q, d_k, d_v = dq.astype(BF16), dk.astype(BF16), dv[:, :k_width].astype(BF16)
-    d_q, d_k, d_v, block_out = lax.optimization_barrier((d_q, d_k, d_v, block_out))
-    d_normed = (nt(d_q, query_w) + nt(d_k, key_weight) + nt(d_v, value_weight)).astype(BF16)
+    d_qkv = jnp.concatenate([d_q, d_k, d_v], axis=1)
+    late_qkv, block_out = lax.optimization_barrier((d_qkv, block_out))
+    d_normed = nt(late_qkv, qkv_w).astype(BF16)
     head_terms = jnp.concatenate([d_qgain, d_kgain])
     terms = jnp.concatenate(
         [
@@ -826,7 +852,7 @@
             jnp.zeros((5, width), F32),
         ]
     )
-    whole_grads = tuple(g.astype(F32) + after for g in (g_gate, g_up, g_down))
+    whole_grads = widen((g_gate, g_up, g_down), d_mlp_gain)
     d_normed, *whole_grads = lax.optimization_barrier((d_normed, *whole_grads))
     d_inputs, _, d_gains = line_sum(
         d_normed,
@@ -838,25 +864,24 @@
         True,
     )
     g_out = tn(mixed, d_resid).astype(BF16)
-    g_query = tn(normed, d_q).astype(BF16)
-    g_key = tn(normed, d_k).astype(BF16)
-    g_value = tn(normed, d_v).astype(BF16)
-    g_out, g_query, g_key, g_value, *whole_grads = lax.optimization_barrier(
-        (g_out, g_query, g_key, g_value, *whole_grads)
-    )
-    g_out, g_query, g_key, g_value = lax.psum((g_out, g_query, g_key, g_value), "dp")
+    g_qkv = tn(normed, d_qkv).astype(BF16)
+    g_out, g_qkv, *whole_grads = lax.optimization_barrier((g_out, g_qkv, *whole_grads))
+    g_out, g_qkv = lax.psum((g_out, g_qkv), "dp")
+    g_query, g_key, g_value = jnp.split(g_qkv.astype(F32), edges, axis=1)
     return (
         block_out,
         d_inputs.astype(F32),
         d_gains[0],
-        g_query.astype(F32),
-        g_key.astype(F32),
-        g_value.astype(F32),
+        g_query,
+        g_key,
+        g_value,
         g_out.astype(F32),
         d_gains[2, :HEAD_SIZE],
         d_gains[2, HEAD_SIZE : 2 * HEAD_SIZE],
         d_gains[1],
-        *whole_grads,
+        whole_grads[0].T,
+        whole_grads[1].T,
+        whole_grads[2],
     )
 
 

time: 881 us -> 843 us (0.957)
  matrix products: 225 us -> 191 us
  other arithmetic: 70.4 us -> 40.7 us
  local copies, waits for them, and re-layouts: 23.7 us -> 40.7 us
  Pallas kernels: 519 us -> 531 us
    add x3 -> x0, other arithmetic: 22 us -> none  [on_device(): whole_grads = tuple((g.astype(F32) + after for g in (g_gate, g_up, g_down)))]
    dot_general x7 -> x5, matrix products: 90.7 us -> 71.5 us  [nt(): lax.dot_general(a, b, (((1,), (1,)), ((), ())), preferred_element_type=F32)]
    unnamed x111 -> x110, local copies, waits for them, and re-layouts: 8.57 us -> 22.6 us
    pallas_call x0 -> x1, Pallas kernels: none -> 11.8 us  [widen(): pl.pallas_call(widen_kernel, grid=(rows // size,), out_shape=(jax.ShapeDt...]
    dot_general x6 -> x4, matrix products: 68.6 us -> 59.9 us  [nn(): lax.dot_general(a, b, (((1,), (0,)), ((), ())), preferred_element_type=F32)]
    dot_general x7 -> x5, matrix products: 65.6 us -> 60 us  [tn(): lax.dot_general(a, b, (((0,), (0,)), ((), ())), preferred_element_type=F32)]
  transfers between devices with their start and end apart: 4 -> 4, of which waited for: 1 -> 2; matrix products, arithmetic and copies ran while one was open for 21% -> 19% of each run, Pallas kernels for 44% -> 47%
where the time goes in v5:
time: 843 us; the launch traced here: 835 us
  Pallas kernels  531 us (63%)
  matrix products  191 us (23%)
  local copies, waits for them, and re-layouts  40.7 us (5%)
  other arithmetic  40.7 us (5%)
  between operations  17.3 us (2%)
  waiting for transfers between devices  14.6 us (2%)
    pallas_call x2, Pallas kernels, line_sum(): pl.pallas_call(functools.partial(line_sum_kernel, count, pieces, finish,...  332 us
    pallas_call x1, Pallas kernels, attn_gather(): pl.pallas_call(functools.partial(attn_gather_kernel, count, ways, head_pl...  138 us
    dot_general x5, matrix products, nt(): lax.dot_general(a, b, (((1,), (1,)), ((), ())), preferred_element_type=F32)  71.5 us
    dot_general x5, matrix products, tn(): lax.dot_general(a, b, (((0,), (0,)), ((), ())), preferred_element_type=F32)  60 us
    dot_general x4, matrix products, nn(): lax.dot_general(a, b, (((1,), (0,)), ((), ())), preferred_element_type=F32)  59.9 us
    pallas_call x1, Pallas kernels, attn_bwd(): pl.pallas_call(functools.partial(bwd_kernel, places, tiles, bq, bk), out_...  49.3 us
    unnamed x110, local copies, waits for them, and re-layouts  22.6 us
  transfers between devices with their start and end apart: 4, of which 2 were waited for; matrix products, arithmetic and copies ran while one was open for 19% of the time, Pallas kernels for 47%

profile of v5, /device:TPU:0, one launch (start us, length us, event | category | flops | bytes accessed | tf_op | source)
XLA Modules:
  0.0 835.4 jit_solution(11848201321591617441)
XLA Ops:
  9.7 4.8 fusion
  14.8 4.5 fusion.7
  31.5 137.6 %attention_gather.1 = (bf16[2048,1536]{1,0:T(8,128)(2,1)}, f32[512,1536]{1,0:T(8,128)}, bf16[2048,384]{1,0:T(8,128)(2,1)}, f32[2048,384]{1,0:T(8,128)}) custom-call(s32[1]{0:T(128)} %copy.62.len_ref, bf16[2048,384]{1,0:T(8,128)(2,1)} %copy.48.q_ref, bf16[2048,128]{1,0:T(8,128)(2,1)} %copy.47.k_ref, bf16[2048,128]{1,0:T(8,128)(2,1)} %copy.53.v_ref, ...), custom_call_target="tpu_custom_call" | custom-call | flops 6442450944 | bytes 377487360 | tf_op jit(solution)/shard_map/attention_gather/pallas_call | solution.py:634
  169.1 17.2 %fusion.16 = f32[2048,1728]{0,1:T(8,128)} fusion(bf16[2048,1536]{1,0:T(8,128)(2,1)} %get-tuple-element.47, bf16[1536,1728]{0,1:T(8,128)(2,1)} %param.25), kind=kOutput, calls=%fused_computation.83 | convolution fusion | flops 10871635968 | bytes 25755648 | tf_op jit(solution)/shard_map/dot_general | solution.py:24
  186.3 22.6 %multiply_convert_fusion.2 = (bf16[2048,1728]{0,1:T(8,128)(2,1)}, f32[2048,1728]{0,1:T(8,128)}) fusion(f32[2048,1728]{0,1:T(8,128)} %fusion.16, bf16[2048,1536]{1,0:T(8,128)(2,1)} %get-tuple-element.47, bf16[1536,1728]{0,1:T(8,128)(2,1)} %param.26), kind=kOutput, calls=%fused_computation.5 | convolution fusion | flops 10892869632 | bytes 46989312 | tf_op jit(solution)/shard_map/dot_general | solution.py:24
  208.9 15.6 %convolution_convert_fusion.4 = bf16[2048,1536]{1,0:T(8,128)(2,1)} fusion(bf16[2048,1728]{0,1:T(8,128)(2,1)} %get-tuple-element.111, bf16[1728,1536]{1,0:T(8,128)(2,1)S(1)} %bitcast.108), kind=kOutput, calls=%fused_computation.14 | convolution fusion | flops 10874781696 | bytes 18677760 | tf_op jit(solution)/shard_map/dot_general | solution.py:24
  224.6 4.3 broadcast_select_fusion
  228.9 17.3 %convolution_convert_fusion = bf16[1728,1536]{1,0:T(8,128)(2,1)} fusion(bf16[2048,1728]{0,1:T(8,128)(2,1)} %get-tuple-element.111, bf16[2048,1536]{1,0:T(8,128)(2,1)S(1)} %broadcast_select_fusion), kind=kOutput, calls=%fused_computation.10 | convolution fusion | flops 10874290176 | bytes 18677760 | tf_op jit(solution)/shard_map/dot_general | solution.py:23
  246.2 23.6 %multiply_convert_fusion = (bf16[2048,1728]{0,1:T(8,128)(2,1)}, bf16[2048,1728]{0,1:T(8,128)(2,1)}) fusion(f32[2048,1728]{0,1:T(8,128)} %fusion.16, f32[2048,1728]{0,1:T(8,128)} %get-tuple-element.48, bf16[2048,1536]{1,0:T(8,128)(2,1)S(1)} %broadcast_select_fusion, bf16[1728,1536]{1,0:T(8,128)(2,1)} %param.27), kind=kOutput, calls=%fused_computation.2 | convolution fusion | flops 10917642240 | bytes 54067200 | tf_op jit(solution)/shard_map/dot_general | solution.py:22
  269.8 16.8 %convolution_convert_fusion.1 = bf16[1728,1536]{1,0:T(8,128)(2,1)} fusion(bf16[2048,1728]{0,1:T(8,128)(2,1)} %get-tuple-element.86, bf16[2048,1536]{1,0:T(8,128)(2,1)} %get-tuple-element.47), kind=kOutput, calls=%fused_computation.11 | convolution fusion | flops 10874290176 | bytes 18677760 | tf_op jit(solution)/shard_map/dot_general | solution.py:23
  286.5 15.4 %convolution_convert_fusion.2 = bf16[1728,1536]{1,0:T(8,128)(2,1)} fusion(bf16[2048,1728]{0,1:T(8,128)(2,1)S(1)} %copy-done.38, bf16[2048,1536]{1,0:T(8,128)(2,1)} %get-tuple-element.47), kind=kOutput, calls=%fused_computation.12 | convolution fusion | flops 10874290176 | bytes 18677760 | tf_op jit(solution)/shard_map/dot_general | solution.py:23
  302.0 6.2 dynamic-slice_convert_fusion
  308.3 18.2 %fusion.17 = f32[2048,1536]{1,0:T(8,128)} fusion(bf16[2048,1728]{0,1:T(8,128)(2,1)} %get-tuple-element.87, bf16[1536,1728]{0,1:T(8,128)(2,1)} %param.25), kind=kOutput, calls=%fused_computation.84 | convolution fusion | flops 10871635968 | bytes 24969216 | tf_op jit(solution)/shard_map/dot_general | solution.py:22
  326.5 16.4 %add_convert_fusion.part_ref = bf16[2048,1536]{1,0:T(8,128)(2,1)} fusion(f32[2048,1536]{1,0:T(8,128)} %fusion.17, bf16[2048,1728]{0,1:T(8,128)(2,1)S(1)} %bitcast.112, bf16[1536,1728]{0,1:T(8,128)(2,1)S(1)} %bitcast.110), kind=kOutput, calls=%fused_computation.9 | convolution fusion | flops 10877927424 | bytes 31260672 | tf_op jit(solution)/shard_map/dot_general | solution.py:22
  342.9 161.8 %line_sum.2 = (bf16[2048,1536]{1,0:T(8,128)(2,1)}, f32[512,1536]{1,0:T(8,128)}, f32[8,1536]{1,0:T(8,128)}) custom-call(bf16[2048,1536]{1,0:T(8,128)(2,1)} %add_convert_fusion.part_ref, f32[512,1536]{1,0:T(8,128)} %get-tuple-element.114.refs_0_, f32[512,1536]{1,0:T(8,128)} %get-tuple-element.46.refs_1_, f32[1,1536]{1,0:T(1,128)} %broadcast_in_dim.20.gain_ref.refs_2_), custom_call_target="tpu_custom_call" | custom-call | flops 25165824 | bytes 629145600 | tf_op jit(solution)/shard_map/line_sum/pallas_call | solution.py:367
  519.1 11.8 %widen.1 = (f32[1728,1536]{1,0:T(8,128)}, f32[1728,1536]{1,0:T(8,128)}, f32[1728,1536]{1,0:T(8,128)}) custom-call(f32[8,1536]{1,0:T(8,128)S(1)} %copy-done.6, bf16[1728,1536]{1,0:T(8,128)(2,1)S(1)} %copy-done.1, bf16[1728,1536]{1,0:T(8,128)(2,1)S(1)} %copy-done.2, bf16[1728,1536]{1,0:T(8,128)(2,1)S(1)} %copy-done.3), custom_call_target="tpu_custom_call" | custom-call | flops 1728 | bytes 2654208 | tf_op jit(solution)/shard_map/widen/pallas_call | solution.py:681
  531.0 4.5 convolution_convert_fusion.7.do_ref
  535.5 49.3 %attention_backward.1 = (f32[2048,384]{1,0:T(8,128)}, f32[2048,128]{1,0:T(8,128)S(1)}, f32[2048,128]{1,0:T(8,128)S(1)}) custom-call(s32[1]{0:T(128)} %copy.62.len_ref, bf16[2048,384]{1,0:T(8,128)(2,1)S(1)} %copy-done, bf16[2048,384]{1,0:T(8,128)(2,1)} %convolution_convert_fusion.7.do_ref, bf16[2048,384]{1,0:T(8,128)(2,1)} %get-tuple-element.56.o_ref, ...), custom_call_target="tpu_custom_call" | custom-call | flops 786432 | bytes 1572864 | tf_op jit(solution)/shard_map/attention_backward/pallas_call | solution.py:107
  603.4 6.9 convolution_convert_fusion.5
  610.3 12.6 %all-gather.2.cloned.1.call-done = bf16[2048,1536]{1,0:T(8,128)(2,1)} async-done(((bf16[512,1536]{1,0:T(8,128)(2,1)}), bf16[2048,1536]{1,0:T(8,128)(2,1)}) %all-gather.2.cloned.1.call-update) | async-done | bytes 6291472 | tf_op jit(solution)/shard_map/all_gather | solution.py:835
  623.0 8.8 %convolution_convert_fusion.3.part_ref = bf16[2048,1536]{1,0:T(8,128)(2,1)} fusion(bf16[2048,640]{0,1:T(8,128)(2,1)S(1)} %pad_maximum_fusion.1, bf16[1536,640]{1,0:T(8,128)(2,1)} %copy-done.23), kind=kOutput, calls=%fused_computation.13 | convolution fusion | flops 4029677568 | bytes 10878976 | tf_op jit(solution)/shard_map/dot_general | solution.py:22
  633.4 170.1 %line_sum.3 = (bf16[2048,1536]{1,0:T(8,128)(2,1)}, f32[512,1536]{1,0:T(8,128)}, f32[8,1536]{1,0:T(8,128)}) custom-call(bf16[2048,1536]{1,0:T(8,128)(2,1)} %convolution_convert_fusion.3.part_ref, f32[512,1536]{1,0:T(8,128)} %get-tuple-element.68.refs_0_, f32[512,1536]{1,0:T(8,128)} %get-tuple-element.113.refs_1_, f32[1,1536]{1,0:T(1,128)} %broadcast_in_dim.23.refs_2_, ...), custom_call_target="tpu_custom_call" | custom-call | flops 25165824 | bytes 629145600 | tf_op jit(solution)/shard_map/line_sum/pallas_call | solution.py:367
  803.6 9.3 %convert_element_type.178 = f32[2048,1536]{1,0:T(8,128)} convert(bf16[2048,1536]{1,0:T(8,128)(2,1)} %get-tuple-element.69) | non-fusion elementwise | flops 3145728 | bytes 18874368 | tf_op jit(solution)/shard_map/convert_element_type | solution.py:873
  821.7 5.9 copy.63
  (184 shorter events, 56.6 us)
Async XLA Ops:
  8.0 6.5 copy-start.24
  8.0 6.6 copy-start.25
  8.0 6.7 copy-start.29
  8.0 334.9 %reduce-scatter.2.cloned.1.call-start = ((), (), s32[]{:S(2)}) async-start(), calls=%async_computation.1 | async-start | bytes 7864320 | tf_op jit(solution)/shard_map/reduce_scatter | solution.py:812
  8.1 6.7 copy-start.11
  25.0 5.9 copy-start.28
  26.6 142.5 %copy-start.26 = (f32[2048,2]{0,1:T(2,128)}, f32[2048,2]{0,1:T(2,128)S(1)}, u32[]{:S(2)}) copy-start(f32[2048,2]{0,1:T(2,128)S(1)} %add_rsqrt_fusion.1) | copy-start | bytes 49156
  169.1 39.8 %slice-start.8 = ((s8[5308416]{0:T(1024)(128)(4,1)}), s8[4194304]{0:T(1024)(128)(4,1)S(1)}, s32[]{:S(2)}) async-start(s8[5308416]{0:T(1024)(128)(4,1)} %bitcast.107), calls=%async_computation.13 | async-start | bytes 8388608
  186.3 22.6 %slice-start.9 = ((s8[5308416]{0:T(1024)(128)(4,1)}), s8[1114112]{0:T(1024)(128)(4,1)S(1)}, s32[]{:S(2)}) async-start(s8[5308416]{0:T(1024)(128)(4,1)} %bitcast.107), calls=%async_computation.14 | async-start | bytes 2228224
  224.5 286.1 %all-reduce.8.cloned.1.call-start = ((), (), s32[]{:S(2)}) async-start(), calls=%async_computation.4 | async-start | bytes 31850496 | tf_op jit(solution)/shard_map/psum | solution.py:830
  228.9 17.3 %copy-start.12 = (bf16[2048,1536]{1,0:T(8,128)(2,1)}, bf16[2048,1536]{1,0:T(8,128)(2,1)S(1)}, u32[]{:S(2)}) copy-start(bf16[2048,1536]{1,0:T(8,128)(2,1)S(1)} %broadcast_select_fusion) | copy-start | bytes 18874372
  269.8 16.8 %copy-start.38 = (bf16[2048,1728]{0,1:T(8,128)(2,1)S(1)}, bf16[2048,1728]{0,1:T(8,128)(2,1)}, u32[]{:S(2)}) copy-start(bf16[2048,1728]{0,1:T(8,128)(2,1)} %get-tuple-element.87) | copy-start | bytes 21233668
  301.9 321.0 %all-gather.2.cloned.1.call-start = ((), (), s32[]{:S(2)}) async-start(), calls=%async_computation.2 | async-start | bytes 7864320 | tf_op jit(solution)/shard_map/all_gather | solution.py:835
  302.0 24.5 %slice-start.10 = ((s8[5308416]{0:T(1024)(128)(4,1)}), s8[4194304]{0:T(1024)(128)(4,1)S(1)}, s32[]{:S(2)}) async-start(s8[5308416]{0:T(1024)(128)(4,1)} %bitcast.109), calls=%async_computation.15 | async-start | bytes 8388608
  302.0 24.5 %slice-start.12 = ((s8[7077888]{0:T(1024)(128)(4,1)}), s8[4194304]{0:T(1024)(128)(4,1)S(1)}, s32[]{:S(2)}) async-start(s8[7077888]{0:T(1024)(128)(4,1)} %bitcast.111), calls=%async_computation.17 | async-start | bytes 8388608
  308.3 18.2 %slice-start.11 = ((s8[5308416]{0:T(1024)(128)(4,1)}), s8[1114112]{0:T(1024)(128)(4,1)S(1)}, s32[]{:S(2)}) async-start(s8[5308416]{0:T(1024)(128)(4,1)} %bitcast.109), calls=%async_computation.16 | async-start | bytes 2228224
  308.3 18.2 %slice-start.13 = ((s8[7077888]{0:T(1024)(128)(4,1)}), s8[2883584]{0:T(1024)(128)(4,1)S(1)}, s32[]{:S(2)}) async-start(s8[7077888]{0:T(1024)(128)(4,1)} %bitcast.111), calls=%async_computation.18 | async-start | bytes 5767168
  342.9 163.1 %copy-start.10 = (f32[512,1536]{1,0:T(8,128)S(1)}, f32[512,1536]{1,0:T(8,128)}, u32[]{:S(2)}) copy-start(f32[512,1536]{1,0:T(8,128)} %get-tuple-element.46.refs_1_) | copy-start | bytes 9437188
  342.9 163.1 %copy-start.19 = (bf16[512,1536]{1,0:T(8,128)(2,1)S(1)}, bf16[512,1536]{1,0:T(8,128)(2,1)}, u32[]{:S(2)}) copy-start(bf16[512,1536]{1,0:T(8,128)(2,1)} %reduce-scatter.2.cloned.1.call-done) | copy-start | bytes 4718596
  506.0 24.9 %slice-start.4 = ((s8[6291456]{0:T(1024)(128)(4,1)}), s8[2097152]{0:T(1024)(128)(4,1)S(1)}, s32[]{:S(2)}) async-start(s8[6291456]{0:T(1024)(128)(4,1)} %bitcast.103), calls=%async_computation.9 | async-start | bytes 4194304
  508.4 307.3 %all-reduce.6.cloned.1.call-start = ((), (), s32[]{:S(2)}) async-start(), calls=%async_computation.3 | async-start | bytes 6291456 | tf_op jit(solution)/shard_map/psum | solution.py:869
  519.1 11.8 %slice-start.5 = ((s8[6291456]{0:T(1024)(128)(4,1)}), s8[4194304]{0:T(1024)(128)(4,1)S(1)}, s32[]{:S(2)}) async-start(s8[6291456]{0:T(1024)(128)(4,1)} %bitcast.103), calls=%async_computation.10 | async-start | bytes 8388608
  519.1 11.8 %copy-start.37 = (bf16[384,1536]{1,0:T(8,128)(2,1)S(1)}, bf16[384,1536]{1,0:T(8,128)(2,1)}, u32[]{:S(2)}) copy-start(bf16[384,1536]{1,0:T(8,128)(2,1)} %w_ref.1) | copy-start | bytes 3538948
  597.2 6.2 slice-start.2
  (33 other events, 108.7 us)
Sparse Core Ops, SparseCore 0:
  224.6 111.0 reduce-scatter.1
  508.6 114.3 all-gather.1
Sparse Core Ops, SparseCore 1:
  302.0 208.5 all-reduce.7
  631.9 67.5 all-reduce.5

commit v6 on v5

--- a/solution.py
+++ b/solution.py
@@ -256,8 +256,8 @@
             sum_wait(c, last, False)
             acc[...] += down_buf[c, last - 1].astype(F32)
 
-        mine = pl.ds(c * size, size)
-        full_ref[rows(me, c), :] = finish(c, mine, acc[...], own_refs, out_refs)
+        mine = pl.ds(pl.multiple_of(c * size, size), size)
+        full_ref[rows(me, c), :] = finish(mine, acc[...], own_refs, out_refs)
 
     def share(axis, to, sender, at):
         here, place, sem = (me, shared, 8) if axis == "tensor" else (spot, shared_ways, 10)
@@ -295,32 +295,47 @@
         out_refs[1][...] = terms
 
     greet_line(count, ways if share_terms else 0)
-    for slot in range(pieces + 2 * last):
-        if slot < pieces:
+    if len(out_refs) > 1:
+        out_refs[1][...] = own_refs[3][...] if len(own_refs) > 3 else jnp.zeros_like(out_refs[1])
+
+    def stage(c, run):
+        @pl.when((c >= 0) & (c < pieces))
+        def _():
+            run(c)
+
+    def both(start, s):
+        def run(c):
             for upward in (True, False):
-                sum_start(slot, 1, upward)
+                start(c, s, upward)
+
+        return run
+
+    def owner_turn(c):
+        settle(c)
+        both(give_start, 1)(c)
+
+    @pl.loop(0, pieces + 2 * last)
+    def _(slot):
+        stage(slot, both(sum_start, 1))
         for s in range(last, 1, -1):
-            c = slot - last - (s - 1)
-            if 0 <= c < pieces:
-                for upward in (True, False):
-                    give_start(c, s, upward)
-        c = slot - last
-        if 0 <= c < pieces:
-            settle(c)
-            for upward in (True, False):
-                give_start(c, 1, upward)
-            if share_terms and c == pieces - 1:
+            stage(slot - last - (s - 1), both(give_start, s))
+        stage(slot - last, owner_turn)
+        if share_terms:
+
+            @pl.when(slot == pieces - 1 + last)
+            def _():
                 share_start("tensor", count, me)
-        if share_terms and c == pieces + last - 2:
-            share_finish("tensor", count, me, shared)
-            share_start("dp", ways, spot)
+
+            @pl.when(slot == pieces + 2 * last - 2)
+            def _():
+                share_finish("tensor", count, me, shared)
+                share_start("dp", ways, spot)
+
         for s in range(last, 1, -1):
-            c = slot - (s - 1)
-            if 0 <= c < pieces:
-                for upward in (True, False):
-                    sum_start(c, s, upward)
-    for c in range(pieces):
-
+            stage(slot - (s - 1), both(sum_start, s))
+
+    @pl.loop(0, pieces)
+    def _(c):
         @pl.when(me == last)
         def _():
             give_wait(c, last, True)
@@ -389,21 +404,15 @@
     )(part, *owned)
 
 
-def finish_back(c, mine, total, own_refs, out_refs):
+def finish_back(mine, total, own_refs, out_refs):
     base, value, gain = own_refs[:3]
-    x = value[mine, :]
+    x = value[mine, :].astype(F32)
     r = inverse_rms(x)
     y = x * r
     e = gain[...] * total
-    out = base[mine, :] + r * (e - y * jnp.mean(e * y, axis=-1, keepdims=True))
+    out = base[mine, :].astype(F32) + r * (e - y * jnp.mean(e * y, axis=-1, keepdims=True))
     out_refs[0][mine, :] = out
-    term = jnp.sum(total * y, axis=0, keepdims=True)
-    row = lax.broadcasted_iota(jnp.int32, (8, 1), 0)
-    if c == 0:
-        more = own_refs[3][...] if len(own_refs) > 3 else 0.0
-        out_refs[1][...] = jnp.where(row == 0, term, more)
-    else:
-        out_refs[1][...] += jnp.where(row == 0, term, 0.0)
+    out_refs[1][0:1, :] += jnp.sum(total * y, axis=0, keepdims=True)
     return out.astype(BF16)
 
 
@@ -671,21 +680,21 @@
 def widen_kernel(after_ref, *refs):
     half = len(refs) // 2
     for narrow, wide in zip(refs[:half], refs[half:]):
-        wide[...] = narrow[...].astype(F32)
-
-
-def widen(arrays, after):
+        wide[...] = narrow[...].astype(wide.dtype)
+
+
+def widen(arrays, types, sizes, after):
     rows, width = arrays[0].shape
-    size = next(s for s in (288, 144, 96, 16, rows) if rows % s == 0)
+    size = next(s for s in (*sizes, rows) if rows % s == 0)
     block = pl.BlockSpec((size, width), lambda i: (i, 0))
     return pl.pallas_call(
         widen_kernel,
         grid=(rows // size,),
-        out_shape=(jax.ShapeDtypeStruct((rows, width), F32),) * len(arrays),
-        in_specs=[pl.BlockSpec(after.shape, lambda i: (0, 0))] + [block] * len(arrays),
+        out_shape=tuple(jax.ShapeDtypeStruct((rows, width), t) for t in types),
+        in_specs=[pl.BlockSpec((8, LANES), lambda i: (0, 0))] + [block] * len(arrays),
         out_specs=(block,) * len(arrays),
         compiler_params=pltpu.CompilerParams(
-            dimension_semantics=("arbitrary",), vmem_limit_bytes=32 << 20
+            dimension_semantics=("arbitrary",), vmem_limit_bytes=58 << 20
         ),
         cost_estimate=pl.CostEstimate(flops=rows, transcendentals=0, bytes_accessed=rows * width),
         name="widen",
@@ -781,7 +790,7 @@
     d_out = jnp.where(live, cotangent, jnp.zeros_like(cotangent))
     inputs = tokens.astype(F32)
     normed = (inputs * inverse_rms(inputs) * norm_gain).astype(BF16)
-    inputs_own = own(tokens).astype(F32)
+    inputs_own = own(tokens)
     qkv_w = jnp.concatenate([query_w, key_weight, value_weight], axis=1)
     edges = (q_width, q_width + k_width)
     queries, keys_val, values = jnp.split(nn(normed, qkv_w), edges, axis=1)
@@ -818,7 +827,7 @@
     d_normed2, mlp_own = lax.optimization_barrier((d_normed2, mlp_own))
     d_resid, d_resid_own, d_mlp_gain = line_sum(
         d_normed2,
-        (own(d_out).astype(F32), resid_own, mlp_gain[None]),
+        (own(d_out), resid_own, mlp_gain[None]),
         (own_shape, gain_shape),
         finish_back,
         pieces,
@@ -852,7 +861,7 @@
             jnp.zeros((5, width), F32),
         ]
     )
-    whole_grads = widen((g_gate, g_up, g_down), d_mlp_gain)
+    whole_grads = widen((g_gate, g_up, g_down), (F32,) * 3, (96,), d_mlp_gain)
     d_normed, *whole_grads = lax.optimization_barrier((d_normed, *whole_grads))
     d_inputs, _, d_gains = line_sum(
         d_normed,
@@ -867,10 +876,11 @@
     g_qkv = tn(normed, d_qkv).astype(BF16)
     g_out, g_qkv, *whole_grads = lax.optimization_barrier((g_out, g_qkv, *whole_grads))
     g_out, g_qkv = lax.psum((g_out, g_qkv), "dp")
-    g_query, g_key, g_value = jnp.split(g_qkv.astype(F32), edges, axis=1)
+    g_query, g_key, g_value = (g.astype(F32) for g in jnp.split(g_qkv, edges, axis=1))
+    d_inputs, block_out = widen((d_inputs, block_out), (F32, BF16), (256,), d_gains)
     return (
         block_out,
-        d_inputs.astype(F32),
+        d_inputs,
         d_gains[0],
         g_query,
         g_key,

time: 843 us -> 840 us (level)
  Pallas kernels: 531 us -> 549 us
  local copies, waits for them, and re-layouts: 40.7 us -> 28.9 us
  other arithmetic: 40.7 us -> 31.2 us
    pallas_call x1 -> x2, Pallas kernels: 11.8 us -> 31.1 us  [widen(): pl.pallas_call(widen_kernel, grid=(rows // size,), out_shape=tuple((jax.S...]
    unnamed x110 -> x97, local copies, waits for them, and re-layouts: 22.6 us -> 8.11 us
    convert_element_type x2, other arithmetic: 15.6 us -> 5.29 us  [on_device(): g.astype(F32)]
  transfers between devices with their start and end apart: 4 -> 4, of which waited for: 2 -> 2; matrix products, arithmetic and copies ran while one was open for 19% -> 19% of each run, Pallas kernels for 47% -> 50%
where the time goes in v6:
time: 840 us; the launch traced here: 832 us
  Pallas kernels  549 us (65%)
  matrix products  195 us (23%)
  other arithmetic  31.2 us (4%)
  local copies, waits for them, and re-layouts  28.9 us (3%)
  between operations  17.3 us (2%)
  waiting for transfers between devices  9.75 us (1%)
    pallas_call x2, Pallas kernels, line_sum(): pl.pallas_call(functools.partial(line_sum_kernel, count, pieces, finish,...  331 us
    pallas_call x1, Pallas kernels, attn_gather(): pl.pallas_call(functools.partial(attn_gather_kernel, count, ways, head_pl...  137 us
    dot_general x5, matrix products, nt(): lax.dot_general(a, b, (((1,), (1,)), ((), ())), preferred_element_type=F32)  75.3 us
    dot_general x4, matrix products, nn(): lax.dot_general(a, b, (((1,), (0,)), ((), ())), preferred_element_type=F32)  59.8 us
    dot_general x5, matrix products, tn(): lax.dot_general(a, b, (((0,), (0,)), ((), ())), preferred_element_type=F32)  59.8 us
    pallas_call x1, Pallas kernels, attn_bwd(): pl.pallas_call(functools.partial(bwd_kernel, places, tiles, bq, bk), out_...  49.3 us
    pallas_call x2, Pallas kernels, widen(): pl.pallas_call(widen_kernel, grid=(rows // size,), out_shape=tuple((jax.S...  31.1 us
  transfers between devices with their start and end apart: 4, of which 2 were waited for; matrix products, arithmetic and copies ran while one was open for 19% of the time, Pallas kernels for 50%

profile of v6, /device:TPU:0, one launch (start us, length us, event | category | flops | bytes accessed | tf_op | source)
XLA Modules:
  0.0 831.7 jit_solution(3117171933842836744)
XLA Ops:
  9.7 4.8 fusion
  14.8 4.5 fusion.7
  31.5 137.3 %attention_gather.1 = (bf16[2048,1536]{1,0:T(8,128)(2,1)}, f32[512,1536]{1,0:T(8,128)}, bf16[2048,384]{1,0:T(8,128)(2,1)}, f32[2048,384]{1,0:T(8,128)}) custom-call(s32[1]{0:T(128)} %copy.61.len_ref, bf16[2048,384]{1,0:T(8,128)(2,1)} %copy.48.q_ref, bf16[2048,128]{1,0:T(8,128)(2,1)} %copy.47.k_ref, bf16[2048,128]{1,0:T(8,128)(2,1)} %copy.53.v_ref, ...), custom_call_target="tpu_custom_call" | custom-call | flops 6442450944 | bytes 377487360 | tf_op jit(solution)/shard_map/attention_gather/pallas_call | solution.py:643
  168.8 17.2 %fusion.15 = f32[2048,1728]{0,1:T(8,128)} fusion(bf16[2048,1536]{1,0:T(8,128)(2,1)} %get-tuple-element.49, bf16[1536,1728]{0,1:T(8,128)(2,1)} %param.25), kind=kOutput, calls=%fused_computation.85 | convolution fusion | flops 10871635968 | bytes 25755648 | tf_op jit(solution)/shard_map/dot_general | solution.py:24
  186.0 22.6 %multiply_convert_fusion.2 = (bf16[2048,1728]{0,1:T(8,128)(2,1)}, f32[2048,1728]{0,1:T(8,128)}) fusion(f32[2048,1728]{0,1:T(8,128)} %fusion.15, bf16[2048,1536]{1,0:T(8,128)(2,1)} %get-tuple-element.49, bf16[1536,1728]{0,1:T(8,128)(2,1)} %param.26), kind=kOutput, calls=%fused_computation.5 | convolution fusion | flops 10892869632 | bytes 46989312 | tf_op jit(solution)/shard_map/dot_general | solution.py:24
  208.5 15.6 %convolution_convert_fusion.4 = bf16[2048,1536]{1,0:T(8,128)(2,1)} fusion(bf16[2048,1728]{0,1:T(8,128)(2,1)} %get-tuple-element.115, bf16[1728,1536]{1,0:T(8,128)(2,1)S(1)} %bitcast.106), kind=kOutput, calls=%fused_computation.14 | convolution fusion | flops 10874781696 | bytes 18677760 | tf_op jit(solution)/shard_map/dot_general | solution.py:24
  224.2 4.5 broadcast_select_fusion
  228.8 17.3 %convolution_convert_fusion = bf16[1728,1536]{1,0:T(8,128)(2,1)} fusion(bf16[2048,1728]{0,1:T(8,128)(2,1)} %get-tuple-element.115, bf16[2048,1536]{1,0:T(8,128)(2,1)S(1)} %broadcast_select_fusion), kind=kOutput, calls=%fused_computation.10 | convolution fusion | flops 10874290176 | bytes 18677760 | tf_op jit(solution)/shard_map/dot_general | solution.py:23
  246.0 23.6 %multiply_convert_fusion = (bf16[2048,1728]{0,1:T(8,128)(2,1)}, bf16[2048,1728]{0,1:T(8,128)(2,1)}) fusion(f32[2048,1728]{0,1:T(8,128)} %fusion.15, f32[2048,1728]{0,1:T(8,128)} %get-tuple-element.50, bf16[2048,1536]{1,0:T(8,128)(2,1)S(1)} %broadcast_select_fusion, bf16[1728,1536]{1,0:T(8,128)(2,1)} %param.27), kind=kOutput, calls=%fused_computation.2 | convolution fusion | flops 10917642240 | bytes 54067200 | tf_op jit(solution)/shard_map/dot_general | solution.py:22
  269.6 16.8 %convolution_convert_fusion.1 = bf16[1728,1536]{1,0:T(8,128)(2,1)} fusion(bf16[2048,1728]{0,1:T(8,128)(2,1)} %get-tuple-element.90, bf16[2048,1536]{1,0:T(8,128)(2,1)} %get-tuple-element.49), kind=kOutput, calls=%fused_computation.11 | convolution fusion | flops 10874290176 | bytes 18677760 | tf_op jit(solution)/shard_map/dot_general | solution.py:23
  286.3 15.2 %convolution_convert_fusion.2 = bf16[1728,1536]{1,0:T(8,128)(2,1)} fusion(bf16[2048,1728]{0,1:T(8,128)(2,1)S(1)} %copy-done.34, bf16[2048,1536]{1,0:T(8,128)(2,1)} %get-tuple-element.49), kind=kOutput, calls=%fused_computation.12 | convolution fusion | flops 10874290176 | bytes 18677760 | tf_op jit(solution)/shard_map/dot_general | solution.py:23
  301.6 4.0 constant_dynamic-slice_fusion
  305.6 19.3 %fusion.16 = f32[2048,1536]{1,0:T(8,128)} fusion(bf16[2048,1728]{0,1:T(8,128)(2,1)} %get-tuple-element.91, bf16[1536,1728]{0,1:T(8,128)(2,1)} %param.25), kind=kOutput, calls=%fused_computation.86 | convolution fusion | flops 10871635968 | bytes 24969216 | tf_op jit(solution)/shard_map/dot_general | solution.py:22
  325.0 16.0 %add_convert_fusion.part_ref = bf16[2048,1536]{1,0:T(8,128)(2,1)} fusion(f32[2048,1536]{1,0:T(8,128)} %fusion.16, bf16[2048,1728]{0,1:T(8,128)(2,1)S(1)} %bitcast.110, bf16[1536,1728]{0,1:T(8,128)(2,1)S(1)} %bitcast.108), kind=kOutput, calls=%fused_computation.9 | convolution fusion | flops 10877927424 | bytes 31260672 | tf_op jit(solution)/shard_map/dot_general | solution.py:22
  341.0 161.7 %line_sum.2 = (bf16[2048,1536]{1,0:T(8,128)(2,1)}, f32[512,1536]{1,0:T(8,128)}, f32[8,1536]{1,0:T(8,128)}) custom-call(bf16[2048,1536]{1,0:T(8,128)(2,1)} %add_convert_fusion.part_ref, bf16[512,1536]{1,0:T(8,128)(2,1)} %get-tuple-element.118.refs_0_, f32[512,1536]{1,0:T(8,128)} %get-tuple-element.48.refs_1_, f32[1,1536]{1,0:T(1,128)} %broadcast_in_dim.20.gain_ref.refs_2_), custom_call_target="tpu_custom_call" | custom-call | flops 25165824 | bytes 629145600 | tf_op jit(solution)/shard_map/line_sum/pallas_call | solution.py:382
  510.2 18.8 %widen.2 = (f32[1728,1536]{1,0:T(8,128)}, f32[1728,1536]{1,0:T(8,128)}, f32[1728,1536]{1,0:T(8,128)}) custom-call(f32[8,1536]{1,0:T(8,128)} %get-tuple-element.54.after_ref, bf16[1728,1536]{1,0:T(8,128)(2,1)} %get-tuple-element.87.refs_0_, bf16[1728,1536]{1,0:T(8,128)(2,1)} %get-tuple-element.88.refs_1_, bf16[1728,1536]{1,0:T(8,128)(2,1)} %get-tuple-element.89.refs_2_), custom_call_target="tpu_custom_call" | custom-call | flops 1728 | bytes 2654208 | tf_op jit(solution)/shard_map/widen/pallas_call | solution.py:690
  529.0 7.6 convolution_convert_fusion.7.do_ref
  536.6 49.3 %attention_backward.1 = (f32[2048,384]{1,0:T(8,128)}, f32[2048,128]{1,0:T(8,128)S(1)}, f32[2048,128]{1,0:T(8,128)S(1)}) custom-call(s32[1]{0:T(128)} %copy.61.len_ref, bf16[2048,384]{1,0:T(8,128)(2,1)S(1)} %copy-done, bf16[2048,384]{1,0:T(8,128)(2,1)} %convolution_convert_fusion.7.do_ref, bf16[2048,384]{1,0:T(8,128)(2,1)} %get-tuple-element.58.o_ref, ...), custom_call_target="tpu_custom_call" | custom-call | flops 786432 | bytes 1572864 | tf_op jit(solution)/shard_map/attention_backward/pallas_call | solution.py:107
  585.9 3.8 copy.50
  607.4 6.9 convolution_convert_fusion.5
  614.3 6.2 all-gather.2.cloned.1.call-done.refs_1_
  620.5 8.8 %convolution_convert_fusion.3.part_ref = bf16[2048,1536]{1,0:T(8,128)(2,1)} fusion(bf16[2048,640]{0,1:T(8,128)(2,1)S(1)} %pad_maximum_fusion.1, bf16[1536,640]{1,0:T(8,128)(2,1)} %copy-done.19), kind=kOutput, calls=%fused_computation.13 | convolution fusion | flops 4029677568 | bytes 10878976 | tf_op jit(solution)/shard_map/dot_general | solution.py:22
  631.8 169.7 %line_sum.3 = (bf16[2048,1536]{1,0:T(8,128)(2,1)}, f32[512,1536]{1,0:T(8,128)}, f32[8,1536]{1,0:T(8,128)}) custom-call(bf16[2048,1536]{1,0:T(8,128)(2,1)} %convolution_convert_fusion.3.part_ref, f32[512,1536]{1,0:T(8,128)} %get-tuple-element.69.refs_0_, bf16[512,1536]{1,0:T(8,128)(2,1)} %get-tuple-element.117.refs_1_, f32[1,1536]{1,0:T(1,128)} %broadcast_in_dim.23.refs_2_, ...), custom_call_target="tpu_custom_call" | custom-call | flops 25165824 | bytes 629145600 | tf_op jit(solution)/shard_map/line_sum/pallas_call | solution.py:382
  801.5 12.4 %widen.3 = (f32[2048,1536]{1,0:T(8,128)}, bf16[2048,1536]{1,0:T(8,128)(2,1)}) custom-call(f32[8,1536]{1,0:T(8,128)} %get-tuple-element.70.after_ref, bf16[2048,1536]{1,0:T(8,128)(2,1)} %get-tuple-element.71.refs_0_, bf16[2048,1536]{1,0:T(8,128)(2,1)} %all-gather.2.cloned.1.call-done.refs_1_), custom_call_target="tpu_custom_call" | custom-call | flops 2048 | bytes 3145728 | tf_op jit(solution)/shard_map/widen/pallas_call | solution.py:690
  (170 shorter events, 50.6 us)
Async XLA Ops:
  8.0 6.5 copy-start.20
  8.0 6.6 copy-start.21
  8.0 6.7 copy-start.25
  8.0 332.9 %reduce-scatter.2.cloned.1.call-start = ((), (), s32[]{:S(2)}) async-start(), calls=%async_computation.1 | async-start | bytes 7864320 | tf_op jit(solution)/shard_map/reduce_scatter | solution.py:821
  8.1 6.7 copy-start.7
  168.8 39.7 %slice-start.6 = ((s8[5308416]{0:T(1024)(128)(4,1)}), s8[4194304]{0:T(1024)(128)(4,1)S(1)}, s32[]{:S(2)}) async-start(s8[5308416]{0:T(1024)(128)(4,1)} %bitcast.105), calls=%async_computation.11 | async-start | bytes 8388608
  186.0 22.6 %slice-start.7 = ((s8[5308416]{0:T(1024)(128)(4,1)}), s8[1114112]{0:T(1024)(128)(4,1)S(1)}, s32[]{:S(2)}) async-start(s8[5308416]{0:T(1024)(128)(4,1)} %bitcast.105), calls=%async_computation.12 | async-start | bytes 2228224
  224.2 286.0 %all-reduce.8.cloned.1.call-start = ((), (), s32[]{:S(2)}) async-start(), calls=%async_computation.4 | async-start | bytes 31850496 | tf_op jit(solution)/shard_map/psum | solution.py:839
  228.7 17.3 %copy-start.8 = (bf16[2048,1536]{1,0:T(8,128)(2,1)}, bf16[2048,1536]{1,0:T(8,128)(2,1)S(1)}, u32[]{:S(2)}) copy-start(bf16[2048,1536]{1,0:T(8,128)(2,1)S(1)} %broadcast_select_fusion) | copy-start | bytes 18874372
  269.6 16.8 %copy-start.34 = (bf16[2048,1728]{0,1:T(8,128)(2,1)S(1)}, bf16[2048,1728]{0,1:T(8,128)(2,1)}, u32[]{:S(2)}) copy-start(bf16[2048,1728]{0,1:T(8,128)(2,1)} %get-tuple-element.91) | copy-start | bytes 21233668
  301.6 319.0 %all-gather.2.cloned.1.call-start = ((), (), s32[]{:S(2)}) async-start(), calls=%async_computation.2 | async-start | bytes 7864320 | tf_op jit(solution)/shard_map/all_gather | solution.py:844
  301.6 23.3 %slice-start.8 = ((s8[5308416]{0:T(1024)(128)(4,1)}), s8[4194304]{0:T(1024)(128)(4,1)S(1)}, s32[]{:S(2)}) async-start(s8[5308416]{0:T(1024)(128)(4,1)} %bitcast.107), calls=%async_computation.13 | async-start | bytes 8388608
  301.6 23.3 %slice-start.10 = ((s8[7077888]{0:T(1024)(128)(4,1)}), s8[4194304]{0:T(1024)(128)(4,1)S(1)}, s32[]{:S(2)}) async-start(s8[7077888]{0:T(1024)(128)(4,1)} %bitcast.109), calls=%async_computation.15 | async-start | bytes 8388608
  305.6 19.3 %slice-start.9 = ((s8[5308416]{0:T(1024)(128)(4,1)}), s8[1114112]{0:T(1024)(128)(4,1)S(1)}, s32[]{:S(2)}) async-start(s8[5308416]{0:T(1024)(128)(4,1)} %bitcast.107), calls=%async_computation.14 | async-start | bytes 2228224
  305.6 19.4 %slice-start.11 = ((s8[7077888]{0:T(1024)(128)(4,1)}), s8[2883584]{0:T(1024)(128)(4,1)S(1)}, s32[]{:S(2)}) async-start(s8[7077888]{0:T(1024)(128)(4,1)} %bitcast.109), calls=%async_computation.16 | async-start | bytes 5767168
  341.0 163.0 %copy-start.6 = (f32[512,1536]{1,0:T(8,128)S(1)}, f32[512,1536]{1,0:T(8,128)}, u32[]{:S(2)}) copy-start(f32[512,1536]{1,0:T(8,128)} %get-tuple-element.48.refs_1_) | copy-start | bytes 9437188
  341.0 163.0 %copy-start.15 = (bf16[512,1536]{1,0:T(8,128)(2,1)S(1)}, bf16[512,1536]{1,0:T(8,128)(2,1)}, u32[]{:S(2)}) copy-start(bf16[512,1536]{1,0:T(8,128)(2,1)} %reduce-scatter.2.cloned.1.call-done) | copy-start | bytes 4718596
  506.2 310.5 %all-reduce.6.cloned.1.call-start = ((), (), s32[]{:S(2)}) async-start(), calls=%async_computation.3 | async-start | bytes 6291456 | tf_op jit(solution)/shard_map/psum | solution.py:878
  510.2 18.8 %copy-start.33 = (bf16[384,1536]{1,0:T(8,128)(2,1)S(1)}, bf16[384,1536]{1,0:T(8,128)(2,1)}, u32[]{:S(2)}) copy-start(bf16[384,1536]{1,0:T(8,128)(2,1)} %w_ref.1) | copy-start | bytes 3538948
  529.0 7.6 copy-start
  529.0 7.6 copy-start.1
  529.0 7.6 copy-start.2
  585.9 8.2 copy-start.10
  601.1 6.3 slice-start.2
  (27 other events, 87.6 us)
Sparse Core Ops, SparseCore 0:
  224.3 110.9 reduce-scatter.1
  506.3 114.1 all-gather.1
Sparse Core Ops, SparseCore 1:
  301.6 208.5 all-reduce.7
  629.5 67.5 all-reduce.5

commit v7 on v6

--- a/solution.py
+++ b/solution.py
@@ -683,7 +683,7 @@
         wide[...] = narrow[...].astype(wide.dtype)
 
 
-def widen(arrays, types, sizes, after):
+def widen(arrays, types, sizes, after, vmem):
     rows, width = arrays[0].shape
     size = next(s for s in (*sizes, rows) if rows % s == 0)
     block = pl.BlockSpec((size, width), lambda i: (i, 0))
@@ -694,7 +694,7 @@
         in_specs=[pl.BlockSpec((8, LANES), lambda i: (0, 0))] + [block] * len(arrays),
         out_specs=(block,) * len(arrays),
         compiler_params=pltpu.CompilerParams(
-            dimension_semantics=("arbitrary",), vmem_limit_bytes=58 << 20
+            dimension_semantics=("arbitrary",), vmem_limit_bytes=vmem << 20
         ),
         cost_estimate=pl.CostEstimate(flops=rows, transcendentals=0, bytes_accessed=rows * width),
         name="widen",
@@ -850,8 +850,7 @@
     dk, d_kgain = prepare_back(keys_val, key_gain, tables, dk[:, :k_width])
     d_q, d_k, d_v = dq.astype(BF16), dk.astype(BF16), dv[:, :k_width].astype(BF16)
     d_qkv = jnp.concatenate([d_q, d_k, d_v], axis=1)
-    late_qkv, block_out = lax.optimization_barrier((d_qkv, block_out))
-    d_normed = nt(late_qkv, qkv_w).astype(BF16)
+    d_normed = nt(d_qkv, qkv_w).astype(BF16)
     head_terms = jnp.concatenate([d_qgain, d_kgain])
     terms = jnp.concatenate(
         [
@@ -861,8 +860,10 @@
             jnp.zeros((5, width), F32),
         ]
     )
-    whole_grads = widen((g_gate, g_up, g_down), (F32,) * 3, (96,), d_mlp_gain)
-    d_normed, *whole_grads = lax.optimization_barrier((d_normed, *whole_grads))
+    whole_grads = widen((g_gate, g_up, g_down), (F32,) * 3, (288, 96), d_mlp_gain, 58)
+    d_normed, block_out, *whole_grads = lax.optimization_barrier(
+        (d_normed, block_out, *whole_grads)
+    )
     d_inputs, _, d_gains = line_sum(
         d_normed,
         (d_resid_own, inputs_own, norm_gain[None], terms),
@@ -877,7 +878,7 @@
     g_out, g_qkv, *whole_grads = lax.optimization_barrier((g_out, g_qkv, *whole_grads))
     g_out, g_qkv = lax.psum((g_out, g_qkv), "dp")
     g_query, g_key, g_value = (g.astype(F32) for g in jnp.split(g_qkv, edges, axis=1))
-    d_inputs, block_out = widen((d_inputs, block_out), (F32, BF16), (256,), d_gains)
+    d_inputs, block_out = widen((d_inputs, block_out), (F32, BF16), (256,), d_gains, 16)
     return (
         block_out,
         d_inputs,

time: 840 us -> 827 us (0.985)
  transfers between devices with their start and end apart: 4 -> 4, of which waited for: 2 -> 2; matrix products, arithmetic and copies ran while one was open for 19% -> 20% of each run, Pallas kernels for 50% -> 49%
where the time goes in v7:
time: 827 us; the launch traced here: 820 us
  Pallas kernels  542 us (66%)
  matrix products  193 us (23%)
  other arithmetic  30.8 us (4%)
  local copies, waits for them, and re-layouts  29.3 us (4%)
  between operations  17.4 us (2%)
    pallas_call x2, Pallas kernels, line_sum(): pl.pallas_call(functools.partial(line_sum_kernel, count, pieces, finish,...  331 us
    pallas_call x1, Pallas kernels, attn_gather(): pl.pallas_call(functools.partial(attn_gather_kernel, count, ways, head_pl...  137 us
    dot_general x5, matrix products, nt(): lax.dot_general(a, b, (((1,), (1,)), ((), ())), preferred_element_type=F32)  73.8 us
    dot_general x4, matrix products, nn(): lax.dot_general(a, b, (((1,), (0,)), ((), ())), preferred_element_type=F32)  59.8 us
    dot_general x5, matrix products, tn(): lax.dot_general(a, b, (((0,), (0,)), ((), ())), preferred_element_type=F32)  59.8 us
    pallas_call x1, Pallas kernels, attn_bwd(): pl.pallas_call(functools.partial(bwd_kernel, places, tiles, bq, bk), out_...  49.3 us
    pallas_call x2, Pallas kernels, widen(): pl.pallas_call(widen_kernel, grid=(rows // size,), out_shape=tuple((jax.S...  24.2 us
  transfers between devices with their start and end apart: 4, of which 2 were waited for; matrix products, arithmetic and copies ran while one was open for 20% of the time, Pallas kernels for 49%

profile of v7, /device:TPU:0, one launch (start us, length us, event | category | flops | bytes accessed | tf_op | source)
XLA Modules:
  0.0 819.6 jit_solution(14779941073310246483)
XLA Ops:
  9.7 4.8 fusion
  14.8 4.5 fusion.7
  31.5 137.4 %attention_gather.1 = (bf16[2048,1536]{1,0:T(8,128)(2,1)}, f32[512,1536]{1,0:T(8,128)}, bf16[2048,384]{1,0:T(8,128)(2,1)}, f32[2048,384]{1,0:T(8,128)}) custom-call(s32[1]{0:T(128)} %copy.61.len_ref, bf16[2048,384]{1,0:T(8,128)(2,1)} %copy.48.q_ref, bf16[2048,128]{1,0:T(8,128)(2,1)} %copy.47.k_ref, bf16[2048,128]{1,0:T(8,128)(2,1)} %copy.53.v_ref, ...), custom_call_target="tpu_custom_call" | custom-call | flops 6442450944 | bytes 377487360 | tf_op jit(solution)/shard_map/attention_gather/pallas_call | solution.py:643
  168.9 17.2 %fusion.17 = f32[2048,1728]{0,1:T(8,128)} fusion(bf16[2048,1536]{1,0:T(8,128)(2,1)} %get-tuple-element.48, bf16[1536,1728]{0,1:T(8,128)(2,1)} %param.25), kind=kOutput, calls=%fused_computation.87 | convolution fusion | flops 10871635968 | bytes 25755648 | tf_op jit(solution)/shard_map/dot_general | solution.py:24
  186.1 22.6 %multiply_convert_fusion.2 = (bf16[2048,1728]{0,1:T(8,128)(2,1)}, f32[2048,1728]{0,1:T(8,128)}) fusion(f32[2048,1728]{0,1:T(8,128)} %fusion.17, bf16[2048,1536]{1,0:T(8,128)(2,1)} %get-tuple-element.48, bf16[1536,1728]{0,1:T(8,128)(2,1)} %param.26), kind=kOutput, calls=%fused_computation.5 | convolution fusion | flops 10892869632 | bytes 46989312 | tf_op jit(solution)/shard_map/dot_general | solution.py:24
  208.6 15.6 %convolution_convert_fusion.4 = bf16[2048,1536]{1,0:T(8,128)(2,1)} fusion(bf16[2048,1728]{0,1:T(8,128)(2,1)} %get-tuple-element.113, bf16[1728,1536]{1,0:T(8,128)(2,1)S(1)} %bitcast.107), kind=kOutput, calls=%fused_computation.14 | convolution fusion | flops 10874781696 | bytes 18677760 | tf_op jit(solution)/shard_map/dot_general | solution.py:24
  224.3 4.5 broadcast_select_fusion
  228.9 17.3 %convolution_convert_fusion = bf16[1728,1536]{1,0:T(8,128)(2,1)} fusion(bf16[2048,1728]{0,1:T(8,128)(2,1)} %get-tuple-element.113, bf16[2048,1536]{1,0:T(8,128)(2,1)S(1)} %broadcast_select_fusion), kind=kOutput, calls=%fused_computation.10 | convolution fusion | flops 10874290176 | bytes 18677760 | tf_op jit(solution)/shard_map/dot_general | solution.py:23
  246.1 23.6 %multiply_convert_fusion = (bf16[2048,1728]{0,1:T(8,128)(2,1)}, bf16[2048,1728]{0,1:T(8,128)(2,1)}) fusion(f32[2048,1728]{0,1:T(8,128)} %fusion.17, f32[2048,1728]{0,1:T(8,128)} %get-tuple-element.49, bf16[2048,1536]{1,0:T(8,128)(2,1)S(1)} %broadcast_select_fusion, bf16[1728,1536]{1,0:T(8,128)(2,1)} %param.27), kind=kOutput, calls=%fused_computation.2 | convolution fusion | flops 10917642240 | bytes 54067200 | tf_op jit(solution)/shard_map/dot_general | solution.py:22
  269.7 16.8 %convolution_convert_fusion.1 = bf16[1728,1536]{1,0:T(8,128)(2,1)} fusion(bf16[2048,1728]{0,1:T(8,128)(2,1)} %get-tuple-element.88, bf16[2048,1536]{1,0:T(8,128)(2,1)} %get-tuple-element.48), kind=kOutput, calls=%fused_computation.11 | convolution fusion | flops 10874290176 | bytes 18677760 | tf_op jit(solution)/shard_map/dot_general | solution.py:23
  286.5 15.1 %convolution_convert_fusion.2 = bf16[1728,1536]{1,0:T(8,128)(2,1)} fusion(bf16[2048,1728]{0,1:T(8,128)(2,1)S(1)} %copy-done.37, bf16[2048,1536]{1,0:T(8,128)(2,1)} %get-tuple-element.48), kind=kOutput, calls=%fused_computation.12 | convolution fusion | flops 10874290176 | bytes 18677760 | tf_op jit(solution)/shard_map/dot_general | solution.py:23
  301.8 3.9 constant_dynamic-slice_fusion
  305.7 19.4 %fusion.18 = f32[2048,1536]{1,0:T(8,128)} fusion(bf16[2048,1728]{0,1:T(8,128)(2,1)} %get-tuple-element.89, bf16[1536,1728]{0,1:T(8,128)(2,1)} %param.25), kind=kOutput, calls=%fused_computation.88 | convolution fusion | flops 10871635968 | bytes 24969216 | tf_op jit(solution)/shard_map/dot_general | solution.py:22
  325.1 16.0 %add_convert_fusion.part_ref = bf16[2048,1536]{1,0:T(8,128)(2,1)} fusion(f32[2048,1536]{1,0:T(8,128)} %fusion.18, bf16[2048,1728]{0,1:T(8,128)(2,1)S(1)} %bitcast.111, bf16[1536,1728]{0,1:T(8,128)(2,1)S(1)} %bitcast.109), kind=kOutput, calls=%fused_computation.9 | convolution fusion | flops 10877927424 | bytes 31260672 | tf_op jit(solution)/shard_map/dot_general | solution.py:22
  341.1 161.5 %line_sum.2 = (bf16[2048,1536]{1,0:T(8,128)(2,1)}, f32[512,1536]{1,0:T(8,128)}, f32[8,1536]{1,0:T(8,128)}) custom-call(bf16[2048,1536]{1,0:T(8,128)(2,1)} %add_convert_fusion.part_ref, bf16[512,1536]{1,0:T(8,128)(2,1)} %get-tuple-element.116.refs_0_, f32[512,1536]{1,0:T(8,128)} %get-tuple-element.47.refs_1_, f32[1,1536]{1,0:T(1,128)} %broadcast_in_dim.20.gain_ref.refs_2_), custom_call_target="tpu_custom_call" | custom-call | flops 25165824 | bytes 629145600 | tf_op jit(solution)/shard_map/line_sum/pallas_call | solution.py:382
  506.5 3.8 all-reduce.8.cloned.1.call-done
  510.3 17.4 %widen.2 = (f32[1728,1536]{1,0:T(8,128)}, f32[1728,1536]{1,0:T(8,128)}, f32[1728,1536]{1,0:T(8,128)}) custom-call(f32[8,1536]{1,0:T(8,128)} %get-tuple-element.53.after_ref, bf16[1728,1536]{1,0:T(8,128)(2,1)} %get-tuple-element.85.refs_0_, bf16[1728,1536]{1,0:T(8,128)(2,1)} %get-tuple-element.86.refs_1_, bf16[1728,1536]{1,0:T(8,128)(2,1)} %get-tuple-element.87.refs_2_), custom_call_target="tpu_custom_call" | custom-call | flops 1728 | bytes 2654208 | tf_op jit(solution)/shard_map/widen/pallas_call | solution.py:690
  527.7 7.6 convolution_convert_fusion.7.do_ref
  535.3 49.3 %attention_backward.1 = (f32[2048,384]{1,0:T(8,128)}, f32[2048,128]{1,0:T(8,128)S(1)}, f32[2048,128]{1,0:T(8,128)S(1)}) custom-call(s32[1]{0:T(128)} %copy.61.len_ref, bf16[2048,384]{1,0:T(8,128)(2,1)S(1)} %copy-done.1, bf16[2048,384]{1,0:T(8,128)(2,1)} %convolution_convert_fusion.7.do_ref, bf16[2048,384]{1,0:T(8,128)(2,1)} %get-tuple-element.57.o_ref, ...), custom_call_target="tpu_custom_call" | custom-call | flops 786432 | bytes 1572864 | tf_op jit(solution)/shard_map/attention_backward/pallas_call | solution.py:107
  584.6 3.8 copy.50
  604.2 7.4 convolution_convert_fusion.3.part_ref
  611.6 6.9 convolution_convert_fusion.5
  623.0 169.9 %line_sum.3 = (bf16[2048,1536]{1,0:T(8,128)(2,1)}, f32[512,1536]{1,0:T(8,128)}, f32[8,1536]{1,0:T(8,128)}) custom-call(bf16[2048,1536]{1,0:T(8,128)(2,1)} %convolution_convert_fusion.3.part_ref, f32[512,1536]{1,0:T(8,128)} %get-tuple-element.67.refs_0_, bf16[512,1536]{1,0:T(8,128)(2,1)} %get-tuple-element.115.refs_1_, f32[1,1536]{1,0:T(1,128)} %broadcast_in_dim.23.refs_2_, ...), custom_call_target="tpu_custom_call" | custom-call | flops 25165824 | bytes 629145600 | tf_op jit(solution)/shard_map/line_sum/pallas_call | solution.py:382
  796.6 6.8 widen.3
  (180 shorter events, 49.2 us)
Async XLA Ops:
  8.0 333.0 %reduce-scatter.2.cloned.1.call-start = ((), (), s32[]{:S(2)}) async-start(), calls=%async_computation.1 | async-start | bytes 7864320 | tf_op jit(solution)/shard_map/reduce_scatter | solution.py:821
  168.9 39.7 %slice-start.8 = ((s8[5308416]{0:T(1024)(128)(4,1)}), s8[4194304]{0:T(1024)(128)(4,1)S(1)}, s32[]{:S(2)}) async-start(s8[5308416]{0:T(1024)(128)(4,1)} %bitcast.106), calls=%async_computation.13 | async-start | bytes 8388608
  186.1 22.6 %slice-start.9 = ((s8[5308416]{0:T(1024)(128)(4,1)}), s8[1114112]{0:T(1024)(128)(4,1)S(1)}, s32[]{:S(2)}) async-start(s8[5308416]{0:T(1024)(128)(4,1)} %bitcast.106), calls=%async_computation.14 | async-start | bytes 2228224
  224.3 286.0 %all-reduce.8.cloned.1.call-start = ((), (), s32[]{:S(2)}) async-start(), calls=%async_computation.4 | async-start | bytes 31850496 | tf_op jit(solution)/shard_map/psum | solution.py:839
  228.8 17.3 %copy-start.10 = (bf16[2048,1536]{1,0:T(8,128)(2,1)}, bf16[2048,1536]{1,0:T(8,128)(2,1)S(1)}, u32[]{:S(2)}) copy-start(bf16[2048,1536]{1,0:T(8,128)(2,1)S(1)} %broadcast_select_fusion) | copy-start | bytes 18874372
  269.7 16.8 %copy-start.37 = (bf16[2048,1728]{0,1:T(8,128)(2,1)S(1)}, bf16[2048,1728]{0,1:T(8,128)(2,1)}, u32[]{:S(2)}) copy-start(bf16[2048,1728]{0,1:T(8,128)(2,1)} %get-tuple-element.89) | copy-start | bytes 21233668
  301.7 318.9 %all-gather.2.cloned.1.call-start = ((), (), s32[]{:S(2)}) async-start(), calls=%async_computation.2 | async-start | bytes 7864320 | tf_op jit(solution)/shard_map/all_gather | solution.py:844
  301.7 23.3 %slice-start.10 = ((s8[5308416]{0:T(1024)(128)(4,1)}), s8[4194304]{0:T(1024)(128)(4,1)S(1)}, s32[]{:S(2)}) async-start(s8[5308416]{0:T(1024)(128)(4,1)} %bitcast.108), calls=%async_computation.15 | async-start | bytes 8388608
  301.7 23.3 %slice-start.12 = ((s8[7077888]{0:T(1024)(128)(4,1)}), s8[4194304]{0:T(1024)(128)(4,1)S(1)}, s32[]{:S(2)}) async-start(s8[7077888]{0:T(1024)(128)(4,1)} %bitcast.110), calls=%async_computation.17 | async-start | bytes 8388608
  305.7 19.4 %slice-start.11 = ((s8[5308416]{0:T(1024)(128)(4,1)}), s8[1114112]{0:T(1024)(128)(4,1)S(1)}, s32[]{:S(2)}) async-start(s8[5308416]{0:T(1024)(128)(4,1)} %bitcast.108), calls=%async_computation.16 | async-start | bytes 2228224
  305.7 19.4 %slice-start.13 = ((s8[7077888]{0:T(1024)(128)(4,1)}), s8[2883584]{0:T(1024)(128)(4,1)S(1)}, s32[]{:S(2)}) async-start(s8[7077888]{0:T(1024)(128)(4,1)} %bitcast.110), calls=%async_computation.18 | async-start | bytes 5767168
  341.1 162.7 %copy-start.8 = (f32[512,1536]{1,0:T(8,128)S(1)}, f32[512,1536]{1,0:T(8,128)}, u32[]{:S(2)}) copy-start(f32[512,1536]{1,0:T(8,128)} %get-tuple-element.47.refs_1_) | copy-start | bytes 9437188
  341.1 162.7 %copy-start.16 = (bf16[512,1536]{1,0:T(8,128)(2,1)S(1)}, bf16[512,1536]{1,0:T(8,128)(2,1)}, u32[]{:S(2)}) copy-start(bf16[512,1536]{1,0:T(8,128)(2,1)} %reduce-scatter.2.cloned.1.call-done) | copy-start | bytes 4718596
  506.1 298.6 %all-reduce.6.cloned.1.call-start = ((), (), s32[]{:S(2)}) async-start(), calls=%async_computation.3 | async-start | bytes 6291456 | tf_op jit(solution)/shard_map/psum | solution.py:879
  510.3 17.4 %copy-start.36 = (bf16[384,1536]{1,0:T(8,128)(2,1)S(1)}, bf16[384,1536]{1,0:T(8,128)(2,1)}, u32[]{:S(2)}) copy-start(bf16[384,1536]{1,0:T(8,128)(2,1)} %w_ref.1) | copy-start | bytes 3538948
  527.7 7.6 copy-start.1
  527.7 7.6 copy-start.2
  527.7 7.6 copy-start.3
  584.6 8.2 copy-start.12
  600.5 11.1 %slice-start.4 = ((s8[6291456]{0:T(1024)(128)(4,1)}), s8[4194304]{0:T(1024)(128)(4,1)S(1)}, s32[]{:S(2)}) async-start(s8[6291456]{0:T(1024)(128)(4,1)} %bitcast.97), calls=%async_computation.9 | async-start | bytes 8388608
  604.2 7.4 copy-start.29
  604.2 7.4 copy-start.31
  620.6 172.4 %slice-start = ((s8[6291456]{0:T(1024)(128)(4,1)}), s8[2097152]{0:T(1024)(128)(4,1)S(1)}, s32[]{:S(2)}) async-start(s8[6291456]{0:T(1024)(128)(4,1)} %bitcast.89), calls=%async_computation.5 | async-start | bytes 4194304
  623.0 169.9 %slice-start.1 = ((s8[6291456]{0:T(1024)(128)(4,1)}), s8[4194304]{0:T(1024)(128)(4,1)S(1)}, s32[]{:S(2)}) async-start(s8[6291456]{0:T(1024)(128)(4,1)} %bitcast.89), calls=%async_computation.6 | async-start | bytes 8388608
  (32 other events, 122.3 us)
Sparse Core Ops, SparseCore 0:
  224.4 110.9 reduce-scatter.1
  506.2 114.3 all-gather.1
Sparse Core Ops, SparseCore 1:
  301.8 208.5 all-reduce.7
  620.7 67.4 all-reduce.5

commit v8 on v7

--- a/solution.py
+++ b/solution.py
@@ -791,6 +791,8 @@
     inputs = tokens.astype(F32)
     normed = (inputs * inverse_rms(inputs) * norm_gain).astype(BF16)
     inputs_own = own(tokens)
+    own_live = (me * m + jnp.arange(m, dtype=jnp.int32) < lengths[0])[:, None]
+    d_out_own = jnp.where(own_live, own(cotangent), jnp.zeros((), BF16))
     qkv_w = jnp.concatenate([query_w, key_weight, value_weight], axis=1)
     edges = (q_width, q_width + k_width)
     queries, keys_val, values = jnp.split(nn(normed, qkv_w), edges, axis=1)
@@ -820,14 +822,14 @@
     mlp_part, gate, up = lax.optimization_barrier((mlp_part, gate, up))
     mlp_own = lax.psum_scatter(mlp_part, "tensor", scatter_dimension=0, tiled=True)
     sig = jax.nn.sigmoid(gate)
-    d_hidden = nt(d_out, down_w)
+    d_hidden = jnp.where(live, nt(cotangent, down_w), 0.0)
     d_gate = (d_hidden * up * sig * (1.0 + gate * (1.0 - sig))).astype(BF16)
     d_up = (d_hidden * gate * sig).astype(BF16)
     d_normed2 = (nt(d_gate, gate_w) + nt(d_up, up_w)).astype(BF16)
     d_normed2, mlp_own = lax.optimization_barrier((d_normed2, mlp_own))
     d_resid, d_resid_own, d_mlp_gain = line_sum(
         d_normed2,
-        (own(d_out), resid_own, mlp_gain[None]),
+        (d_out_own, resid_own, mlp_gain[None]),
         (own_shape, gain_shape),
         finish_back,
         pieces,

time: 827 us -> 823 us (level)
  transfers between devices with their start and end apart: 4 -> 4, of which waited for: 2 -> 2; matrix products, arithmetic and copies ran while one was open for 20% -> 19% of each run, Pallas kernels for 49% -> 50%
where the time goes in v8:
time: 823 us; the launch traced here: 816 us
  Pallas kernels  543 us (66%)
  matrix products  194 us (24%)
  other arithmetic  30.5 us (4%)
  local copies, waits for them, and re-layouts  25.4 us (3%)
  between operations  17.1 us (2%)
    pallas_call x2, Pallas kernels, line_sum(): pl.pallas_call(functools.partial(line_sum_kernel, count, pieces, finish,...  332 us
    pallas_call x1, Pallas kernels, attn_gather(): pl.pallas_call(functools.partial(attn_gather_kernel, count, ways, head_pl...  137 us
    dot_general x5, matrix products, nt(): lax.dot_general(a, b, (((1,), (1,)), ((), ())), preferred_element_type=F32)  77.9 us
    dot_general x4, matrix products, nn(): lax.dot_general(a, b, (((1,), (0,)), ((), ())), preferred_element_type=F32)  60 us
    dot_general x5, matrix products, tn(): lax.dot_general(a, b, (((0,), (0,)), ((), ())), preferred_element_type=F32)  55.8 us
    pallas_call x1, Pallas kernels, attn_bwd(): pl.pallas_call(functools.partial(bwd_kernel, places, tiles, bq, bk), out_...  49.3 us
    pallas_call x2, Pallas kernels, widen(): pl.pallas_call(widen_kernel, grid=(rows // size,), out_shape=tuple((jax.S...  23.9 us
  transfers between devices with their start and end apart: 4, of which 2 were waited for; matrix products, arithmetic and copies ran while one was open for 19% of the time, Pallas kernels for 50%

profile of v8, /device:TPU:0, one launch (start us, length us, event | category | flops | bytes accessed | tf_op | source)
XLA Modules:
  0.0 815.6 jit_solution(11026946209383314495)
XLA Ops:
  9.7 4.8 fusion
  14.8 4.5 fusion.10
  31.5 137.4 %attention_gather.1 = (bf16[2048,1536]{1,0:T(8,128)(2,1)}, f32[512,1536]{1,0:T(8,128)}, bf16[2048,384]{1,0:T(8,128)(2,1)}, f32[2048,384]{1,0:T(8,128)}) custom-call(s32[1]{0:T(128)} %copy.61.len_ref, bf16[2048,384]{1,0:T(8,128)(2,1)} %copy.48.q_ref, bf16[2048,128]{1,0:T(8,128)(2,1)} %copy.47.k_ref, bf16[2048,128]{1,0:T(8,128)(2,1)} %copy.53.v_ref, ...), custom_call_target="tpu_custom_call" | custom-call | flops 6442450944 | bytes 377487360 | tf_op jit(solution)/shard_map/attention_gather/pallas_call | solution.py:643
  168.9 17.2 %fusion.21 = f32[2048,1728]{0,1:T(8,128)} fusion(bf16[2048,1536]{1,0:T(8,128)(2,1)} %get-tuple-element.48, bf16[1536,1728]{0,1:T(8,128)(2,1)} %param.25), kind=kOutput, calls=%fused_computation.91 | convolution fusion | flops 10871635968 | bytes 25755648 | tf_op jit(solution)/shard_map/dot_general | solution.py:24
  186.1 22.6 %multiply_convert_fusion.2 = (bf16[2048,1728]{0,1:T(8,128)(2,1)}, f32[2048,1728]{0,1:T(8,128)}) fusion(f32[2048,1728]{0,1:T(8,128)} %fusion.21, bf16[2048,1536]{1,0:T(8,128)(2,1)} %get-tuple-element.48, bf16[1536,1728]{0,1:T(8,128)(2,1)} %param.26), kind=kOutput, calls=%fused_computation.5 | convolution fusion | flops 10892869632 | bytes 46989312 | tf_op jit(solution)/shard_map/dot_general | solution.py:24
  208.7 15.7 %convolution_convert_fusion.4 = bf16[2048,1536]{1,0:T(8,128)(2,1)} fusion(bf16[2048,1728]{0,1:T(8,128)(2,1)} %get-tuple-element.113, bf16[1728,1536]{1,0:T(8,128)(2,1)S(1)} %bitcast.109), kind=kOutput, calls=%fused_computation.14 | convolution fusion | flops 10874781696 | bytes 18677760 | tf_op jit(solution)/shard_map/dot_general | solution.py:24
  224.4 27.7 %multiply_convert_fusion = (bf16[2048,1728]{0,1:T(8,128)(2,1)}, bf16[2048,1728]{0,1:T(8,128)(2,1)}) fusion(f32[2048,1728]{0,1:T(8,128)} %fusion.21, pred[2048]{0:T(1024)(128)(4,1)S(1)} %iota_compare_fusion.2, f32[2048,1728]{0,1:T(8,128)} %get-tuple-element.49, bf16[2048,1536]{1,0:T(8,128)(2,1)} %param.16, bf16[1728,1536]{1,0:T(8,128)(2,1)} %param.27), kind=kOutput, calls=%fused_computation.2 | convolution fusion | flops 10921181184 | bytes 54069248 | tf_op jit(solution)/shard_map/dot_general | solution.py:22
  252.2 14.9 %convolution_convert_fusion.1 = bf16[1728,1536]{1,0:T(8,128)(2,1)} fusion(bf16[2048,1728]{0,1:T(8,128)(2,1)} %get-tuple-element.88, bf16[2048,1536]{1,0:T(8,128)(2,1)S(1)} %bitcast.113), kind=kOutput, calls=%fused_computation.11 | convolution fusion | flops 10874290176 | bytes 18677760 | tf_op jit(solution)/shard_map/dot_general | solution.py:23
  267.1 15.0 %convolution_convert_fusion.2 = bf16[1728,1536]{1,0:T(8,128)(2,1)} fusion(bf16[2048,1728]{0,1:T(8,128)(2,1)} %get-tuple-element.89, bf16[2048,1536]{1,0:T(8,128)(2,1)S(1)} %bitcast.113), kind=kOutput, calls=%fused_computation.12 | convolution fusion | flops 10874290176 | bytes 18677760 | tf_op jit(solution)/shard_map/dot_general | solution.py:23
  282.1 15.3 %convolution_convert_fusion = bf16[1728,1536]{1,0:T(8,128)(2,1)} fusion(bf16[2048,1728]{0,1:T(8,128)(2,1)} %get-tuple-element.113, bf16[2048,1536]{1,0:T(8,128)(2,1)S(1)} %bitcast.103, pred[2048]{0:T(1024)(128)(4,1)S(1)} %iota_compare_fusion.2), kind=kOutput, calls=%fused_computation.10 | convolution fusion | flops 10877435904 | bytes 18679808 | tf_op jit(solution)/shard_map/dot_general | solution.py:23
  297.5 4.2 dynamic-slice_select_fusion
  301.7 19.1 %fusion.22 = f32[2048,1536]{1,0:T(8,128)} fusion(bf16[2048,1728]{0,1:T(8,128)(2,1)} %get-tuple-element.89, bf16[1536,1728]{0,1:T(8,128)(2,1)} %param.25), kind=kOutput, calls=%fused_computation.92 | convolution fusion | flops 10871635968 | bytes 24969216 | tf_op jit(solution)/shard_map/dot_general | solution.py:22
  320.9 16.0 %add_convert_fusion.part_ref = bf16[2048,1536]{1,0:T(8,128)(2,1)} fusion(f32[2048,1536]{1,0:T(8,128)} %fusion.22, bf16[2048,1728]{0,1:T(8,128)(2,1)S(1)} %bitcast.115, bf16[1536,1728]{0,1:T(8,128)(2,1)S(1)} %bitcast.111), kind=kOutput, calls=%fused_computation.9 | convolution fusion | flops 10877927424 | bytes 31260672 | tf_op jit(solution)/shard_map/dot_general | solution.py:22
  336.9 162.3 %line_sum.2 = (bf16[2048,1536]{1,0:T(8,128)(2,1)}, f32[512,1536]{1,0:T(8,128)}, f32[8,1536]{1,0:T(8,128)}) custom-call(bf16[2048,1536]{1,0:T(8,128)(2,1)} %add_convert_fusion.part_ref, bf16[512,1536]{1,0:T(8,128)(2,1)} %get-tuple-element.115.refs_0_, f32[512,1536]{1,0:T(8,128)} %get-tuple-element.47.refs_1_, f32[1,1536]{1,0:T(1,128)} %broadcast_in_dim.44.gain_ref.refs_2_), custom_call_target="tpu_custom_call" | custom-call | flops 25165824 | bytes 629145600 | tf_op jit(solution)/shard_map/line_sum/pallas_call | solution.py:382
  505.6 17.1 %widen.2 = (f32[1728,1536]{1,0:T(8,128)}, f32[1728,1536]{1,0:T(8,128)}, f32[1728,1536]{1,0:T(8,128)}) custom-call(f32[8,1536]{1,0:T(8,128)} %get-tuple-element.53.after_ref, bf16[1728,1536]{1,0:T(8,128)(2,1)} %get-tuple-element.85.refs_0_, bf16[1728,1536]{1,0:T(8,128)(2,1)} %get-tuple-element.86.refs_1_, bf16[1728,1536]{1,0:T(8,128)(2,1)} %get-tuple-element.87.refs_2_), custom_call_target="tpu_custom_call" | custom-call | flops 1728 | bytes 2654208 | tf_op jit(solution)/shard_map/widen/pallas_call | solution.py:690
  522.7 7.6 convolution_convert_fusion.7.do_ref
  530.3 49.3 %attention_backward.1 = (f32[2048,384]{1,0:T(8,128)}, f32[2048,128]{1,0:T(8,128)S(1)}, f32[2048,128]{1,0:T(8,128)S(1)}) custom-call(s32[1]{0:T(128)} %copy.61.len_ref, bf16[2048,384]{1,0:T(8,128)(2,1)S(1)} %copy-done.1, bf16[2048,384]{1,0:T(8,128)(2,1)} %convolution_convert_fusion.7.do_ref, bf16[2048,384]{1,0:T(8,128)(2,1)} %get-tuple-element.57.o_ref, ...), custom_call_target="tpu_custom_call" | custom-call | flops 786432 | bytes 1572864 | tf_op jit(solution)/shard_map/attention_backward/pallas_call | solution.py:107
  579.6 3.8 copy.50
  595.5 3.6 convolution_convert_fusion.6
  599.2 7.5 convolution_convert_fusion.3.part_ref
  606.8 6.9 convolution_convert_fusion.5
  613.7 3.3 all-gather.2.cloned.1.call-done.refs_1_
  619.5 169.9 %line_sum.3 = (bf16[2048,1536]{1,0:T(8,128)(2,1)}, f32[512,1536]{1,0:T(8,128)}, f32[8,1536]{1,0:T(8,128)}) custom-call(bf16[2048,1536]{1,0:T(8,128)(2,1)} %convolution_convert_fusion.3.part_ref, f32[512,1536]{1,0:T(8,128)} %get-tuple-element.67.refs_0_, bf16[512,1536]{1,0:T(8,128)(2,1)} %get-tuple-element.116.refs_1_, f32[1,1536]{1,0:T(1,128)} %broadcast_in_dim.76.refs_2_, ...), custom_call_target="tpu_custom_call" | custom-call | flops 25165824 | bytes 629145600 | tf_op jit(solution)/shard_map/line_sum/pallas_call | solution.py:382
  793.0 6.8 widen.3
  (186 shorter events, 46.0 us)
Async XLA Ops:
  8.0 328.8 %reduce-scatter.2.cloned.1.call-start = ((), (), s32[]{:S(2)}) async-start(), calls=%async_computation.1 | async-start | bytes 7864320 | tf_op jit(solution)/shard_map/reduce_scatter | solution.py:823
  168.9 39.8 %slice-start.10 = ((s8[5308416]{0:T(1024)(128)(4,1)}), s8[4194304]{0:T(1024)(128)(4,1)S(1)}, s32[]{:S(2)}) async-start(s8[5308416]{0:T(1024)(128)(4,1)} %bitcast.108), calls=%async_computation.15 | async-start | bytes 8388608
  186.1 22.6 %slice-start.11 = ((s8[5308416]{0:T(1024)(128)(4,1)}), s8[1114112]{0:T(1024)(128)(4,1)S(1)}, s32[]{:S(2)}) async-start(s8[5308416]{0:T(1024)(128)(4,1)} %bitcast.108), calls=%async_computation.16 | async-start | bytes 2228224
  224.3 27.8 %slice-start.14 = ((s8[6291456]{0:T(1024)(128)(4,1)}), s8[2097152]{0:T(1024)(128)(4,1)S(1)}, s32[]{:S(2)}) async-start(s8[6291456]{0:T(1024)(128)(4,1)} %bitcast.112), calls=%async_computation.19 | async-start | bytes 4194304
  224.4 281.2 %all-reduce.8.cloned.1.call-start = ((), (), s32[]{:S(2)}) async-start(), calls=%async_computation.4 | async-start | bytes 31850496 | tf_op jit(solution)/shard_map/psum | solution.py:841
  224.4 27.7 %slice-start.15 = ((s8[6291456]{0:T(1024)(128)(4,1)}), s8[4194304]{0:T(1024)(128)(4,1)S(1)}, s32[]{:S(2)}) async-start(s8[6291456]{0:T(1024)(128)(4,1)} %bitcast.112), calls=%async_computation.20 | async-start | bytes 8388608
  252.2 29.9 %slice-start.6 = ((s8[6291456]{0:T(1024)(128)(4,1)}), s8[4194304]{0:T(1024)(128)(4,1)S(1)}, s32[]{:S(2)}) async-start(s8[6291456]{0:T(1024)(128)(4,1)} %bitcast.102), calls=%async_computation.11 | async-start | bytes 8388608
  267.1 15.0 %slice-start.7 = ((s8[6291456]{0:T(1024)(128)(4,1)}), s8[2097152]{0:T(1024)(128)(4,1)S(1)}, s32[]{:S(2)}) async-start(s8[6291456]{0:T(1024)(128)(4,1)} %bitcast.102), calls=%async_computation.12 | async-start | bytes 4194304
  297.4 319.6 %all-gather.2.cloned.1.call-start = ((), (), s32[]{:S(2)}) async-start(), calls=%async_computation.2 | async-start | bytes 7864320 | tf_op jit(solution)/shard_map/all_gather | solution.py:846
  297.5 23.4 %slice-start.12 = ((s8[5308416]{0:T(1024)(128)(4,1)}), s8[4194304]{0:T(1024)(128)(4,1)S(1)}, s32[]{:S(2)}) async-start(s8[5308416]{0:T(1024)(128)(4,1)} %bitcast.110), calls=%async_computation.17 | async-start | bytes 8388608
  297.5 23.4 %slice-start.16 = ((s8[7077888]{0:T(1024)(128)(4,1)}), s8[4194304]{0:T(1024)(128)(4,1)S(1)}, s32[]{:S(2)}) async-start(s8[7077888]{0:T(1024)(128)(4,1)} %bitcast.114), calls=%async_computation.21 | async-start | bytes 8388608
  301.7 19.1 %slice-start.13 = ((s8[5308416]{0:T(1024)(128)(4,1)}), s8[1114112]{0:T(1024)(128)(4,1)S(1)}, s32[]{:S(2)}) async-start(s8[5308416]{0:T(1024)(128)(4,1)} %bitcast.110), calls=%async_computation.18 | async-start | bytes 2228224
  301.7 19.1 %slice-start.17 = ((s8[7077888]{0:T(1024)(128)(4,1)}), s8[2883584]{0:T(1024)(128)(4,1)S(1)}, s32[]{:S(2)}) async-start(s8[7077888]{0:T(1024)(128)(4,1)} %bitcast.114), calls=%async_computation.22 | async-start | bytes 5767168
  336.9 163.5 %copy-start.8 = (f32[512,1536]{1,0:T(8,128)S(1)}, f32[512,1536]{1,0:T(8,128)}, u32[]{:S(2)}) copy-start(f32[512,1536]{1,0:T(8,128)} %get-tuple-element.47.refs_1_) | copy-start | bytes 9437188
  336.9 163.5 %copy-start.15 = (bf16[512,1536]{1,0:T(8,128)(2,1)S(1)}, bf16[512,1536]{1,0:T(8,128)(2,1)}, u32[]{:S(2)}) copy-start(bf16[512,1536]{1,0:T(8,128)(2,1)} %reduce-scatter.2.cloned.1.call-done) | copy-start | bytes 4718596
  502.7 298.3 %all-reduce.6.cloned.1.call-start = ((), (), s32[]{:S(2)}) async-start(), calls=%async_computation.3 | async-start | bytes 6291456 | tf_op jit(solution)/shard_map/psum | solution.py:881
  505.6 17.1 %copy-start.35 = (bf16[384,1536]{1,0:T(8,128)(2,1)S(1)}, bf16[384,1536]{1,0:T(8,128)(2,1)}, u32[]{:S(2)}) copy-start(bf16[384,1536]{1,0:T(8,128)(2,1)} %w_ref.1) | copy-start | bytes 3538948
  522.7 7.6 copy-start.1
  579.6 8.2 %copy-start.11 = (f32[2048,32]{0,1:T(8,128)S(1)}, f32[2048,32]{0,1:T(8,128)}, u32[]{:S(2)}) copy-start(f32[2048,32]{0,1:T(8,128)} %copy-done.10) | copy-start | bytes 786436
  595.5 11.2 %slice-start.4 = ((s8[6291456]{0:T(1024)(128)(4,1)}), s8[4194304]{0:T(1024)(128)(4,1)S(1)}, s32[]{:S(2)}) async-start(s8[6291456]{0:T(1024)(128)(4,1)} %bitcast.97), calls=%async_computation.9 | async-start | bytes 8388608
  599.1 7.6 copy-start.28
  599.2 7.6 copy-start.30
  617.0 172.4 %slice-start = ((s8[6291456]{0:T(1024)(128)(4,1)}), s8[2097152]{0:T(1024)(128)(4,1)S(1)}, s32[]{:S(2)}) async-start(s8[6291456]{0:T(1024)(128)(4,1)} %bitcast.89), calls=%async_computation.5 | async-start | bytes 4194304
  619.5 169.9 %slice-start.1 = ((s8[6291456]{0:T(1024)(128)(4,1)}), s8[4194304]{0:T(1024)(128)(4,1)S(1)}, s32[]{:S(2)}) async-start(s8[6291456]{0:T(1024)(128)(4,1)} %bitcast.89), calls=%async_computation.6 | async-start | bytes 8388608
  (34 other events, 135.9 us)
Sparse Core Ops, SparseCore 0:
  224.5 110.9 reduce-scatter.1
  502.8 114.1 all-gather.1
Sparse Core Ops, SparseCore 1:
  297.5 208.0 all-reduce.7
  617.1 67.4 all-reduce.5
